TPU v7x, 128 devices: a whole 4x4x4 slice. The times are simulated.
128 devices in a mesh: row: 8 (over x, z_lo), col: 16 (over z_hi, y, core).
Axes of the slice: x: 4, y: 4, z: 4 (z_hi: 2, z_lo: 2; z = z_hi * 2 + z_lo), core: 2. Of those that a mesh axis runs over, the one named last changes fastest.
Arguments:
- pair: bfloat16 [512, 512, 128], P('row', 'col'), may hold values from -6 to 6
- cotangent: bfloat16 [512, 512, 128], P('row', 'col'), may hold values from -6 to 6
- res_mask: int32 [512], replicated, may hold values 0 or 1
- chain: int32 [512], replicated, may hold values from 0 to 3, never falling along the last dimension, each value on 1 to 256 neighbouring positions
- ln_in_gain: float32 [128], replicated, may hold values from 0.5 to 1.5
- ln_in_bias: float32 [128], replicated, may hold values from -3 to 3
- w_proj: bfloat16 [128, 512], replicated, may hold values from -0.5 to 0.5
- w_gate: bfloat16 [128, 128], replicated, may hold values from -0.5 to 0.5
- chain_bias: float32 [128], replicated, may hold values from -4 to 4
- ln_out_gain: float32 [128], replicated, may hold values from 0.5 to 1.5
- ln_out_bias: float32 [128], replicated, may hold values from -3 to 3
- w_out: bfloat16 [128, 128], replicated, may hold values from -0.5 to 0.5
Outputs:
- grad_pair: bfloat16 [512, 512, 128], P('row', 'col')
- grad_proj: float32 [128, 512], replicated
- grad_gate: float32 [128, 128], replicated
- grad_out: float32 [128, 128], replicated
Inputs may be any that keep to these rules, and one draw needn't show every extreme that they name: chain never decreases along the residues.
All inputs are finite; a program needn't handle non-finite values.
Results may differ from a plain program's by a relative error of at most 0.02.
Values may be sent and summed in bfloat16 or wider, within the bound.
No kernel may reach another device: no remote copies, remote signals or barrier semaphores. Data moves between devices by JAX's collectives and lax.ppermute only.
A program may use at most 128 MiB of HBM per device.

v0:
```python
import jax
import jax.numpy as jnp
from jax import lax
from jax.sharding import PartitionSpec as P

EPS = 1e-05


def layer_norm(values, gain, bias):
    mean = jnp.mean(values, axis=-1, keepdims=True)
    centred = values - mean
    inverse = lax.rsqrt(jnp.mean(centred * centred, axis=-1, keepdims=True) + EPS)
    normed = centred * inverse
    return (normed * gain + bias, normed, inverse)


def norm_back(grad_normed, normed, inverse):
    first = jnp.mean(grad_normed, axis=-1, keepdims=True)
    second = jnp.mean(grad_normed * normed, axis=-1, keepdims=True)
    return (grad_normed - first - normed * second) * inverse


def matmul_last(left, right):
    shape = left.shape
    flat = jnp.dot(left.reshape(-1, shape[-1]), right, preferred_element_type=jnp.float32)
    return flat.reshape(shape[:-1] + (right.shape[1],))


def contract_pairs(left, right):
    flat_left = left.reshape(-1, left.shape[-1])
    flat_right = right.reshape(-1, right.shape[-1])
    return lax.dot_general(
        flat_left, flat_right, (((0,), (0,)), ((), ())), preferred_element_type=jnp.float32
    )


def project(pair, ln_in_gain, ln_in_bias, w_proj):
    scaled, normed, inverse = layer_norm(pair.astype(jnp.float32), ln_in_gain, ln_in_bias)
    normed_b = scaled.astype(jnp.bfloat16)
    return (normed_b, normed, inverse, matmul_last(normed_b, w_proj))


def activations(proj, pair_mask):
    width = proj.shape[-1] // 4
    gate_a = jax.nn.sigmoid(proj[..., :width])
    gate_b = jax.nn.sigmoid(proj[..., 2 * width : 3 * width])
    act_a = (gate_a * proj[..., width : 2 * width] * pair_mask).astype(jnp.bfloat16)
    act_b = (gate_b * proj[..., 3 * width :] * pair_mask).astype(jnp.bfloat16)
    return (act_a, act_b)


def gated_output(
    mixed, cotangent, normed_b, same, chain_bias, w_gate, ln_out_gain, ln_out_bias, w_out
):
    scaled, normed, inverse = layer_norm(mixed, ln_out_gain, ln_out_bias)
    out_b = scaled.astype(jnp.bfloat16)
    update = matmul_last(out_b, w_out)
    gate = jax.nn.sigmoid(matmul_last(normed_b, w_gate) + same * chain_bias)
    cot = cotangent.astype(jnp.float32)
    grad_update = (cot * gate).astype(jnp.bfloat16)
    grad_logit = (cot * update * gate * (1.0 - gate)).astype(jnp.bfloat16)
    grad_scaled = matmul_last(grad_update, w_out.T)
    grad_mixed = norm_back(grad_scaled * ln_out_gain, normed, inverse).astype(jnp.bfloat16)
    return (
        grad_mixed,
        grad_logit,
        contract_pairs(out_b, grad_update),
        contract_pairs(normed_b, grad_logit),
    )


def input_back(
    normed_b,
    normed,
    inverse,
    proj,
    pair_mask,
    grad_a,
    grad_b,
    grad_logit,
    ln_in_gain,
    w_proj,
    w_gate,
):
    width = proj.shape[-1] // 4
    gate_a = jax.nn.sigmoid(proj[..., :width])
    gate_b = jax.nn.sigmoid(proj[..., 2 * width : 3 * width])
    masked_a = grad_a * pair_mask
    masked_b = grad_b * pair_mask
    grad_p = jnp.concatenate(
        [
            masked_a * proj[..., width : 2 * width] * gate_a * (1.0 - gate_a),
            masked_a * gate_a,
            masked_b * proj[..., 3 * width :] * gate_b * (1.0 - gate_b),
            masked_b * gate_b,
        ],
        axis=-1,
    ).astype(jnp.bfloat16)
    grad_zn = matmul_last(grad_p, w_proj.T) + matmul_last(grad_logit, w_gate.T)
    grad_pair = norm_back(grad_zn * ln_in_gain, normed, inverse).astype(jnp.bfloat16)
    return (grad_pair, contract_pairs(normed_b, grad_p))


def body(
    pair,
    cotangent,
    res_mask,
    chain,
    ln_in_gain,
    ln_in_bias,
    w_proj,
    w_gate,
    chain_bias,
    ln_out_gain,
    ln_out_bias,
    w_out,
):
    tile_rows = pair.shape[0]
    tile_cols = pair.shape[1]
    total = tile_rows * lax.axis_size("row")
    row_start = lax.axis_index("row") * tile_rows
    col_start = lax.axis_index("col") * tile_cols
    maskf = res_mask.astype(jnp.float32)
    mask_rows = lax.dynamic_slice_in_dim(maskf, row_start, tile_rows)
    mask_cols = lax.dynamic_slice_in_dim(maskf, col_start, tile_cols)
    pair_mask = mask_rows[:, None, None] * mask_cols[None, :, None]
    chain_rows = lax.dynamic_slice_in_dim(chain, row_start, tile_rows)
    chain_cols = lax.dynamic_slice_in_dim(chain, col_start, tile_cols)
    same = (chain_rows[:, None] == chain_cols[None, :]).astype(jnp.float32)[:, :, None]
    normed_b, normed, inverse, proj = project(pair, ln_in_gain, ln_in_bias, w_proj)
    act_a, act_b = activations(proj, pair_mask)
    b_cols = lax.all_gather(act_b, "row", axis=0, tiled=True)
    piece = b_cols
    mixed = jnp.transpose(
        lax.psum_scatter(
            jnp.einsum("ikh,jkh->jih", act_a, piece, preferred_element_type=jnp.float32).astype(
                jnp.bfloat16
            ),
            "col",
            scatter_dimension=0,
            tiled=True,
        ).astype(jnp.float32),
        (1, 0, 2),
    )
    grad_mixed, grad_logit, term_out, term_gate = gated_output(
        mixed, cotangent, normed_b, same, chain_bias, w_gate, ln_out_gain, ln_out_bias, w_out
    )
    dx_rows = lax.all_gather(grad_mixed, "col", axis=1, tiled=True)
    grad_a = jnp.einsum("ijh,jkh->ikh", dx_rows, b_cols, preferred_element_type=jnp.float32)
    piece = dx_rows
    grad_b = lax.psum_scatter(
        jnp.einsum("ijh,ikh->jkh", piece, act_a, preferred_element_type=jnp.float32).astype(
            jnp.bfloat16
        ),
        "row",
        scatter_dimension=0,
        tiled=True,
    ).astype(jnp.float32)
    grad_pair, term_proj = input_back(
        normed_b,
        normed,
        inverse,
        proj,
        pair_mask,
        grad_a,
        grad_b,
        grad_logit,
        ln_in_gain,
        w_proj,
        w_gate,
    )
    sums = lax.psum((term_proj, term_gate, term_out), ("row", "col"))
    scale = 1.0 / total
    return (grad_pair, sums[0] * scale, sums[1] * scale, sums[2] * scale)


def solution(mesh):
    return jax.shard_map(
        body,
        mesh=mesh,
        in_specs=(
            P("row", "col", None),
            P("row", "col", None),
            P(),
            P(),
            P(),
            P(),
            P(),
            P(),
            P(),
            P(),
            P(),
            P(),
        ),
        out_specs=(P("row", "col", None), P(), P(), P()),
        check_vma=False,
    )
```

profile of v0, /device:TPU:1, one launch (start us, length us, event | category | flops | bytes accessed | tf_op | source)
XLA Modules:
  0.0 634.5 jit_solution(537603368556544840)
XLA Ops:
  9.5 1.7 fusion.19
  11.2 2.0 fusion.42
  13.3 2.0 copy-done.2
  15.2 1.4 multiply_convert_fusion.4
  16.7 1.7 copy.32
  18.4 91.4 %all-gather.3.cloned.1.call-done = bf16[512,32,128]{2,1,0:T(8,128)(2,1)} async-done(((bf16[64,32,128]{2,1,0:T(8,128)(2,1)}), bf16[512,32,128]{2,1,0:T(8,128)(2,1)}) %all-gather.3.cloned.1.call-update) | async-done | bytes 4194320 | tf_op jit(solution)/shard_map/all_gather | solution.py:132
  109.8 8.6 %copy.34 = bf16[512,32,128]{0,1,2:T(8,128)(2,1)} copy(bf16[512,32,128]{2,1,0:T(8,128)(2,1)} %all-gather.3.cloned.1.call-done) | data formatting | bytes 8388608 | tf_op jit(solution)/shard_map/all_gather | solution.py:132
  118.4 7.8 %fusion.59 = bf16[128,512,64]{1,2,0:T(8,128)(2,1)} fusion(bf16[512,32,128]{0,1,2:T(8,128)(2,1)} %copy.34, bf16[64,32,128]{0,1,2:T(8,128)(2,1)S(1)} %copy.32), kind=kOutput, calls=%fused_computation.89 | convolution fusion | flops 268435456 | bytes 13107200 | tf_op jit(solution)/shard_map/ikh,jkh->jih/dot_general | solution.py:136
  126.2 13.0 %copy.33 = bf16[128,512,64]{0,1,2:T(8,128)(2,1)} copy(bf16[128,512,64]{1,2,0:T(8,128)(2,1)} %fusion.59) | data formatting | bytes 16777216 | tf_op jit(solution)/shard_map/ikh,jkh->jih/dot_general | solution.py:136
  140.3 1.9 fusion.6
  142.1 101.5 %reduce-scatter.3.cloned.1.call-done = bf16[32,64,128]{2,0,1:T(8,128)(2,1)} async-done(((bf16[512,64,128]{2,0,1:T(8,128)(2,1)}), bf16[32,64,128]{2,0,1:T(8,128)(2,1)}) %reduce-scatter.3.cloned.1.call-update) | async-done | bytes 524304 | tf_op jit(solution)/shard_map/reduce_scatter | solution.py:135
  243.6 1.5 bitcast_reduce_fusion
  245.1 1.7 fusion.38
  246.8 2.6 fusion.58
  249.4 1.9 fusion.35
  251.6 80.1 %all-gather.5.cloned.1.call-done = bf16[64,512,128]{2,1,0:T(8,128)(2,1)} async-done(((bf16[64,32,128]{2,1,0:T(8,128)(2,1)}), bf16[64,512,128]{2,1,0:T(8,128)(2,1)}) %all-gather.5.cloned.1.call-update) | async-done | bytes 8388624 | tf_op jit(solution)/shard_map/all_gather | solution.py:148
  331.8 29.2 %copy.35 = bf16[64,512,128]{0,1,2:T(8,128)(2,1)} copy(bf16[64,512,128]{2,1,0:T(8,128)(2,1)} %all-gather.5.cloned.1.call-done) | data formatting | bytes 16777216 | tf_op jit(solution)/shard_map/all_gather | solution.py:148
  360.9 10.5 %fusion.61 = bf16[128,32,512]{2,1,0:T(8,128)(2,1)} fusion(bf16[64,32,128]{0,1,2:T(8,128)(2,1)S(1)} %copy.32, bf16[64,512,128]{0,1,2:T(8,128)(2,1)} %copy.35), kind=kOutput, calls=%fused_computation.91 | convolution fusion | flops 268435456 | bytes 13107200 | tf_op jit(solution)/shard_map/ijh,ikh->jkh/dot_general | solution.py:152
  371.5 9.1 %copy.39 = bf16[128,32,512]{0,1,2:T(8,128)(2,1)} copy(bf16[128,32,512]{2,1,0:T(8,128)(2,1)} %fusion.61) | data formatting | bytes 8388608 | tf_op jit(solution)/shard_map/ijh,ikh->jkh/dot_general | solution.py:152
  382.8 1.6 convolution_bitcast_fusion.2
  384.4 1.6 convolution_bitcast_fusion.1
  387.2 7.4 %fusion.60 = f32[128,32,64]{2,1,0:T(8,128)S(1)} fusion(bf16[512,32,128]{0,1,2:T(8,128)(2,1)S(1)} %copy-done.1, bf16[64,512,128]{0,1,2:T(8,128)(2,1)} %copy.35), kind=kOutput, calls=%fused_computation.90 | convolution fusion | flops 268435456 | bytes 13631488 | tf_op jit(solution)/shard_map/ijh,jkh->ikh/dot_general | solution.py:149
  394.5 2.5 copy.36
  397.1 71.9 %reduce-scatter.5.cloned.1.call-done = bf16[64,32,128]{2,1,0:T(8,128)(2,1)} async-done(((bf16[512,32,128]{2,1,0:T(8,128)(2,1)}), bf16[64,32,128]{2,1,0:T(8,128)(2,1)}) %reduce-scatter.5.cloned.1.call-update) | async-done | bytes 524304 | tf_op jit(solution)/shard_map/reduce_scatter | solution.py:151
  469.0 3.2 multiply_convert_fusion.3
  473.0 1.8 convolution_bitcast_fusion
  474.8 2.5 fusion.57
  477.4 1.9 fusion.18
  479.3 144.0 %all-reduce.3.cloned.1.call-done = (f32[128,512]{1,0:T(8,128)}, f32[128,128]{1,0:T(8,128)}, f32[128,128]{1,0:T(8,128)}) async-done(((f32[128,512]{1,0:T(8,128)}, f32[128,128]{1,0:T(8,128)}, f32[128,128]{1,0:T(8,128)}), (f32[128,512]{1,0:T(8,128)}, f32[128,128]{1,0:T(8,128)}, f32[128,128]{1,0:T(8,128)})) %all-reduce.3.cloned.1.call-update) | async-done | bytes 393232 | tf_op jit(solution)/shard_map/psum | solution.py:172
  623.3 1.7 broadcast_multiply_fusion
  625.0 1.5 broadcast_multiply_fusion.2
  626.5 1.5 broadcast_multiply_fusion.1
  (64 shorter events, 8.0 us)
Async XLA Ops:
  7.2 4.1 copy-start
  7.2 102.6 %all-gather.3.cloned.1.call-start = ((), (), s32[]{:S(2)}) async-start(), calls=%async_computation.2 | async-start | bytes 4718592 | tf_op jit(solution)/shard_map/all_gather | solution.py:132
  13.3 2.0 copy-start.2
  16.6 227.0 %reduce-scatter.3.cloned.1.call-start = ((), (), s32[]{:S(2)}) async-start(), calls=%async_computation.3 | async-start | bytes 8912896 | tf_op jit(solution)/shard_map/reduce_scatter | solution.py:135
  139.2 0.7 copy-start.16
  139.2 1.1 copy-start.4
  139.2 1.1 copy-start.12
  139.2 1.1 copy-start.14
  139.2 1.1 copy-start.15
  139.2 1.0 copy-start.17
  139.2 107.5 %copy-start.7 = (bf16[64,32,128]{2,1,0:T(8,128)(2,1)S(1)}, bf16[64,32,128]{2,1,0:T(8,128)(2,1)}, u32[]{:S(2)}) copy-start(bf16[64,32,128]{2,1,0:T(8,128)(2,1)} %param.13) | copy-start | bytes 1572868
  139.3 107.5 %copy-start.11 = (bf16[128,128]{1,0:T(8,128)(2,1)S(1)}, bf16[128,128]{1,0:T(8,128)(2,1)}, u32[]{:S(2)}) copy-start(bf16[128,128]{1,0:T(8,128)(2,1)} %param.23) | copy-start | bytes 98308
  139.3 107.5 %copy-start.13 = (f32[128]{0:T(128)S(1)}, f32[128]{0:T(128)}, u32[]{:S(2)}) copy-start(f32[128]{0:T(128)} %param.21) | copy-start | bytes 1540
  139.3 192.5 %all-gather.5.cloned.1.call-start = ((), (), s32[]{:S(2)}) async-start(), calls=%async_computation.4 | async-start | bytes 8912896 | tf_op jit(solution)/shard_map/all_gather | solution.py:148
  243.6 5.8 copy-start.3
  251.4 217.6 %reduce-scatter.5.cloned.1.call-start = ((), (), s32[]{:S(2)}) async-start(), calls=%async_computation.5 | async-start | bytes 4718592 | tf_op jit(solution)/shard_map/reduce_scatter | solution.py:151
  380.6 1.2 copy-start.5
  380.6 1.2 copy-start.18
  380.6 242.7 %all-reduce.3.cloned.1.call-start = ((), (), s32[]{:S(2)}) async-start(), calls=%async_computation.6 | async-start | bytes 786432 | tf_op jit(solution)/shard_map/psum | solution.py:172
  382.8 4.4 copy-start.1
  472.2 0.8 copy-start.10
  472.2 2.6 copy-start.8
  472.2 2.6 copy-start.9
  473.0 1.8 copy-start.6
Sparse Core Ops, SparseCore 0:
  16.7 92.9 all-gather.2
  139.4 104.1 reduce-scatter.2
  251.5 80.1 all-gather.4
  380.7 88.1 reduce-scatter.4
  477.5 145.7 all-reduce.2
where the time goes:
time: 636 us; the launch traced here: 634 us
  waiting for transfers between devices  489 us (77%)
  local copies, waits for them, and re-layouts  69.1 us (11%)
  matrix products  41.8 us (7%)
  other arithmetic  20.2 us (3%)
  between operations  14.1 us (2%)
    psum x1, waiting for transfers between devices, body(): sums = lax.psum((term_proj, term_gate, term_out), ('row', 'col'))  144 us
    reduce_scatter x1, waiting for transfers between devices, body(): lax.psum_scatter(jnp.einsum('ikh,jkh->jih', act_a, piece, preferred_eleme...  101 us
    all_gather x1, waiting for transfers between devices, body(): b_cols = lax.all_gather(act_b, 'row', axis=0, tiled=True)  91.4 us
    all_gather x1, waiting for transfers between devices, body(): dx_rows = lax.all_gather(grad_mixed, 'col', axis=1, tiled=True)  80.1 us
    reduce_scatter x1, waiting for transfers between devices, body(): lax.psum_scatter(jnp.einsum('ijh,ikh->jkh', piece, act_a, preferred_eleme...  71.9 us
    all_gather x1, local copies, waits for them, and re-layouts, body(): dx_rows = lax.all_gather(grad_mixed, 'col', axis=1, tiled=True)  29.2 us
    dot_general x1, local copies, waits for them, and re-layouts, body(): jnp.einsum('ikh,jkh->jih', act_a, piece, preferred_element_type=jnp.float32)  13 us
  transfers between devices with their start and end apart: 5, of which 5 were waited for; matrix products, arithmetic and copies ran while one was open for 3% of the time, Pallas kernels for 0%

commit v1 on v0

v1 whole, which is shorter than its diff:
```python
import functools

import jax
import jax.numpy as jnp
from jax import lax
from jax.experimental import pallas as pl
from jax.experimental.pallas import tpu as pltpu
from jax.sharding import PartitionSpec as P

EPS = 1e-05
F32 = jnp.float32
BF16 = jnp.bfloat16
AXES = ("row", "col")

ROWS = 64
COLS = 32
NROW = 8
NCOL = 16
DEV = NROW * NCOL
CH = 128
N = 512
PAIRS = ROWS * COLS
LANES = 128
CHUNKS = PAIRS // LANES
TILES = N // LANES


def dot(left, right, dim_left, dim_right):
    return lax.dot_general(
        left, right, (((dim_left,), (dim_right,)), ((), ())), preferred_element_type=F32
    )


def sigmoid(x):
    return 0.5 * jnp.tanh(0.5 * x) + 0.5


def column(row):
    return jnp.broadcast_to(row, (LANES, row.shape[1])).T


def lanes_of(s, offset=0):
    return pl.ds(pl.multiple_of(s * LANES + offset, LANES), LANES)


def swap_halves(first, second):
    low = lax.broadcasted_iota(jnp.int32, first.shape, 1) < LANES // 2
    return (
        jnp.where(low, first, pltpu.roll(second, LANES // 2, 1)),
        jnp.where(low, pltpu.roll(first, LANES // 2, 1), second),
    )


def load_chunk(ref, s):
    top = ref[pl.ds(2 * s, ROWS, stride=COLS), :]
    bottom = ref[pl.ds(2 * s + 1, ROWS, stride=COLS), :]
    return jnp.concatenate([top, bottom], axis=0)


def front_kernel(mask_s, chain_s, pair, gain, bias, w_proj, send, zn_t, normed_t, aux, xs, w_t):
    row_start = lax.axis_index("row") * ROWS
    col_start = lax.axis_index("col") * COLS
    xs[...] = pair[...].astype(F32).reshape(PAIRS, CH)
    w_t[...] = w_proj[...].astype(F32).T.astype(BF16)
    gain_c = column(gain[...])
    bias_c = column(bias[...])
    lane = lax.broadcasted_iota(jnp.int32, (1, LANES), 1)
    place = lane % ROWS
    mask_row = jnp.zeros((1, LANES), jnp.int32)
    chain_row = jnp.zeros((1, LANES), jnp.int32)
    for i in range(ROWS):
        here = place == i
        mask_row = jnp.where(here, mask_s[row_start + i], mask_row)
        chain_row = jnp.where(here, chain_s[row_start + i], chain_row)
    low = lane < ROWS

    def step(s, carry):
        x = load_chunk(xs, s).T
        mean = jnp.mean(x, axis=0, keepdims=True)
        centred = x - mean
        inverse = lax.rsqrt(jnp.mean(centred * centred, axis=0, keepdims=True) + EPS)
        normed = centred * inverse
        zn = (normed * gain_c + bias_c).astype(BF16)
        k = col_start + 2 * s
        mask = (jnp.where(low, mask_s[k], mask_s[k + 1]) * mask_row).astype(F32)
        same = (jnp.where(low, chain_s[k], chain_s[k + 1]) == chain_row).astype(F32)
        proj = dot(w_t[...], zn, 1, 0)
        act_a = sigmoid(proj[:CH]) * proj[CH : 2 * CH] * mask
        act_b = sigmoid(proj[2 * CH : 3 * CH]) * proj[3 * CH :] * mask
        send[:, lanes_of(s)] = act_a.astype(BF16)
        send[:, lanes_of(s, PAIRS)] = act_b.astype(BF16)
        zn_t[:, lanes_of(s)] = zn
        normed_t[:, lanes_of(s)] = normed
        aux[0:1, lanes_of(s)] = mask
        aux[1:2, lanes_of(s)] = same
        aux[2:3, lanes_of(s)] = inverse
        return carry

    lax.fori_loop(0, CHUNKS, step, 0)


def mix_kernel(recv, send, a_t, b_t, mixed):
    def gather(s, carry):
        for t in range(TILES):
            for offset, out in ((0, a_t), (PAIRS, b_t)):
                first = recv[32 * t : 32 * t + 16, lanes_of(s, offset)].astype(F32)
                second = recv[32 * t + 16 : 32 * t + 32, lanes_of(s, offset)].astype(F32)
                even, odd = swap_halves(first, second)
                spot = slice(t * LANES, (t + 1) * LANES)
                row = pl.multiple_of(s * 32, 32)
                out[pl.ds(row, 16), spot] = even.astype(BF16)
                out[pl.ds(row + 16, 16), spot] = odd.astype(BF16)
        return carry

    lax.fori_loop(0, CHUNKS, gather, 0)
    for t in range(TILES):
        spot = slice(t * LANES, (t + 1) * LANES)
        mixed[t] = dot(b_t[...], a_t[:, spot], 0, 0)

    def scatter(s, carry):
        for t in range(TILES):
            first = mixed[t, pl.ds(2 * s, NCOL, stride=COLS), :]
            second = mixed[t, pl.ds(2 * s + 1, NCOL, stride=COLS), :]
            even, odd = swap_halves(first, second)
            send[32 * t : 32 * t + 16, lanes_of(s)] = even.astype(BF16)
            send[32 * t + 16 : 32 * t + 32, lanes_of(s)] = odd.astype(BF16)
        return carry

    lax.fori_loop(0, CHUNKS, scatter, 0)


def middle_kernel(
    recv, cot, zn_t, aux, w_gate, chain_bias, gain, bias, w_out,
    send, logit_t, cs, wg_t, wo_t, term_out, term_gate,
):
    cs[...] = cot[...].astype(F32).reshape(PAIRS, CH)
    wg_t[...] = w_gate[...].astype(F32).T.astype(BF16)
    wo_t[...] = w_out[...].astype(F32).T.astype(BF16)
    gain_c = column(gain[...])
    bias_c = column(bias[...])
    chain_c = column(chain_bias[...])
    term_out[...] = jnp.zeros_like(term_out)
    term_gate[...] = jnp.zeros_like(term_gate)

    def step(s, carry):
        here = lanes_of(s)
        mixed = recv[:, here].astype(F32)
        mean = jnp.mean(mixed, axis=0, keepdims=True)
        centred = mixed - mean
        inverse = lax.rsqrt(jnp.mean(centred * centred, axis=0, keepdims=True) + EPS)
        normed = centred * inverse
        y = (normed * gain_c + bias_c).astype(BF16)
        zn = zn_t[:, here]
        update = dot(wo_t[...], y, 1, 0)
        gate = sigmoid(dot(wg_t[...], zn, 1, 0) + aux[1:2, here] * chain_c)
        cot_t = load_chunk(cs, s).T
        grad_gated = cot_t * gate
        grad_update = grad_gated.astype(BF16)
        grad_logit = (grad_gated * update * (1.0 - gate)).astype(BF16)
        q = dot(w_out[...], grad_update, 1, 0) * gain_c
        first = jnp.mean(q, axis=0, keepdims=True)
        second = jnp.mean(q * normed, axis=0, keepdims=True)
        grad_mixed = (q - first - normed * second) * inverse
        send[:, here] = grad_mixed.astype(BF16)
        logit_t[:, here] = grad_logit
        term_out[...] += dot(y, grad_update, 1, 1)
        term_gate[...] += dot(zn, grad_logit, 1, 1)
        return carry

    lax.fori_loop(0, CHUNKS, step, 0)
    send[:, PAIRS : PAIRS + CH] = term_out[...].astype(BF16)
    send[:, PAIRS + CH : PAIRS + 2 * CH] = term_gate[...].astype(BF16)


def unmix_kernel(recv, a_t, b_t, send, strided, grad, product):
    def gather(s, carry):
        for t in range(TILES):
            first = recv[32 * t : 32 * t + 16, lanes_of(s)].astype(F32)
            second = recv[32 * t + 16 : 32 * t + 32, lanes_of(s)].astype(F32)
            even, odd = swap_halves(first, second)
            strided[t, pl.ds(2 * s, NCOL, stride=COLS), :] = even
            strided[t, pl.ds(2 * s + 1, NCOL, stride=COLS), :] = odd
        return carry

    lax.fori_loop(0, CHUNKS, gather, 0)
    for t in range(TILES):
        grad[:, t * LANES : (t + 1) * LANES] = strided[t].astype(BF16)
    for offset, left, dim in ((0, b_t, 0), (PAIRS, a_t, 1)):
        product[...] = dot(left[...], grad[...], 1, dim)

        def scatter(s, carry):
            row = pl.multiple_of(s * 32, 32)
            for t in range(TILES):
                spot = slice(t * LANES, (t + 1) * LANES)
                even, odd = swap_halves(
                    product[pl.ds(row, 16), spot], product[pl.ds(row + 16, 16), spot]
                )
                send[32 * t : 32 * t + 16, lanes_of(s, offset)] = even.astype(BF16)
                send[32 * t + 16 : 32 * t + 32, lanes_of(s, offset)] = odd.astype(BF16)
            return carry

        lax.fori_loop(0, CHUNKS, scatter, 0)
    terms = recv[:, PAIRS : PAIRS + 2 * CH].astype(F32)
    total = jnp.sum(terms, axis=0, keepdims=True) * (1.0 / N)
    high = total.astype(BF16)
    rest = (total - high.astype(F32)).astype(BF16)
    wide = (DEV, 2 * CH)
    send[:, 2 * PAIRS : 2 * PAIRS + 2 * CH] = jnp.broadcast_to(high.astype(F32), wide).astype(BF16)
    send[:, 2 * PAIRS + 2 * CH :] = jnp.broadcast_to(rest.astype(F32), wide).astype(BF16)


def back_kernel(
    recv, zn_t, normed_t, aux, logit_t, gain, w_proj, w_gate,
    grad_pair, term_proj, grad_gate, grad_out, ys, w_t,
):
    w_t[...] = w_proj[...].astype(F32).T.astype(BF16)
    gain_c = column(gain[...])
    term_proj[...] = jnp.zeros_like(term_proj)

    def step(s, carry):
        here = lanes_of(s)
        zn = zn_t[:, here]
        mask = aux[0:1, here]
        inverse = aux[2:3, here]
        proj = dot(w_t[...], zn, 1, 0)
        gate_a = sigmoid(proj[:CH])
        gate_b = sigmoid(proj[2 * CH : 3 * CH])
        gated_a = recv[:, here].astype(F32) * mask * gate_a
        gated_b = recv[:, lanes_of(s, PAIRS)].astype(F32) * mask * gate_b
        grad_p = jnp.concatenate(
            [
                gated_a * proj[CH : 2 * CH] * (1.0 - gate_a),
                gated_a,
                gated_b * proj[3 * CH :] * (1.0 - gate_b),
                gated_b,
            ],
            axis=0,
        ).astype(BF16)
        term_proj[...] += dot(zn, grad_p, 1, 1)
        grad_zn = dot(w_proj[...], grad_p, 1, 0) + dot(w_gate[...], logit_t[:, here], 1, 0)
        normed = normed_t[:, here]
        q = grad_zn * gain_c
        first = jnp.mean(q, axis=0, keepdims=True)
        second = jnp.mean(q * normed, axis=0, keepdims=True)
        out = ((q - first - normed * second) * inverse).T
        ys[pl.ds(2 * s, ROWS, stride=COLS), :] = out[:ROWS]
        ys[pl.ds(2 * s + 1, ROWS, stride=COLS), :] = out[ROWS:]
        return carry

    lax.fori_loop(0, CHUNKS, step, 0)
    grad_pair[...] = ys[...].reshape(ROWS, COLS, CH).astype(BF16)
    base = 2 * PAIRS
    total = recv[:, base : base + 2 * CH].astype(F32) + recv[:, base + 2 * CH :].astype(F32)
    grad_out[...] = total[:, :CH]
    grad_gate[...] = total[:, CH:]


def sum_kernel(parts, out):
    total = jnp.sum(parts[...], axis=0, keepdims=True) * (1.0 / N)
    out[...] = jnp.broadcast_to(total, out.shape)


def call(kernel, outs, scratch, flops, args, smem=0):
    specs = [pl.BlockSpec(memory_space=pltpu.SMEM)] * smem
    specs += [pl.BlockSpec(memory_space=pltpu.VMEM)] * (len(args) - smem)
    moved = sum(x.size * x.dtype.itemsize for x in args) + sum(
        x.size * x.dtype.itemsize for x in outs
    )
    return pl.pallas_call(
        kernel,
        out_shape=outs,
        in_specs=specs,
        out_specs=[pl.BlockSpec(memory_space=pltpu.VMEM)] * len(outs),
        scratch_shapes=scratch,
        compiler_params=pltpu.CompilerParams(vmem_limit_bytes=48 << 20),
        cost_estimate=pl.CostEstimate(flops=flops, bytes_accessed=moved, transcendentals=0),
    )(*args)


def exchange(x):
    split = x.reshape(DEV, -1, LANES)
    return lax.all_to_all(split, AXES, 0, 0, tiled=True).reshape(x.shape)


def body(
    pair,
    cotangent,
    res_mask,
    chain,
    ln_in_gain,
    ln_in_bias,
    w_proj,
    w_gate,
    chain_bias,
    ln_out_gain,
    ln_out_bias,
    w_out,
):
    S = jax.ShapeDtypeStruct
    V = pltpu.VMEM

    def flat(x):
        return x.reshape(1, -1)

    send_ab, zn_t, normed_t, aux = call(
        front_kernel,
        [S((CH, 2 * PAIRS), BF16), S((CH, PAIRS), BF16), S((CH, PAIRS), F32), S((8, PAIRS), F32)],
        [V((PAIRS, CH), F32), V((4 * CH, CH), BF16)],
        2 * PAIRS * CH * 4 * CH,
        (res_mask, chain, pair, flat(ln_in_gain), flat(ln_in_bias), w_proj),
        smem=2,
    )
    send_mixed, a_t, b_t = call(
        mix_kernel,
        [S((DEV, PAIRS), BF16), S((N, N), BF16), S((N, N), BF16)],
        [V((TILES, N, LANES), F32)],
        2 * N * N * N,
        (exchange(send_ab),),
    )
    send_grad, logit_t = call(
        middle_kernel,
        [S((CH, PAIRS + 2 * CH), BF16), S((CH, PAIRS), BF16)],
        [V((PAIRS, CH), F32), V((CH, CH), BF16), V((CH, CH), BF16), V((CH, CH), F32), V((CH, CH), F32)],
        10 * PAIRS * CH * CH,
        (
            exchange(send_mixed), cotangent, zn_t, aux, w_gate, flat(chain_bias),
            flat(ln_out_gain), flat(ln_out_bias), w_out,
        ),
    )
    (send_back,) = call(
        unmix_kernel,
        [S((DEV, 2 * PAIRS + 4 * CH), BF16)],
        [V((TILES, N, LANES), F32), V((N, N), BF16), V((N, N), F32)],
        4 * N * N * N,
        (exchange(send_grad), a_t, b_t),
    )
    grad_pair, term_proj, grad_gate, grad_out = call(
        back_kernel,
        [S((ROWS, COLS, CH), BF16), S((CH, 4 * CH), F32), S((CH, CH), F32), S((CH, CH), F32)],
        [V((PAIRS, CH), F32), V((4 * CH, CH), BF16)],
        26 * PAIRS * CH * CH,
        (exchange(send_back), zn_t, normed_t, aux, logit_t, flat(ln_in_gain), w_proj, w_gate),
    )
    (summed,) = call(sum_kernel, [S((CH, 4 * CH), F32)], [], 0, (exchange(term_proj),))
    return (grad_pair, exchange(summed), grad_gate, grad_out)


def solution(mesh):
    return jax.shard_map(
        body,
        mesh=mesh,
        in_specs=(P("row", "col", None), P("row", "col", None)) + (P(),) * 10,
        out_specs=(P("row", "col", None), P(), P(), P()),
        check_vma=False,
    )
```

time: 636 us -> 183 us (0.29)
  waiting for transfers between devices: 489 us -> 0 us
  blocking collectives: 0 us -> 125 us
  local copies, waits for them, and re-layouts: 69.1 us -> 23.1 us
  matrix products: 41.8 us -> 0 us
  Pallas kernels: 0 us -> 32.5 us
  other arithmetic: 20.2 us -> 0 us
  between operations: 14.1 us -> 0.91 us
    reduce_scatter x2 -> x0, waiting for transfers between devices: 173 us -> none  [the longest x1 101 us: body(): lax.psum_scatter(jnp.einsum('ikh,jkh->jih', act_a, piece, preferred_eleme...]
    all_gather x2 -> x0, waiting for transfers between devices: 172 us -> none  [the longest x1 91.4 us: body(): b_cols = lax.all_gather(act_b, 'row', axis=0, tiled=True)]
    psum x1 -> x0, waiting for transfers between devices: 144 us -> none  [body(): sums = lax.psum((term_proj, term_gate, term_out), ('row', 'col'))]
    all_to_all x0 -> x6, blocking collectives: none -> 125 us  [exchange(): return lax.all_to_all(split, AXES, 0, 0, tiled=True).reshape(x.shape)]
    dot_general x12 -> x0, matrix products: 41.8 us -> none  [the longest x6 11.2 us: matmul_last(): jnp.dot(left.reshape(-1, shape[-1]), right, preferred_element_type=jnp.fl...]
    all_gather x2 -> x0, local copies, waits for them, and re-layouts: 37.8 us -> none  [the longest x1 29.2 us: body(): dx_rows = lax.all_gather(grad_mixed, 'col', axis=1, tiled=True)]
    pallas_call x0 -> x6, Pallas kernels: none -> 32.5 us  [call(): pl.pallas_call(kernel, out_shape=outs, in_specs=specs, out_specs=[pl.Bloc...]
    dot_general x3 -> x0, local copies, waits for them, and re-layouts: 24.7 us -> none  [the longest x1 13 us: body(): jnp.einsum('ikh,jkh->jih', act_a, piece, preferred_element_type=jnp.float32)]
  transfers between devices with their start and end apart: 5 -> 0, of which waited for: 5 -> 0; matrix products, arithmetic and copies ran while one was open for 3% -> 0% of each run, Pallas kernels for 0% -> 0%
where the time goes in v1:
time: 183 us; the launch traced here: 182 us
  blocking collectives  125 us (68%)
  Pallas kernels  32.5 us (18%)
  local copies, waits for them, and re-layouts  23.1 us (13%)
    all_to_all x6, blocking collectives, exchange(): return lax.all_to_all(split, AXES, 0, 0, tiled=True).reshape(x.shape)  125 us
    pallas_call x6, Pallas kernels, call(): pl.pallas_call(kernel, out_shape=outs, in_specs=specs, out_specs=[pl.Bloc...  32.5 us
    unnamed x48, local copies, waits for them, and re-layouts  10.8 us
    all_to_all x2, local copies, waits for them, and re-layouts, exchange(): return lax.all_to_all(split, AXES, 0, 0, tiled=True).reshape(x.shape)  3.93 us
    reshape x4, local copies, waits for them, and re-layouts, exchange(): split = x.reshape(DEV, -1, LANES)  3.68 us

profile of v1, /device:TPU:1, one launch (start us, length us, event | category | flops | bytes accessed | tf_op | source)
XLA Modules:
  0.0 181.9 jit_solution(14155799689706037857)
XLA Ops:
  0.6 0.9 copy-done.9
  1.5 0.7 copy-done.15
  2.2 1.0 copy-done.17
  3.2 0.7 copy-done.18
  3.9 0.7 copy-done.19
  4.6 0.7 copy-done.20
  5.3 6.5 %shard_map.147 = (bf16[128,4096]{1,0:T(8,128)(2,1)S(1)}, bf16[128,2048]{1,0:T(8,128)(2,1)S(1)}, f32[128,2048]{1,0:T(8,128)S(1)}, f32[8,2048]{1,0:T(8,128)S(1)}) custom-call(s32[512]{0:T(512)S(1)} %copy-done.18, s32[512]{0:T(512)S(1)} %copy-done.19, bf16[64,32,128]{2,1,0:T(8,128)(2,1)S(1)} %copy-done.17, f32[1,128]{1,0:T(1,128)S(1)} %bitcast.37, ...), custom_call_target="tpu_custom_call" | custom-call | flops 268435456 | bytes 3347456 | tf_op jit(solution)/shard_map/pallas_call | solution.py:269
  12.0 30.0 %all_to_all.30 = bf16[128,32,128]{2,1,0:T(8,128)(2,1)S(1)} all-to-all(bf16[128,32,128]{2,1,0:T(8,128)(2,1)S(1)} %bitcast.42), channel_id=1, replica_groups=mesh['row'=8,'col'=16] {'row','col'}, dimensions={0} | all-to-all | bytes 2097152 | tf_op jit(solution)/shard_map/all_to_all | solution.py:282
  42.0 0.5 copy.38
  42.5 3.9 %shard_map.148 = (bf16[128,2048]{1,0:T(8,128)(2,1)S(1)}, bf16[512,512]{1,0:T(8,128)(2,1)S(1)}, bf16[512,512]{1,0:T(8,128)(2,1)S(1)}) custom-call(bf16[128,4096]{1,0:T(8,128)(2,1)S(1)} %bitcast.29), custom_call_target="tpu_custom_call" | custom-call | flops 268435456 | bytes 2621440 | tf_op jit(solution)/shard_map/pallas_call | solution.py:269
  46.6 18.2 %all_to_all.31 = bf16[128,16,128]{2,1,0:T(8,128)(2,1)S(1)} all-to-all(bf16[128,16,128]{2,1,0:T(8,128)(2,1)S(1)} %bitcast.46), channel_id=1, replica_groups=mesh['row'=8,'col'=16] {'row','col'}, dimensions={0} | all-to-all | bytes 1048576 | tf_op jit(solution)/shard_map/all_to_all | solution.py:282
  65.0 6.4 %shard_map.149 = (bf16[128,2304]{1,0:T(8,128)(2,1)S(1)}, bf16[128,2048]{1,0:T(8,128)(2,1)S(1)}) custom-call(bf16[128,2048]{1,0:T(8,128)(2,1)S(1)} %bitcast.30, bf16[64,32,128]{2,1,0:T(8,128)(2,1)S(1)} %copy-done, bf16[128,2048]{1,0:T(8,128)(2,1)S(1)} %get-tuple-element.19.zn_t, f32[8,2048]{1,0:T(8,128)S(1)} %get-tuple-element.20.aux, ...), custom_call_target="tpu_custom_call" | custom-call | flops 335544320 | bytes 2819584 | tf_op jit(solution)/shard_map/pallas_call | solution.py:269
  71.5 0.8 copy-done.1
  72.6 0.4 copy.21
  73.0 20.3 %all_to_all.32 = bf16[128,18,128]{2,1,0:T(8,128)(2,1)S(1)} all-to-all(bf16[128,18,128]{2,1,0:T(8,128)(2,1)S(1)} %copy.21), channel_id=1, replica_groups=mesh['row'=8,'col'=16] {'row','col'}, dimensions={0} | all-to-all | bytes 1179648 | tf_op jit(solution)/shard_map/all_to_all | solution.py:282
  93.3 1.2 copy.22
  94.5 1.3 copy.23.recv
  95.9 1.0 copy-done.4
  96.9 1.0 copy-done.6
  97.9 5.6 %shard_map.150 = bf16[128,4608]{1,0:T(8,128)(2,1)S(1)} custom-call(bf16[128,2304]{1,0:T(8,128)(2,1)S(1)} %copy.23.recv, bf16[512,512]{1,0:T(8,128)(2,1)S(1)} %copy-done.4, bf16[512,512]{1,0:T(8,128)(2,1)S(1)} %copy-done.6), custom_call_target="tpu_custom_call" | custom-call | flops 536870912 | bytes 2818048 | tf_op jit(solution)/shard_map/pallas_call | solution.py:269
  103.6 1.4 copy.24
  105.0 2.1 %copy.25 = bf16[128,36,128]{2,1,0:T(8,128)(2,1)S(1)} copy(bf16[128,36,128]{0,2,1:T(8,128)(2,1)} %bitcast.40) | data formatting | bytes 2359296 | tf_op jit(solution)/shard_map/reshape | solution.py:281
  107.1 25.8 %all_to_all.33 = bf16[128,36,128]{2,1,0:T(8,128)(2,1)} all-to-all(bf16[128,36,128]{2,1,0:T(8,128)(2,1)S(1)} %copy.25), channel_id=1, replica_groups=mesh['row'=8,'col'=16] {'row','col'}, dimensions={0} | all-to-all | bytes 2359296 | tf_op jit(solution)/shard_map/all_to_all | solution.py:282
  132.9 2.7 %copy.26 = bf16[128,36,128]{0,2,1:T(8,128)(2,1)} copy(bf16[128,36,128]{2,1,0:T(8,128)(2,1)} %all_to_all.33) | data formatting | bytes 2359296 | tf_op jit(solution)/shard_map/all_to_all | solution.py:282
  135.6 1.6 copy.27.recv
  137.2 0.9 copy-done.10
  138.1 10.0 %shard_map.151 = (bf16[64,32,128]{2,1,0:T(8,128)(2,1)}, f32[128,512]{1,0:T(8,128)S(1)}, f32[128,128]{1,0:T(8,128)}, f32[128,128]{1,0:T(8,128)}) custom-call(bf16[128,4608]{1,0:T(8,128)(2,1)S(1)} %copy.27.recv, bf16[128,2048]{1,0:T(8,128)(2,1)S(1)} %get-tuple-element.19.zn_t, f32[128,2048]{1,0:T(8,128)S(1)} %get-tuple-element.24.normed_t, ...), custom_call_target="tpu_custom_call" | custom-call | flops 872415232 | bytes 4424192 | tf_op jit(solution)/shard_map/pallas_call | solution.py:269
  148.1 0.7 copy-done.7
  148.8 1.0 reshape.73
  149.8 16.0 %all_to_all.34 = f32[128,4,128]{2,1,0:T(4,128)S(1)} all-to-all(f32[128,4,128]{2,1,0:T(4,128)S(1)} %reshape.73), channel_id=1, replica_groups=mesh['row'=8,'col'=16] {'row','col'}, dimensions={0} | all-to-all | bytes 524288 | tf_op jit(solution)/shard_map/all_to_all | solution.py:282
  166.0 15.2 %all_to_all.35 = f32[128,4,128]{2,1,0:T(4,128)S(1)} all-to-all(f32[128,4,128]{2,1,0:T(4,128)S(1)} %reshape.75), channel_id=1, replica_groups=mesh['row'=8,'col'=16] {'row','col'}, dimensions={0} | all-to-all | bytes 524288 | tf_op jit(solution)/shard_map/all_to_all | solution.py:282
  181.2 0.7 copy.40
  (38 shorter events, 1.0 us)
Async XLA Ops:
  0.6 0.9 copy-start.9
  1.5 0.7 copy-start.15
  2.2 1.0 copy-start.17
  3.2 0.7 copy-start.18
  3.9 0.7 copy-start.19
  4.6 0.7 copy-start.20
  46.4 18.5 %copy-start.3 = (bf16[512,512]{1,0:T(8,128)(2,1)}, bf16[512,512]{1,0:T(8,128)(2,1)S(1)}, u32[]{:S(2)}) copy-start(bf16[512,512]{1,0:T(8,128)(2,1)S(1)} %get-tuple-element.22.a_t) | copy-start | bytes 1572868
  46.4 18.5 %copy-start.5 = (bf16[512,512]{1,0:T(8,128)(2,1)}, bf16[512,512]{1,0:T(8,128)(2,1)S(1)}, u32[]{:S(2)}) copy-start(bf16[512,512]{1,0:T(8,128)(2,1)S(1)} %get-tuple-element.23.b_t) | copy-start | bytes 1572868
  46.5 18.4 %copy-start = (bf16[64,32,128]{2,1,0:T(8,128)(2,1)S(1)}, bf16[64,32,128]{2,1,0:T(8,128)(2,1)}, u32[]{:S(2)}) copy-start(bf16[64,32,128]{2,1,0:T(8,128)(2,1)} %cot.1) | copy-start | bytes 1572868
  46.6 18.4 %copy-start.8 = (bf16[128,128]{1,0:T(8,128)(2,1)S(1)}, bf16[128,128]{1,0:T(8,128)(2,1)}, u32[]{:S(2)}) copy-start(bf16[128,128]{1,0:T(8,128)(2,1)} %w_gate.3) | copy-start | bytes 98308
  46.6 18.4 %copy-start.11 = (bf16[128,128]{1,0:T(8,128)(2,1)S(1)}, bf16[128,128]{1,0:T(8,128)(2,1)}, u32[]{:S(2)}) copy-start(bf16[128,128]{1,0:T(8,128)(2,1)} %w_out.1) | copy-start | bytes 98308
  46.6 18.4 %copy-start.12 = (f32[128]{0:T(128)S(1)}, f32[128]{0:T(128)}, u32[]{:S(2)}) copy-start(f32[128]{0:T(128)} %param.20) | copy-start | bytes 1540
  46.6 18.4 %copy-start.13 = (f32[128]{0:T(128)S(1)}, f32[128]{0:T(128)}, u32[]{:S(2)}) copy-start(f32[128]{0:T(128)} %param.21) | copy-start | bytes 1540
  46.6 18.4 %copy-start.14 = (f32[128]{0:T(128)S(1)}, f32[128]{0:T(128)}, u32[]{:S(2)}) copy-start(f32[128]{0:T(128)} %param.22) | copy-start | bytes 1540
  71.5 0.8 copy-start.1
  95.9 1.0 copy-start.4
  96.9 1.0 copy-start.6
  135.6 1.6 copy-start.2
  135.6 1.6 copy-start.16
  137.2 0.9 copy-start.10
  148.1 0.7 copy-start.7

commit v2 on v1

v2 whole, which is shorter than its diff:
```python
import functools

import jax
import jax.numpy as jnp
from jax import lax
from jax.experimental import pallas as pl
from jax.experimental.pallas import tpu as pltpu
from jax.sharding import PartitionSpec as P

EPS = 1e-05
F32 = jnp.float32
BF16 = jnp.bfloat16
AXES = ("row", "col")

ROWS = 64
COLS = 32
NROW = 8
NCOL = 16
DEV = NROW * NCOL
CH = 128
N = 512
PAIRS = ROWS * COLS
LANES = 128
CHUNKS = PAIRS // LANES
WIDE = 256
STEPS = PAIRS // WIDE
EACH = WIDE // ROWS
TILES = N // LANES


def dot(left, right, dim_left, dim_right):
    return lax.dot_general(
        left, right, (((dim_left,), (dim_right,)), ((), ())), preferred_element_type=F32
    )


def sigmoid(x):
    return 0.5 * jnp.tanh(0.5 * x) + 0.5


def column(row):
    return jnp.broadcast_to(row, (WIDE, row.shape[1])).T


def lanes_of(s, offset=0):
    return pl.ds(pl.multiple_of(s * WIDE + offset, LANES), WIDE)


def swap_halves(first, second):
    low = lax.broadcasted_iota(jnp.int32, first.shape, 1) < LANES // 2
    return (
        jnp.where(low, first, pltpu.roll(second, LANES // 2, 1)),
        jnp.where(low, pltpu.roll(first, LANES // 2, 1), second),
    )


def load_chunk(ref, s):
    parts = [ref[pl.ds(EACH * s + e, ROWS, stride=COLS), :] for e in range(EACH)]
    return jnp.concatenate(parts, axis=0).T


def store_chunk(ref, s, value):
    value = value.T
    for e in range(EACH):
        ref[pl.ds(EACH * s + e, ROWS, stride=COLS), :] = value[e * ROWS : (e + 1) * ROWS]


def loop(step, unroll=2):
    def body(group, carry):
        for u in range(unroll):
            step(group * unroll + u)
        return carry

    lax.fori_loop(0, STEPS // unroll, body, 0)


def front_kernel(
    mask_h, chain_h, pair_h, gain_h, bias_h, w_h,
    send, zn_t, normed_t, aux,
    mask_s, chain_s, pair, gain, bias, w_proj, xs, w_t, sems,
):
    copies = [
        pltpu.make_async_copy(src, dst, sems.at[n])
        for n, (src, dst) in enumerate(
            (
                (pair_h, pair), (w_h, w_proj), (gain_h, gain), (bias_h, bias),
                (mask_h, mask_s), (chain_h, chain_s),
            )
        )
    ]
    for copy in copies:
        copy.start()
    for copy in copies[1:]:
        copy.wait()
    row_start = lax.axis_index("row") * ROWS
    col_start = lax.axis_index("col") * COLS
    w_t[...] = w_proj[...].astype(F32).T.astype(BF16)
    gain_c = column(gain[...])
    bias_c = column(bias[...])
    lane = lax.broadcasted_iota(jnp.int32, (1, LANES), 1)
    place = lane % ROWS
    mask_row = jnp.zeros((1, LANES), jnp.int32)
    chain_row = jnp.zeros((1, LANES), jnp.int32)
    for i in range(ROWS):
        here = place == i
        mask_row = jnp.where(here, mask_s[row_start + i], mask_row)
        chain_row = jnp.where(here, chain_s[row_start + i], chain_row)
    low = lane < ROWS
    copies[0].wait()
    xs[...] = pair[...].astype(F32).reshape(PAIRS, CH)

    def step(s):
        x = load_chunk(xs, s)
        mean = jnp.mean(x, axis=0, keepdims=True)
        centred = x - mean
        inverse = lax.rsqrt(jnp.mean(centred * centred, axis=0, keepdims=True) + EPS)
        normed = centred * inverse
        zn = (normed * gain_c + bias_c).astype(BF16)
        mask, same = [], []
        for e in range(0, EACH, 2):
            k = col_start + EACH * s + e
            mask.append((jnp.where(low, mask_s[k], mask_s[k + 1]) * mask_row).astype(F32))
            same.append((jnp.where(low, chain_s[k], chain_s[k + 1]) == chain_row).astype(F32))
        mask = jnp.concatenate(mask, axis=1)
        proj = dot(w_t[...], zn, 1, 0)
        act_a = sigmoid(proj[:CH]) * proj[CH : 2 * CH] * mask
        act_b = sigmoid(proj[2 * CH : 3 * CH]) * proj[3 * CH :] * mask
        send[:, lanes_of(s)] = act_a.astype(BF16)
        send[:, lanes_of(s, PAIRS)] = act_b.astype(BF16)
        zn_t[:, lanes_of(s)] = zn
        normed_t[:, lanes_of(s)] = normed
        aux[0:1, lanes_of(s)] = mask
        aux[1:2, lanes_of(s)] = jnp.concatenate(same, axis=1)
        aux[2:3, lanes_of(s)] = inverse

    loop(step)


def ahead_kernel(cot, zn_t, aux, w_gate, chain_bias, gain, w_out, grad_update, q_out, slope, cs, wg_t):
    cs[...] = cot[...].astype(F32).reshape(PAIRS, CH)
    wg_t[...] = w_gate[...].astype(F32).T.astype(BF16)
    gain_c = column(gain[...])
    chain_c = column(chain_bias[...])

    def step(s):
        here = lanes_of(s)
        gate = sigmoid(dot(wg_t[...], zn_t[:, here], 1, 0) + aux[1:2, here] * chain_c)
        gated = load_chunk(cs, s) * gate
        update = gated.astype(BF16)
        grad_update[:, here] = update
        slope[:, here] = gated * (1.0 - gate)
        q_out[:, here] = dot(w_out[...], update, 1, 0) * gain_c

    loop(step)


def mix_kernel(recv, send, a_t, b_t, mixed):
    for c in range(NCOL):
        for t in range(TILES):
            for offset, out in ((0, a_t), (CHUNKS, b_t)):
                rows = slice(offset, offset + CHUNKS)
                first = recv[32 * t + c, rows].astype(F32)
                second = recv[32 * t + 16 + c, rows].astype(F32)
                even, odd = swap_halves(first, second)
                spot = slice(t * LANES, (t + 1) * LANES)
                out[32 * c : 32 * c + 16, spot] = even.astype(BF16)
                out[32 * c + 16 : 32 * c + 32, spot] = odd.astype(BF16)
    product = dot(b_t[...], a_t[...], 0, 0)
    for t in range(TILES):
        mixed[t] = product[:, t * LANES : (t + 1) * LANES]
    for c in range(NCOL):
        for t in range(TILES):
            first = mixed[t, pl.ds(32 * c, CHUNKS, stride=2), :]
            second = mixed[t, pl.ds(32 * c + 1, CHUNKS, stride=2), :]
            even, odd = swap_halves(first, second)
            send[32 * t + c] = even.astype(BF16)
            send[32 * t + 16 + c] = odd.astype(BF16)


def middle_kernel(recv, q_in, gain, bias, send, y_out):
    gain_c = column(gain[...])
    bias_c = column(bias[...])

    def step(s):
        here = lanes_of(s)
        mixed = recv[:, here].astype(F32)
        mean = jnp.mean(mixed, axis=0, keepdims=True)
        centred = mixed - mean
        inverse = lax.rsqrt(jnp.mean(centred * centred, axis=0, keepdims=True) + EPS)
        normed = centred * inverse
        y_out[:, here] = (normed * gain_c + bias_c).astype(BF16)
        q = q_in[:, here]
        first = jnp.mean(q, axis=0, keepdims=True)
        second = jnp.mean(q * normed, axis=0, keepdims=True)
        send[:, here] = ((q - first - normed * second) * inverse).astype(BF16)

    loop(step)


def gate_kernel(
    y, zn_t, slope, grad_update, aux, w_gate, w_out, w_proj,
    terms, half, factor, logit_t, wo_t, wp_t,
):
    wo_t[...] = w_out[...].astype(F32).T.astype(BF16)
    wp_t[...] = w_proj[...].astype(F32).T.astype(BF16)

    def step(s):
        here = lanes_of(s)
        update = dot(wo_t[...], y[:, here], 1, 0)
        grad_logit = (slope[:, here] * update).astype(BF16)
        logit_t[:, here] = grad_logit
        half[:, here] = dot(w_gate[...], grad_logit, 1, 0)
        mask = aux[0:1, here]
        proj = dot(wp_t[...], zn_t[:, here], 1, 0)
        gate_a = sigmoid(proj[:CH])
        gate_b = sigmoid(proj[2 * CH : 3 * CH])
        plain_a = mask * gate_a
        plain_b = mask * gate_b
        factor[0:CH, here] = plain_a * proj[CH : 2 * CH] * (1.0 - gate_a)
        factor[CH : 2 * CH, here] = plain_a
        factor[2 * CH : 3 * CH, here] = plain_b * proj[3 * CH :] * (1.0 - gate_b)
        factor[3 * CH : 4 * CH, here] = plain_b

    loop(step)
    terms[:CH] = dot(y[...], grad_update[...], 1, 1).astype(BF16)
    terms[CH:] = dot(zn_t[...], logit_t[...], 1, 1).astype(BF16)


def unmix_kernel(recv, a_t, b_t, send, strided, grad):
    for c in range(NCOL):
        for t in range(TILES):
            even, odd = swap_halves(
                recv[32 * t + c].astype(F32), recv[32 * t + 16 + c].astype(F32)
            )
            strided[t, pl.ds(32 * c, CHUNKS, stride=2), :] = even
            strided[t, pl.ds(32 * c + 1, CHUNKS, stride=2), :] = odd
    for t in range(TILES):
        grad[:, t * LANES : (t + 1) * LANES] = strided[t].astype(BF16)
    for offset, left, dim in ((0, b_t, 0), (CHUNKS, a_t, 1)):
        product = dot(left[...], grad[...], 1, dim)
        rows = slice(offset, offset + CHUNKS)
        for c in range(NCOL):
            for t in range(TILES):
                spot = slice(t * LANES, (t + 1) * LANES)
                even, odd = swap_halves(
                    product[32 * c : 32 * c + 16, spot], product[32 * c + 16 : 32 * c + 32, spot]
                )
                send[32 * t + c, rows] = even.astype(BF16)
                send[32 * t + 16 + c, rows] = odd.astype(BF16)


def back_kernel(recv, zn_t, factor, terms_in, terms, grad_p):
    def step(s):
        here = lanes_of(s)
        for part in range(4):
            rows = slice(part * CH, (part + 1) * CH)
            grad = recv[:, lanes_of(s, (part // 2) * PAIRS)].astype(F32)
            grad_p[rows, here] = (grad * factor[rows, here]).astype(BF16)

    loop(step)
    product = dot(zn_t[...], grad_p[...], 1, 1)
    for part in range(4):
        terms[part * CH : (part + 1) * CH] = product[:, part * CH : (part + 1) * CH].astype(BF16)
    terms[4 * CH : 6 * CH] = terms_in[...]
    terms[6 * CH :] = jnp.zeros((2 * CH, CH), BF16)


def last_kernel(grad_p, half, normed_t, aux, gain, w_proj, grad_pair, ys):
    gain_c = column(gain[...])

    def step(s):
        here = lanes_of(s)
        grad_zn = dot(w_proj[...], grad_p[:, here], 1, 0) + half[:, here]
        normed = normed_t[:, here]
        q = grad_zn * gain_c
        first = jnp.mean(q, axis=0, keepdims=True)
        second = jnp.mean(q * normed, axis=0, keepdims=True)
        store_chunk(ys, s, (q - first - normed * second) * aux[2:3, here])

    loop(step)
    grad_pair[...] = ys[...].reshape(ROWS, COLS, CH).astype(BF16)


def sum_kernel(parts, out):
    total = jnp.sum(parts[...].astype(F32), axis=0, keepdims=True) * (1.0 / N)
    out[...] = jnp.broadcast_to(total, out.shape).astype(BF16)


def split_kernel(sums, grad_proj, grad_gate, grad_out):
    whole = sums[...].astype(F32).reshape(8 * DEV, LANES)
    for part in range(4):
        grad_proj[:, part * CH : (part + 1) * CH] = whole[part * CH : (part + 1) * CH]
    grad_out[...] = whole[4 * CH : 5 * CH]
    grad_gate[...] = whole[5 * CH : 6 * CH]


def call(kernel, outs, scratch, flops, args, in_hbm=False, vmem=16):
    space = pltpu.HBM if in_hbm else pltpu.VMEM
    moved = sum(x.size * x.dtype.itemsize for x in args) + sum(
        x.size * x.dtype.itemsize for x in outs
    )
    if in_hbm:
        args = [pltpu.with_memory_space_constraint(x, pltpu.HBM) for x in args]
    return pl.pallas_call(
        kernel,
        out_shape=outs,
        in_specs=[pl.BlockSpec(memory_space=space)] * len(args),
        out_specs=[pl.BlockSpec(memory_space=pltpu.VMEM)] * len(outs),
        scratch_shapes=scratch,
        compiler_params=pltpu.CompilerParams(vmem_limit_bytes=vmem << 20),
        cost_estimate=pl.CostEstimate(flops=flops, bytes_accessed=moved, transcendentals=0),
    )(*args)


def exchange(x):
    return lax.all_to_all(x, AXES, 0, 0, tiled=True)


def split_rows(x):
    return x.reshape(DEV, -1, LANES)


def join_rows(x):
    return x.reshape(DEV, -1)


def body(
    pair,
    cotangent,
    res_mask,
    chain,
    ln_in_gain,
    ln_in_bias,
    w_proj,
    w_gate,
    chain_bias,
    ln_out_gain,
    ln_out_bias,
    w_out,
):
    S = jax.ShapeDtypeStruct
    V = pltpu.VMEM
    unit = 2 * PAIRS * CH * CH

    def flat(x):
        return x.reshape(1, -1)

    send_ab, zn_t, normed_t, aux = call(
        front_kernel,
        [S((CH, 2 * PAIRS), BF16), S((CH, PAIRS), BF16), S((CH, PAIRS), F32), S((8, PAIRS), F32)],
        [
            pltpu.SMEM((N,), jnp.int32), pltpu.SMEM((N,), jnp.int32), V((ROWS, COLS, CH), BF16),
            V((1, CH), F32), V((1, CH), F32), V((CH, 4 * CH), BF16),
            V((PAIRS, CH), F32), V((4 * CH, CH), BF16), pltpu.SemaphoreType.DMA((6,)),
        ],
        4 * unit,
        (res_mask, chain, pair, flat(ln_in_gain), flat(ln_in_bias), w_proj),
        in_hbm=True,
    )
    recv_ab = exchange(split_rows(send_ab))
    grad_update, q, slope = call(
        ahead_kernel,
        [S((CH, PAIRS), BF16), S((CH, PAIRS), F32), S((CH, PAIRS), F32)],
        [V((PAIRS, CH), F32), V((CH, CH), BF16)],
        2 * unit,
        (cotangent, zn_t, aux, w_gate, flat(chain_bias), flat(ln_out_gain), w_out),
    )
    recv_ab, grad_update, q, slope = lax.optimization_barrier((recv_ab, grad_update, q, slope))
    send_mixed, a_t, b_t = call(
        mix_kernel,
        [S((DEV, CHUNKS, LANES), BF16), S((N, N), BF16), S((N, N), BF16)],
        [V((TILES, N, LANES), F32)],
        2 * N * N * N,
        (recv_ab,),
    )
    send_grad, y = call(
        middle_kernel,
        [S((CH, PAIRS), BF16), S((CH, PAIRS), BF16)],
        [],
        0,
        (join_rows(exchange(send_mixed)), q, flat(ln_out_gain), flat(ln_out_bias)),
    )
    (send_back,) = call(
        unmix_kernel,
        [S((DEV, 2 * CHUNKS, LANES), BF16)],
        [V((TILES, N, LANES), F32), V((N, N), BF16)],
        4 * N * N * N,
        (exchange(split_rows(send_grad)), a_t, b_t),
    )
    send_back, y, slope = lax.optimization_barrier((send_back, y, slope))
    recv_back = exchange(send_back)
    terms_in, half, factor = call(
        gate_kernel,
        [S((2 * CH, CH), BF16), S((CH, PAIRS), F32), S((4 * CH, PAIRS), F32)],
        [V((CH, PAIRS), BF16), V((CH, CH), BF16), V((4 * CH, CH), BF16)],
        8 * unit,
        (y, zn_t, slope, grad_update, aux, w_gate, w_out, w_proj),
    )
    terms, grad_p = call(
        back_kernel,
        [S((8 * DEV, CH), BF16), S((4 * CH, PAIRS), BF16)],
        [],
        4 * unit,
        (join_rows(recv_back), zn_t, factor, terms_in),
    )
    parts = exchange(split_rows(terms))
    (summed,) = call(sum_kernel, [S((DEV, 8, LANES), BF16)], [], 0, (parts,))
    summed, grad_p, half = lax.optimization_barrier((summed, grad_p, half))
    sums = exchange(summed)
    (grad_pair,) = call(
        last_kernel,
        [S((ROWS, COLS, CH), BF16)],
        [V((PAIRS, CH), F32)],
        4 * unit,
        (grad_p, half, normed_t, aux, flat(ln_in_gain), w_proj),
    )
    grad_proj, grad_gate, grad_out = call(
        split_kernel, [S((CH, 4 * CH), F32), S((CH, CH), F32), S((CH, CH), F32)], [], 0, (sums,)
    )
    return (grad_pair, grad_proj, grad_gate, grad_out)


def solution(mesh):
    return jax.shard_map(
        body,
        mesh=mesh,
        in_specs=(P("row", "col", None), P("row", "col", None)) + (P(),) * 10,
        out_specs=(P("row", "col", None), P(), P(), P()),
        check_vma=False,
    )
```

time: 183 us -> 139 us (0.76)
  blocking collectives: 125 us -> 51.7 us
  waiting for transfers between devices: 0 us -> 33.7 us
  starting transfers between devices: 0 us -> 20.5 us
  Pallas kernels: 32.5 us -> 17.9 us
  local copies, waits for them, and re-layouts: 23.1 us -> 14.3 us
    all_to_all x6 -> x3, blocking collectives: 125 us -> 51.7 us  [exchange(): return lax.all_to_all(x, AXES, 0, 0, tiled=True)]
    all_to_all x0 -> x3, waiting for transfers between devices: none -> 33.7 us  [exchange(): return lax.all_to_all(x, AXES, 0, 0, tiled=True)]
    all_to_all x0 -> x3, starting transfers between devices: none -> 20.5 us  [exchange(): return lax.all_to_all(x, AXES, 0, 0, tiled=True)]
    pallas_call x6 -> x10, Pallas kernels: 32.5 us -> 17.9 us  [call(): pl.pallas_call(kernel, out_shape=outs, in_specs=[pl.BlockSpec(memory_spac...]
    reshape x6 -> x0, local copies, waits for them, and re-layouts: 6.6 us -> none  [the longest x4 3.68 us: exchange(): split = x.reshape(DEV, -1, LANES)]
    all_to_all x2 -> x0, local copies, waits for them, and re-layouts: 3.93 us -> none  [exchange(): return lax.all_to_all(split, AXES, 0, 0, tiled=True).reshape(x.shape)]
    unnamed x48 -> x44, local copies, waits for them, and re-layouts: 10.8 us -> 14.3 us
  transfers between devices with their start and end apart: 0 -> 3, of which waited for: 0 -> 3; matrix products, arithmetic and copies ran while one was open for 0% -> 0% of each run, Pallas kernels for 0% -> 5%
where the time goes in v2:
time: 139 us
  blocking collectives  51.7 us (37%)
  waiting for transfers between devices  33.7 us (24%)
  starting transfers between devices  20.5 us (15%)
  Pallas kernels  17.9 us (13%)
  local copies, waits for them, and re-layouts  14.3 us (10%)
    all_to_all x3, blocking collectives, exchange(): return lax.all_to_all(x, AXES, 0, 0, tiled=True)  51.7 us
    all_to_all x3, waiting for transfers between devices, exchange(): return lax.all_to_all(x, AXES, 0, 0, tiled=True)  33.7 us
    all_to_all x3, starting transfers between devices, exchange(): return lax.all_to_all(x, AXES, 0, 0, tiled=True)  20.5 us
    pallas_call x10, Pallas kernels, call(): pl.pallas_call(kernel, out_shape=outs, in_specs=[pl.BlockSpec(memory_spac...  17.9 us
    unnamed x44, local copies, waits for them, and re-layouts  14.3 us
  transfers between devices with their start and end apart: 3, of which 3 were waited for; matrix products, arithmetic and copies ran while one was open for 0% of the time, Pallas kernels for 5%

profile of v2, /device:TPU:1, one launch (start us, length us, event | category | flops | bytes accessed | tf_op | source)
XLA Modules:
  0.0 138.9 jit_solution(896155153425040842)
XLA Ops:
  0.7 3.6 %shard_map.147 = (bf16[128,4096]{1,0:T(8,128)(2,1)S(1)}, bf16[128,2048]{1,0:T(8,128)(2,1)S(1)}, f32[128,2048]{1,0:T(8,128)S(1)}, f32[8,2048]{1,0:T(8,128)S(1)}) custom-call(s32[512]{0:T(512)} %mask_h.1, s32[512]{0:T(512)} %chain_h.1, bf16[64,32,128]{2,1,0:T(8,128)(2,1)} %pair_h.1, f32[1,128]{1,0:T(1,128)} %bitcast.27, f32[1,128]{1,0:T(1,128)} %bitcast.31, ...), custom_call_target="tpu_custom_call" | custom-call | flops 268435456 | bytes 3347456 | tf_op jit(solution)/shard_map/pallas_call | solution.py:304
  4.3 1.0 copy-done.2
  5.3 1.2 copy.16
  6.5 11.5 %all-to-all-start = ((bf16[128,32,128]{2,1,0:T(8,128)(2,1)}), bf16[128,32,128]{2,1,0:T(8,128)(2,1)S(1)}, u32[]{:S(2)}, u32[]{:S(2)}) async-start(bf16[128,32,128]{2,1,0:T(8,128)(2,1)} %bitcast.7), calls=%async_computation | async-start | bytes 2097152 | tf_op jit(solution)/shard_map/all_to_all | solution.py:316
  18.0 1.7 %shard_map.148 = (bf16[128,2048]{1,0:T(8,128)(2,1)S(1)}, f32[128,2048]{1,0:T(8,128)S(1)}, f32[128,2048]{1,0:T(8,128)S(1)}) custom-call(bf16[64,32,128]{2,1,0:T(8,128)(2,1)S(1)} %copy-done.9, bf16[128,2048]{1,0:T(8,128)(2,1)S(1)} %get-tuple-element.35.zn_t, f32[8,2048]{1,0:T(8,128)S(1)} %get-tuple-element.36.aux, bf16[128,128]{1,0:T(8,128)(2,1)S(1)} %copy-done.14, ...), custom_call_target="tpu_custom_call" | custom-call | flops 134217728 | bytes 3802112 | tf_op jit(solution)/shard_map/pallas_call | solution.py:304
  19.8 1.0 copy-done.6
  20.7 0.8 copy-done.10
  21.6 15.1 %all-to-all-done.recv = bf16[128,32,128]{2,1,0:T(8,128)(2,1)S(1)} async-done(((bf16[128,32,128]{2,1,0:T(8,128)(2,1)}), bf16[128,32,128]{2,1,0:T(8,128)(2,1)S(1)}, u32[]{:S(2)}, u32[]{:S(2)}) %all-to-all-start) | async-done | bytes 1048608 | tf_op jit(solution)/shard_map/all_to_all | solution.py:316
  36.7 1.0 shard_map.149
  37.8 18.2 %all_to_all.30 = bf16[128,16,128]{2,1,0:T(8,128)(2,1)S(1)} all-to-all(bf16[128,16,128]{2,1,0:T(8,128)(2,1)S(1)} %get-tuple-element.41), channel_id=1, replica_groups=mesh['row'=8,'col'=16] {'row','col'}, dimensions={0} | all-to-all | bytes 1048576 | tf_op jit(solution)/shard_map/all_to_all | solution.py:316
  55.9 0.1 copy.23
  56.1 0.9 shard_map.150
  57.0 0.1 copy.18
  57.2 0.7 copy-done.12
  57.8 17.7 %all_to_all.31.recv = bf16[128,16,128]{2,1,0:T(8,128)(2,1)S(1)} all-to-all(bf16[128,16,128]{2,1,0:T(8,128)(2,1)S(1)} %bitcast.30), channel_id=1, replica_groups=mesh['row'=8,'col'=16] {'row','col'}, dimensions={0} | all-to-all | bytes 1048576 | tf_op jit(solution)/shard_map/all_to_all | solution.py:316
  75.6 2.0 %shard_map.151 = bf16[128,32,128]{2,1,0:T(8,128)(2,1)} custom-call(bf16[128,16,128]{2,1,0:T(8,128)(2,1)S(1)} %all_to_all.31.recv, bf16[512,512]{1,0:T(8,128)(2,1)S(1)} %get-tuple-element.44.a_t, bf16[512,512]{1,0:T(8,128)(2,1)S(1)} %get-tuple-element.45.b_t), custom_call_target="tpu_custom_call" | custom-call | flops 536870912 | bytes 2621440 | tf_op jit(solution)/shard_map/pallas_call | solution.py:304
  77.5 4.9 %all-to-all-start.3 = ((bf16[128,32,128]{2,1,0:T(8,128)(2,1)}), bf16[128,32,128]{2,1,0:T(8,128)(2,1)}, u32[]{:S(2)}, u32[]{:S(2)}) async-start(bf16[128,32,128]{2,1,0:T(8,128)(2,1)} %shard_map.151), calls=%async_computation.3 | async-start | bytes 2097152 | tf_op jit(solution)/shard_map/all_to_all | solution.py:316
  82.5 2.7 %shard_map.152 = (bf16[256,128]{1,0:T(8,128)(2,1)S(1)}, f32[128,2048]{1,0:T(8,128)S(1)}, f32[512,2048]{1,0:T(8,128)S(1)}) custom-call(bf16[128,2048]{1,0:T(8,128)(2,1)S(1)} %copy-done.13, bf16[128,2048]{1,0:T(8,128)(2,1)S(1)} %get-tuple-element.35.zn_t, f32[128,2048]{1,0:T(8,128)S(1)} %copy-done.7, bf16[128,2048]{1,0:T(8,128)(2,1)S(1)} %copy-done.11, ...), custom_call_target="tpu_custom_call" | custom-call | flops 536870912 | bytes 8192000 | tf_op jit(solution)/shard_map/pallas_call | solution.py:304
  85.2 2.0 %copy-done = f32[512,2048]{1,0:T(8,128)} copy-done((f32[512,2048]{1,0:T(8,128)}, f32[512,2048]{1,0:T(8,128)S(1)}, u32[]{:S(2)}) %copy-start) | copy-done | bytes 4194328
  87.2 1.1 copy-done.4
  88.2 12.7 %all-to-all-done.3 = bf16[128,32,128]{2,1,0:T(8,128)(2,1)} async-done(((bf16[128,32,128]{2,1,0:T(8,128)(2,1)}), bf16[128,32,128]{2,1,0:T(8,128)(2,1)}, u32[]{:S(2)}, u32[]{:S(2)}) %all-to-all-start.3) | async-done | bytes 1048608 | tf_op jit(solution)/shard_map/all_to_all | solution.py:316
  101.0 1.7 %copy.22 = bf16[16,8,32,128]{3,1,2,0:T(8,128)(2,1)S(1)} copy(bf16[16,8,32,128]{3,2,1,0:T(8,128)(2,1)} %bitcast.12) | data formatting | bytes 2097152
  102.7 2.2 %copy-done.1 = f32[512,2048]{1,0:T(8,128)S(1)} copy-done((f32[512,2048]{1,0:T(8,128)S(1)}, f32[512,2048]{1,0:T(8,128)}, u32[]{:S(2)}) %copy-start.1) | copy-done | bytes 4194328
  104.8 1.3 shard_map.153
  106.1 15.7 %all_to_all.32.parts = bf16[128,8,128]{2,1,0:T(8,128)(2,1)S(1)} all-to-all(bf16[128,8,128]{2,1,0:T(8,128)(2,1)S(1)} %bitcast.22), channel_id=1, replica_groups=mesh['row'=8,'col'=16] {'row','col'}, dimensions={0} | all-to-all | bytes 524288 | tf_op jit(solution)/shard_map/all_to_all | solution.py:316
  121.9 0.9 shard_map.154
  122.7 4.1 %all-to-all-start.5 = ((bf16[128,8,128]{2,1,0:T(8,128)(2,1)}), bf16[128,8,128]{2,1,0:T(8,128)(2,1)S(1)}, u32[]{:S(2)}, u32[]{:S(2)}) async-start(bf16[128,8,128]{2,1,0:T(8,128)(2,1)} %shard_map.154), calls=%async_computation.5 | async-start | bytes 524288 | tf_op jit(solution)/shard_map/all_to_all | solution.py:316
  126.8 1.2 copy-done.3
  128.0 1.2 copy-done.5
  129.3 3.1 %shard_map.155 = bf16[64,32,128]{2,1,0:T(8,128)(2,1)} custom-call(bf16[512,2048]{1,0:T(8,128)(2,1)S(1)} %get-tuple-element.57.grad_p, f32[128,2048]{1,0:T(8,128)S(1)} %copy-done.5, f32[128,2048]{1,0:T(8,128)S(1)} %copy-done.3, f32[8,2048]{1,0:T(8,128)S(1)} %get-tuple-element.36.aux, f32[1,128]{1,0:T(1,128)S(1)} %bitcast.28, bf16[128,512]{1,0:T(8,128)(2,1)S(1)} %copy-done.8), custom_call_target="tpu_custom_call" | custom-call | flops 268435456 | bytes 4915712 | tf_op jit(solution)/shard_map/pallas_call | solution.py:304
  132.3 5.8 %all-to-all-done.5.sums = bf16[128,8,128]{2,1,0:T(8,128)(2,1)S(1)} async-done(((bf16[128,8,128]{2,1,0:T(8,128)(2,1)}), bf16[128,8,128]{2,1,0:T(8,128)(2,1)S(1)}, u32[]{:S(2)}, u32[]{:S(2)}) %all-to-all-start.5) | async-done | bytes 262176 | tf_op jit(solution)/shard_map/all_to_all | solution.py:316
  138.1 0.8 shard_map.156
  (31 shorter events, 0.1 us)
Async XLA Ops:
  0.6 17.4 %copy-start.15 = (bf16[128,128]{1,0:T(8,128)(2,1)S(1)}, bf16[128,128]{1,0:T(8,128)(2,1)}, u32[]{:S(2)}) copy-start(bf16[128,128]{1,0:T(8,128)(2,1)} %w_out.3) | copy-start | bytes 98308
  0.6 17.4 %copy-start.14 = (bf16[128,128]{1,0:T(8,128)(2,1)S(1)}, bf16[128,128]{1,0:T(8,128)(2,1)}, u32[]{:S(2)}) copy-start(bf16[128,128]{1,0:T(8,128)(2,1)} %w_gate.3) | copy-start | bytes 98308
  0.7 17.4 %copy-start.16 = (f32[128]{0:T(128)S(1)}, f32[128]{0:T(128)}, u32[]{:S(2)}) copy-start(f32[128]{0:T(128)} %param.21) | copy-start | bytes 1540
  0.7 17.4 %copy-start.17 = (f32[128]{0:T(128)S(1)}, f32[128]{0:T(128)}, u32[]{:S(2)}) copy-start(f32[128]{0:T(128)} %param.20) | copy-start | bytes 1540
  0.7 17.4 %copy-start.9 = (bf16[64,32,128]{2,1,0:T(8,128)(2,1)S(1)}, bf16[64,32,128]{2,1,0:T(8,128)(2,1)}, u32[]{:S(2)}) copy-start(bf16[64,32,128]{2,1,0:T(8,128)(2,1)} %cot.1) | copy-start | bytes 1572868
  4.3 1.0 copy-start.2
  5.3 50.8 %copy-start.18 = (f32[128]{0:T(128)S(1)}, f32[128]{0:T(128)}, u32[]{:S(2)}) copy-start(f32[128]{0:T(128)} %param.22) | copy-start | bytes 1540
  6.5 30.2 %all-to-all-start = ((bf16[128,32,128]{2,1,0:T(8,128)(2,1)}), bf16[128,32,128]{2,1,0:T(8,128)(2,1)S(1)}, u32[]{:S(2)}, u32[]{:S(2)}) async-start(bf16[128,32,128]{2,1,0:T(8,128)(2,1)} %bitcast.7), calls=%async_computation | async-start | bytes 2097152 | tf_op jit(solution)/shard_map/all_to_all | solution.py:316
  19.8 1.0 copy-start.6
  20.7 0.8 copy-start.10
  56.1 26.4 %copy-start.7 = (f32[128,2048]{1,0:T(8,128)S(1)}, f32[128,2048]{1,0:T(8,128)}, u32[]{:S(2)}) copy-start(f32[128,2048]{1,0:T(8,128)} %copy-done.6) | copy-start | bytes 3145732
  56.1 26.4 %copy-start.8 = (bf16[128,512]{1,0:T(8,128)(2,1)S(1)}, bf16[128,512]{1,0:T(8,128)(2,1)}, u32[]{:S(2)}) copy-start(bf16[128,512]{1,0:T(8,128)(2,1)} %w_proj.3) | copy-start | bytes 393220
  56.1 26.4 %copy-start.11 = (bf16[128,2048]{1,0:T(8,128)(2,1)S(1)}, bf16[128,2048]{1,0:T(8,128)(2,1)}, u32[]{:S(2)}) copy-start(bf16[128,2048]{1,0:T(8,128)(2,1)} %copy-done.10) | copy-start | bytes 1572868
  57.0 0.8 copy-start.12
  57.8 24.7 %copy-start.13 = (bf16[128,2048]{1,0:T(8,128)(2,1)S(1)}, bf16[128,2048]{1,0:T(8,128)(2,1)}, u32[]{:S(2)}) copy-start(bf16[128,2048]{1,0:T(8,128)(2,1)} %copy-done.12) | copy-start | bytes 1572868
  77.5 23.4 %all-to-all-start.3 = ((bf16[128,32,128]{2,1,0:T(8,128)(2,1)}), bf16[128,32,128]{2,1,0:T(8,128)(2,1)}, u32[]{:S(2)}, u32[]{:S(2)}) async-start(bf16[128,32,128]{2,1,0:T(8,128)(2,1)} %shard_map.151), calls=%async_computation.3 | async-start | bytes 2097152 | tf_op jit(solution)/shard_map/all_to_all | solution.py:316
  85.2 2.0 %copy-start = (f32[512,2048]{1,0:T(8,128)}, f32[512,2048]{1,0:T(8,128)S(1)}, u32[]{:S(2)}) copy-start(f32[512,2048]{1,0:T(8,128)S(1)} %get-tuple-element.52.factor) | copy-start | bytes 12582916
  87.2 1.1 copy-start.4
  102.6 24.2 %copy-start.19 = (f32[128]{0:T(128)S(1)}, f32[128]{0:T(128)}, u32[]{:S(2)}) copy-start(f32[128]{0:T(128)} %param.16) | copy-start | bytes 1540
  102.6 2.2 %copy-start.1 = (f32[512,2048]{1,0:T(8,128)S(1)}, f32[512,2048]{1,0:T(8,128)}, u32[]{:S(2)}) copy-start(f32[512,2048]{1,0:T(8,128)} %copy-done) | copy-start | bytes 12582916
  122.7 15.4 %all-to-all-start.5 = ((bf16[128,8,128]{2,1,0:T(8,128)(2,1)}), bf16[128,8,128]{2,1,0:T(8,128)(2,1)S(1)}, u32[]{:S(2)}, u32[]{:S(2)}) async-start(bf16[128,8,128]{2,1,0:T(8,128)(2,1)} %shard_map.154), calls=%async_computation.5 | async-start | bytes 524288 | tf_op jit(solution)/shard_map/all_to_all | solution.py:316
  126.8 1.2 copy-start.3
  128.0 1.2 copy-start.5

commit v3 on v2

--- a/solution.py
+++ b/solution.py
@@ -10,7 +10,7 @@
 EPS = 1e-05
 F32 = jnp.float32
 BF16 = jnp.bfloat16
-AXES = ("row", "col")
+AXES = ("col", "row")
 
 ROWS = 64
 COLS = 32
@@ -25,6 +25,7 @@
 WIDE = 256
 STEPS = PAIRS // WIDE
 EACH = WIDE // ROWS
+PIECES = 4
 TILES = N // LANES
 
 
@@ -76,21 +77,25 @@
 
 def front_kernel(
     mask_h, chain_h, pair_h, gain_h, bias_h, w_h,
-    send, zn_t, normed_t, aux,
+    send, zn_t, aux,
     mask_s, chain_s, pair, gain, bias, w_proj, xs, w_t, sems,
 ):
-    copies = [
+    small = [
         pltpu.make_async_copy(src, dst, sems.at[n])
         for n, (src, dst) in enumerate(
             (
-                (pair_h, pair), (w_h, w_proj), (gain_h, gain), (bias_h, bias),
-                (mask_h, mask_s), (chain_h, chain_s),
+                (w_h, w_proj), (gain_h, gain), (bias_h, bias), (mask_h, mask_s),
+                (chain_h, chain_s),
             )
         )
     ]
-    for copy in copies:
+    pieces = []
+    for n in range(PIECES):
+        spot = slice(n * COLS // PIECES, (n + 1) * COLS // PIECES)
+        pieces.append(pltpu.make_async_copy(pair_h.at[:, spot], pair.at[:, spot], sems.at[5 + n]))
+    for copy in small + pieces:
         copy.start()
-    for copy in copies[1:]:
+    for copy in small:
         copy.wait()
     row_start = lax.axis_index("row") * ROWS
     col_start = lax.axis_index("col") * COLS
@@ -106,11 +111,9 @@
         mask_row = jnp.where(here, mask_s[row_start + i], mask_row)
         chain_row = jnp.where(here, chain_s[row_start + i], chain_row)
     low = lane < ROWS
-    copies[0].wait()
-    xs[...] = pair[...].astype(F32).reshape(PAIRS, CH)
 
     def step(s):
-        x = load_chunk(xs, s)
+        x = load_chunk(xs.reshape(PAIRS, CH), s)
         mean = jnp.mean(x, axis=0, keepdims=True)
         centred = x - mean
         inverse = lax.rsqrt(jnp.mean(centred * centred, axis=0, keepdims=True) + EPS)
@@ -128,28 +131,46 @@
         send[:, lanes_of(s)] = act_a.astype(BF16)
         send[:, lanes_of(s, PAIRS)] = act_b.astype(BF16)
         zn_t[:, lanes_of(s)] = zn
-        normed_t[:, lanes_of(s)] = normed
         aux[0:1, lanes_of(s)] = mask
         aux[1:2, lanes_of(s)] = jnp.concatenate(same, axis=1)
-        aux[2:3, lanes_of(s)] = inverse
-
-    loop(step)
-
-
-def ahead_kernel(cot, zn_t, aux, w_gate, chain_bias, gain, w_out, grad_update, q_out, slope, cs, wg_t):
+
+    for n in range(PIECES):
+        pieces[n].wait()
+        spot = slice(n * COLS // PIECES, (n + 1) * COLS // PIECES)
+        xs[:, spot] = pair[:, spot].astype(F32)
+        for u in range(STEPS // PIECES):
+            step(n * (STEPS // PIECES) + u)
+
+
+def ahead_kernel(
+    cot, zn_t, aux, w_gate, chain_bias, gain, w_out, w_proj,
+    grad_update, q_out, slope, factor, cs, wg_t, wp_t,
+):
     cs[...] = cot[...].astype(F32).reshape(PAIRS, CH)
     wg_t[...] = w_gate[...].astype(F32).T.astype(BF16)
+    wp_t[...] = w_proj[...].astype(F32).T.astype(BF16)
     gain_c = column(gain[...])
     chain_c = column(chain_bias[...])
 
     def step(s):
         here = lanes_of(s)
-        gate = sigmoid(dot(wg_t[...], zn_t[:, here], 1, 0) + aux[1:2, here] * chain_c)
+        zn = zn_t[:, here]
+        gate = sigmoid(dot(wg_t[...], zn, 1, 0) + aux[1:2, here] * chain_c)
         gated = load_chunk(cs, s) * gate
         update = gated.astype(BF16)
         grad_update[:, here] = update
         slope[:, here] = gated * (1.0 - gate)
         q_out[:, here] = dot(w_out[...], update, 1, 0) * gain_c
+        mask = aux[0:1, here]
+        proj = dot(wp_t[...], zn, 1, 0)
+        gate_a = sigmoid(proj[:CH])
+        gate_b = sigmoid(proj[2 * CH : 3 * CH])
+        plain_a = mask * gate_a
+        plain_b = mask * gate_b
+        factor[0:CH, here] = plain_a * proj[CH : 2 * CH] * (1.0 - gate_a)
+        factor[CH : 2 * CH, here] = plain_a
+        factor[2 * CH : 3 * CH, here] = plain_b * proj[3 * CH :] * (1.0 - gate_b)
+        factor[3 * CH : 4 * CH, here] = plain_b
 
     loop(step)
 
@@ -159,8 +180,8 @@
         for t in range(TILES):
             for offset, out in ((0, a_t), (CHUNKS, b_t)):
                 rows = slice(offset, offset + CHUNKS)
-                first = recv[32 * t + c, rows].astype(F32)
-                second = recv[32 * t + 16 + c, rows].astype(F32)
+                first = recv[8 * c + 2 * t, rows].astype(F32)
+                second = recv[8 * c + 2 * t + 1, rows].astype(F32)
                 even, odd = swap_halves(first, second)
                 spot = slice(t * LANES, (t + 1) * LANES)
                 out[32 * c : 32 * c + 16, spot] = even.astype(BF16)
@@ -173,8 +194,8 @@
             first = mixed[t, pl.ds(32 * c, CHUNKS, stride=2), :]
             second = mixed[t, pl.ds(32 * c + 1, CHUNKS, stride=2), :]
             even, odd = swap_halves(first, second)
-            send[32 * t + c] = even.astype(BF16)
-            send[32 * t + 16 + c] = odd.astype(BF16)
+            send[8 * c + 2 * t] = even.astype(BF16)
+            send[8 * c + 2 * t + 1] = odd.astype(BF16)
 
 
 def middle_kernel(recv, q_in, gain, bias, send, y_out):
@@ -197,40 +218,11 @@
     loop(step)
 
 
-def gate_kernel(
-    y, zn_t, slope, grad_update, aux, w_gate, w_out, w_proj,
-    terms, half, factor, logit_t, wo_t, wp_t,
-):
-    wo_t[...] = w_out[...].astype(F32).T.astype(BF16)
-    wp_t[...] = w_proj[...].astype(F32).T.astype(BF16)
-
-    def step(s):
-        here = lanes_of(s)
-        update = dot(wo_t[...], y[:, here], 1, 0)
-        grad_logit = (slope[:, here] * update).astype(BF16)
-        logit_t[:, here] = grad_logit
-        half[:, here] = dot(w_gate[...], grad_logit, 1, 0)
-        mask = aux[0:1, here]
-        proj = dot(wp_t[...], zn_t[:, here], 1, 0)
-        gate_a = sigmoid(proj[:CH])
-        gate_b = sigmoid(proj[2 * CH : 3 * CH])
-        plain_a = mask * gate_a
-        plain_b = mask * gate_b
-        factor[0:CH, here] = plain_a * proj[CH : 2 * CH] * (1.0 - gate_a)
-        factor[CH : 2 * CH, here] = plain_a
-        factor[2 * CH : 3 * CH, here] = plain_b * proj[3 * CH :] * (1.0 - gate_b)
-        factor[3 * CH : 4 * CH, here] = plain_b
-
-    loop(step)
-    terms[:CH] = dot(y[...], grad_update[...], 1, 1).astype(BF16)
-    terms[CH:] = dot(zn_t[...], logit_t[...], 1, 1).astype(BF16)
-
-
 def unmix_kernel(recv, a_t, b_t, send, strided, grad):
     for c in range(NCOL):
         for t in range(TILES):
             even, odd = swap_halves(
-                recv[32 * t + c].astype(F32), recv[32 * t + 16 + c].astype(F32)
+                recv[8 * c + 2 * t].astype(F32), recv[8 * c + 2 * t + 1].astype(F32)
             )
             strided[t, pl.ds(32 * c, CHUNKS, stride=2), :] = even
             strided[t, pl.ds(32 * c + 1, CHUNKS, stride=2), :] = odd
@@ -245,13 +237,19 @@
                 even, odd = swap_halves(
                     product[32 * c : 32 * c + 16, spot], product[32 * c + 16 : 32 * c + 32, spot]
                 )
-                send[32 * t + c, rows] = even.astype(BF16)
-                send[32 * t + 16 + c, rows] = odd.astype(BF16)
-
-
-def back_kernel(recv, zn_t, factor, terms_in, terms, grad_p):
+                send[8 * c + 2 * t, rows] = even.astype(BF16)
+                send[8 * c + 2 * t + 1, rows] = odd.astype(BF16)
+
+
+def back_kernel(
+    recv, zn_t, factor, y, slope, grad_update, w_out, terms, grad_p, logit_t, wo_t
+):
+    wo_t[...] = w_out[...].astype(F32).T.astype(BF16)
+
     def step(s):
         here = lanes_of(s)
+        update = dot(wo_t[...], y[:, here], 1, 0)
+        logit_t[:, here] = (slope[:, here] * update).astype(BF16)
         for part in range(4):
             rows = slice(part * CH, (part + 1) * CH)
             grad = recv[:, lanes_of(s, (part // 2) * PAIRS)].astype(F32)
@@ -261,24 +259,29 @@
     product = dot(zn_t[...], grad_p[...], 1, 1)
     for part in range(4):
         terms[part * CH : (part + 1) * CH] = product[:, part * CH : (part + 1) * CH].astype(BF16)
-    terms[4 * CH : 6 * CH] = terms_in[...]
+    terms[4 * CH : 5 * CH] = dot(y[...], grad_update[...], 1, 1).astype(BF16)
+    terms[5 * CH : 6 * CH] = dot(zn_t[...], logit_t[...], 1, 1).astype(BF16)
     terms[6 * CH :] = jnp.zeros((2 * CH, CH), BF16)
 
 
-def last_kernel(grad_p, half, normed_t, aux, gain, w_proj, grad_pair, ys):
+def last_kernel(grad_p, logit_t, pair, gain, w_proj, w_gate, grad_pair, xs):
     gain_c = column(gain[...])
+    xs[...] = pair[...].astype(F32).reshape(PAIRS, CH)
 
     def step(s):
         here = lanes_of(s)
-        grad_zn = dot(w_proj[...], grad_p[:, here], 1, 0) + half[:, here]
-        normed = normed_t[:, here]
+        grad_zn = dot(w_proj[...], grad_p[:, here], 1, 0) + dot(w_gate[...], logit_t[:, here], 1, 0)
+        x = load_chunk(xs, s)
+        centred = x - jnp.mean(x, axis=0, keepdims=True)
+        inverse = lax.rsqrt(jnp.mean(centred * centred, axis=0, keepdims=True) + EPS)
+        normed = centred * inverse
         q = grad_zn * gain_c
         first = jnp.mean(q, axis=0, keepdims=True)
         second = jnp.mean(q * normed, axis=0, keepdims=True)
-        store_chunk(ys, s, (q - first - normed * second) * aux[2:3, here])
+        store_chunk(xs, s, (q - first - normed * second) * inverse)
 
     loop(step)
-    grad_pair[...] = ys[...].reshape(ROWS, COLS, CH).astype(BF16)
+    grad_pair[...] = xs[...].reshape(ROWS, COLS, CH).astype(BF16)
 
 
 def sum_kernel(parts, out):
@@ -345,27 +348,33 @@
     def flat(x):
         return x.reshape(1, -1)
 
-    send_ab, zn_t, normed_t, aux = call(
+    send_ab, zn_t, aux = call(
         front_kernel,
-        [S((CH, 2 * PAIRS), BF16), S((CH, PAIRS), BF16), S((CH, PAIRS), F32), S((8, PAIRS), F32)],
+        [S((CH, 2 * PAIRS), BF16), S((CH, PAIRS), BF16), S((8, PAIRS), F32)],
         [
             pltpu.SMEM((N,), jnp.int32), pltpu.SMEM((N,), jnp.int32), V((ROWS, COLS, CH), BF16),
             V((1, CH), F32), V((1, CH), F32), V((CH, 4 * CH), BF16),
-            V((PAIRS, CH), F32), V((4 * CH, CH), BF16), pltpu.SemaphoreType.DMA((6,)),
+            V((ROWS, COLS, CH), F32), V((4 * CH, CH), BF16),
+            pltpu.SemaphoreType.DMA((5 + PIECES,)),
         ],
         4 * unit,
         (res_mask, chain, pair, flat(ln_in_gain), flat(ln_in_bias), w_proj),
         in_hbm=True,
     )
     recv_ab = exchange(split_rows(send_ab))
-    grad_update, q, slope = call(
+    grad_update, q, slope, factor = call(
         ahead_kernel,
-        [S((CH, PAIRS), BF16), S((CH, PAIRS), F32), S((CH, PAIRS), F32)],
-        [V((PAIRS, CH), F32), V((CH, CH), BF16)],
-        2 * unit,
-        (cotangent, zn_t, aux, w_gate, flat(chain_bias), flat(ln_out_gain), w_out),
-    )
-    recv_ab, grad_update, q, slope = lax.optimization_barrier((recv_ab, grad_update, q, slope))
+        [
+            S((CH, PAIRS), BF16), S((CH, PAIRS), F32), S((CH, PAIRS), F32),
+            S((4 * CH, PAIRS), F32),
+        ],
+        [V((PAIRS, CH), F32), V((CH, CH), BF16), V((4 * CH, CH), BF16)],
+        6 * unit,
+        (cotangent, zn_t, aux, w_gate, flat(chain_bias), flat(ln_out_gain), w_out, w_proj),
+    )
+    recv_ab, grad_update, q, slope, factor = lax.optimization_barrier(
+        (recv_ab, grad_update, q, slope, factor)
+    )
     send_mixed, a_t, b_t = call(
         mix_kernel,
         [S((DEV, CHUNKS, LANES), BF16), S((N, N), BF16), S((N, N), BF16)],
@@ -387,32 +396,23 @@
         4 * N * N * N,
         (exchange(split_rows(send_grad)), a_t, b_t),
     )
-    send_back, y, slope = lax.optimization_barrier((send_back, y, slope))
-    recv_back = exchange(send_back)
-    terms_in, half, factor = call(
-        gate_kernel,
-        [S((2 * CH, CH), BF16), S((CH, PAIRS), F32), S((4 * CH, PAIRS), F32)],
-        [V((CH, PAIRS), BF16), V((CH, CH), BF16), V((4 * CH, CH), BF16)],
-        8 * unit,
-        (y, zn_t, slope, grad_update, aux, w_gate, w_out, w_proj),
-    )
-    terms, grad_p = call(
+    terms, grad_p, logit_t = call(
         back_kernel,
-        [S((8 * DEV, CH), BF16), S((4 * CH, PAIRS), BF16)],
-        [],
-        4 * unit,
-        (join_rows(recv_back), zn_t, factor, terms_in),
+        [S((8 * DEV, CH), BF16), S((4 * CH, PAIRS), BF16), S((CH, PAIRS), BF16)],
+        [V((CH, CH), BF16)],
+        7 * unit,
+        (join_rows(exchange(send_back)), zn_t, factor, y, slope, grad_update, w_out),
     )
     parts = exchange(split_rows(terms))
     (summed,) = call(sum_kernel, [S((DEV, 8, LANES), BF16)], [], 0, (parts,))
-    summed, grad_p, half = lax.optimization_barrier((summed, grad_p, half))
+    summed, grad_p, logit_t = lax.optimization_barrier((summed, grad_p, logit_t))
     sums = exchange(summed)
     (grad_pair,) = call(
         last_kernel,
         [S((ROWS, COLS, CH), BF16)],
         [V((PAIRS, CH), F32)],
-        4 * unit,
-        (grad_p, half, normed_t, aux, flat(ln_in_gain), w_proj),
+        5 * unit,
+        (grad_p, logit_t, pair, flat(ln_in_gain), w_proj, w_gate),
     )
     grad_proj, grad_gate, grad_out = call(
         split_kernel, [S((CH, 4 * CH), F32), S((CH, CH), F32), S((CH, CH), F32)], [], 0, (sums,)

time: 139 us -> 135 us (0.971)
  blocking collectives: 51.7 us -> 75.5 us
  waiting for transfers between devices: 33.7 us -> 15.5 us
  local copies, waits for them, and re-layouts: 14.3 us -> 8.89 us
  starting transfers between devices: 20.5 us -> 16.4 us
    all_to_all x3 -> x4, blocking collectives: 51.7 us -> 75.5 us  [exchange(): return lax.all_to_all(x, AXES, 0, 0, tiled=True)]
    all_to_all x3 -> x2, waiting for transfers between devices: 33.7 us -> 15.5 us  [exchange(): return lax.all_to_all(x, AXES, 0, 0, tiled=True)]
    unnamed x44 -> x40, local copies, waits for them, and re-layouts: 14.3 us -> 8.89 us
    all_to_all x3 -> x2, starting transfers between devices: 20.5 us -> 16.4 us  [exchange(): return lax.all_to_all(x, AXES, 0, 0, tiled=True)]
    pallas_call x10 -> x9, Pallas kernels: 17.9 us -> 16.8 us  [call(): pl.pallas_call(kernel, out_shape=outs, in_specs=[pl.BlockSpec(memory_spac...]
  transfers between devices with their start and end apart: 3 -> 2, of which waited for: 3 -> 2; matrix products, arithmetic and copies ran while one was open for 0% -> 0% of each run, Pallas kernels for 5% -> 5%
where the time goes in v3:
time: 135 us; the launch traced here: 134 us
  blocking collectives  75.5 us (56%)
  Pallas kernels  16.8 us (12%)
  starting transfers between devices  16.4 us (12%)
  waiting for transfers between devices  15.5 us (11%)
  local copies, waits for them, and re-layouts  8.89 us (7%)
    all_to_all x4, blocking collectives, exchange(): return lax.all_to_all(x, AXES, 0, 0, tiled=True)  75.5 us
    pallas_call x9, Pallas kernels, call(): pl.pallas_call(kernel, out_shape=outs, in_specs=[pl.BlockSpec(memory_spac...  16.8 us
    all_to_all x2, starting transfers between devices, exchange(): return lax.all_to_all(x, AXES, 0, 0, tiled=True)  16.4 us
    all_to_all x2, waiting for transfers between devices, exchange(): return lax.all_to_all(x, AXES, 0, 0, tiled=True)  15.5 us
    unnamed x40, local copies, waits for them, and re-layouts  8.89 us
  transfers between devices with their start and end apart: 2, of which 2 were waited for; matrix products, arithmetic and copies ran while one was open for 0% of the time, Pallas kernels for 5%

profile of v3, /device:TPU:1, one launch (start us, length us, event | category | flops | bytes accessed | tf_op | source)
XLA Modules:
  0.0 134.1 jit_solution(17489353377085458236)
XLA Ops:
  0.7 3.5 %shard_map.147 = (bf16[128,4096]{1,0:T(8,128)(2,1)S(1)}, bf16[128,2048]{1,0:T(8,128)(2,1)S(1)}, f32[8,2048]{1,0:T(8,128)S(1)}) custom-call(s32[512]{0:T(512)} %mask_h.1, s32[512]{0:T(512)} %chain_h.1, bf16[64,32,128]{2,1,0:T(8,128)(2,1)} %pair.1, f32[1,128]{1,0:T(1,128)} %bitcast.26, f32[1,128]{1,0:T(1,128)} %bitcast.32, bf16[128,512]{1,0:T(8,128)(2,1)} %w_proj.3), custom_call_target="tpu_custom_call" | custom-call | flops 268435456 | bytes 2298880 | tf_op jit(solution)/shard_map/pallas_call | solution.py:307
  4.2 0.0 copy-start.5
  4.2 0.0 copy-start.14
  4.2 1.2 copy.16
  5.5 11.5 %all-to-all-start = ((bf16[128,32,128]{2,1,0:T(8,128)(2,1)}), bf16[128,32,128]{2,1,0:T(8,128)(2,1)S(1)}, u32[]{:S(2)}, u32[]{:S(2)}) async-start(bf16[128,32,128]{2,1,0:T(8,128)(2,1)} %bitcast.7), calls=%async_computation | async-start | bytes 2097152 | tf_op jit(solution)/shard_map/all_to_all | solution.py:319
  17.0 0.0 copy-start.6
  17.0 1.0 copy-done.6
  18.1 1.0 copy-done.16
  19.1 2.7 %shard_map.148 = (bf16[128,2048]{1,0:T(8,128)(2,1)S(1)}, f32[128,2048]{1,0:T(8,128)S(1)}, f32[128,2048]{1,0:T(8,128)S(1)}, f32[512,2048]{1,0:T(8,128)S(1)}) custom-call(bf16[64,32,128]{2,1,0:T(8,128)(2,1)S(1)} %copy-done.16, bf16[128,2048]{1,0:T(8,128)(2,1)S(1)} %copy-done.6, f32[8,2048]{1,0:T(8,128)S(1)} %get-tuple-element.32.aux, ...), custom_call_target="tpu_custom_call" | custom-call | flops 402653184 | bytes 8127488 | tf_op jit(solution)/shard_map/pallas_call | solution.py:307
  21.8 1.9 %copy-done = f32[512,2048]{1,0:T(8,128)} copy-done((f32[512,2048]{1,0:T(8,128)}, f32[512,2048]{1,0:T(8,128)S(1)}, u32[]{:S(2)}) %copy-start) | copy-done | bytes 4194328
  23.7 0.8 copy-done.8
  24.5 10.7 %all-to-all-done.recv = bf16[128,32,128]{2,1,0:T(8,128)(2,1)S(1)} async-done(((bf16[128,32,128]{2,1,0:T(8,128)(2,1)}), bf16[128,32,128]{2,1,0:T(8,128)(2,1)S(1)}, u32[]{:S(2)}, u32[]{:S(2)}) %all-to-all-start) | async-done | bytes 1048608 | tf_op jit(solution)/shard_map/all_to_all | solution.py:319
  35.2 1.0 shard_map.149
  36.2 18.4 %all_to_all.30 = bf16[128,16,128]{2,1,0:T(8,128)(2,1)S(1)} all-to-all(bf16[128,16,128]{2,1,0:T(8,128)(2,1)S(1)} %get-tuple-element.38), channel_id=1, replica_groups=mesh['row'=8,'col'=16] {'col','row'}, dimensions={0} | all-to-all | bytes 1048576 | tf_op jit(solution)/shard_map/all_to_all | solution.py:319
  54.6 0.1 copy.23
  54.8 0.9 shard_map.150
  55.7 0.1 copy.18
  55.8 0.0 copy-start.7
  55.9 18.0 %all_to_all.31.recv = bf16[128,16,128]{2,1,0:T(8,128)(2,1)S(1)} all-to-all(bf16[128,16,128]{2,1,0:T(8,128)(2,1)S(1)} %bitcast.31), channel_id=1, replica_groups=mesh['row'=8,'col'=16] {'col','row'}, dimensions={0} | all-to-all | bytes 1048576 | tf_op jit(solution)/shard_map/all_to_all | solution.py:319
  73.9 1.0 shard_map.151
  74.9 23.2 %all_to_all.32 = bf16[128,32,128]{2,1,0:T(8,128)(2,1)S(1)} all-to-all(bf16[128,32,128]{2,1,0:T(8,128)(2,1)S(1)} %shard_map.151), channel_id=1, replica_groups=mesh['row'=8,'col'=16] {'col','row'}, dimensions={0} | all-to-all | bytes 2097152 | tf_op jit(solution)/shard_map/all_to_all | solution.py:319
  98.1 0.5 copy.22
  98.6 0.0 copy-start.15
  98.6 2.4 %shard_map.152 = (bf16[1024,128]{1,0:T(8,128)(2,1)S(1)}, bf16[512,2048]{1,0:T(8,128)(2,1)S(1)}, bf16[128,2048]{1,0:T(8,128)(2,1)S(1)}) custom-call(bf16[128,4096]{1,0:T(8,128)(2,1)S(1)} %bitcast.18, bf16[128,2048]{1,0:T(8,128)(2,1)S(1)} %copy-done.7, f32[512,2048]{1,0:T(8,128)S(1)} %copy-done.1, bf16[128,2048]{1,0:T(8,128)(2,1)S(1)} %get-tuple-element.44.y, ...), custom_call_target="tpu_custom_call" | custom-call | flops 469762048 | bytes 10780672 | tf_op jit(solution)/shard_map/pallas_call | solution.py:307
  101.1 15.9 %all_to_all.33.parts = bf16[128,8,128]{2,1,0:T(8,128)(2,1)S(1)} all-to-all(bf16[128,8,128]{2,1,0:T(8,128)(2,1)S(1)} %bitcast.22), channel_id=1, replica_groups=mesh['row'=8,'col'=16] {'col','row'}, dimensions={0} | all-to-all | bytes 524288 | tf_op jit(solution)/shard_map/all_to_all | solution.py:319
  117.0 0.9 shard_map.153
  117.8 4.9 %all-to-all-start.5 = ((bf16[128,8,128]{2,1,0:T(8,128)(2,1)}), bf16[128,8,128]{2,1,0:T(8,128)(2,1)S(1)}, u32[]{:S(2)}, u32[]{:S(2)}) async-start(bf16[128,8,128]{2,1,0:T(8,128)(2,1)} %shard_map.153), calls=%async_computation.5 | async-start | bytes 524288 | tf_op jit(solution)/shard_map/all_to_all | solution.py:319
  122.7 1.0 copy-done.2
  123.8 1.0 copy-done.4
  124.8 3.6 %shard_map.154 = bf16[64,32,128]{2,1,0:T(8,128)(2,1)} custom-call(bf16[512,2048]{1,0:T(8,128)(2,1)S(1)} %get-tuple-element.50.grad_p, bf16[128,2048]{1,0:T(8,128)(2,1)S(1)} %copy-done.4, bf16[64,32,128]{2,1,0:T(8,128)(2,1)S(1)} %copy-done.2, f32[1,128]{1,0:T(1,128)S(1)} %bitcast.27, bf16[128,512]{1,0:T(8,128)(2,1)S(1)} %copy-done.10, ...), custom_call_target="tpu_custom_call" | custom-call | flops 335544320 | bytes 3834368 | tf_op jit(solution)/shard_map/pallas_call | solution.py:307
  128.4 4.9 %all-to-all-done.5.sums = bf16[128,8,128]{2,1,0:T(8,128)(2,1)S(1)} async-done(((bf16[128,8,128]{2,1,0:T(8,128)(2,1)}), bf16[128,8,128]{2,1,0:T(8,128)(2,1)S(1)}, u32[]{:S(2)}, u32[]{:S(2)}) %all-to-all-start.5) | async-done | bytes 262176 | tf_op jit(solution)/shard_map/all_to_all | solution.py:319
  133.3 0.8 shard_map.155
  (25 shorter events, 0.1 us)
Async XLA Ops:
  0.6 16.3 %copy-start.10 = (bf16[128,512]{1,0:T(8,128)(2,1)S(1)}, bf16[128,512]{1,0:T(8,128)(2,1)}, u32[]{:S(2)}) copy-start(bf16[128,512]{1,0:T(8,128)(2,1)} %w_proj.3) | copy-start | bytes 393220
  0.6 16.3 %copy-start.11 = (bf16[128,128]{1,0:T(8,128)(2,1)S(1)}, bf16[128,128]{1,0:T(8,128)(2,1)}, u32[]{:S(2)}) copy-start(bf16[128,128]{1,0:T(8,128)(2,1)} %w_out.3) | copy-start | bytes 98308
  0.7 16.3 %copy-start.12 = (bf16[128,128]{1,0:T(8,128)(2,1)S(1)}, bf16[128,128]{1,0:T(8,128)(2,1)}, u32[]{:S(2)}) copy-start(bf16[128,128]{1,0:T(8,128)(2,1)} %w_gate.3) | copy-start | bytes 98308
  0.7 16.3 %copy-start.13 = (f32[128]{0:T(128)S(1)}, f32[128]{0:T(128)}, u32[]{:S(2)}) copy-start(f32[128]{0:T(128)} %param.21) | copy-start | bytes 1540
  0.7 16.3 %copy-start.17 = (f32[128]{0:T(128)S(1)}, f32[128]{0:T(128)}, u32[]{:S(2)}) copy-start(f32[128]{0:T(128)} %param.20) | copy-start | bytes 1540
  4.2 1.3 copy-start.5
  4.2 50.6 %copy-start.14 = (f32[128]{0:T(128)S(1)}, f32[128]{0:T(128)}, u32[]{:S(2)}) copy-start(f32[128]{0:T(128)} %param.22) | copy-start | bytes 1540
  5.5 29.7 %all-to-all-start = ((bf16[128,32,128]{2,1,0:T(8,128)(2,1)}), bf16[128,32,128]{2,1,0:T(8,128)(2,1)S(1)}, u32[]{:S(2)}, u32[]{:S(2)}) async-start(bf16[128,32,128]{2,1,0:T(8,128)(2,1)} %bitcast.7), calls=%async_computation | async-start | bytes 2097152 | tf_op jit(solution)/shard_map/all_to_all | solution.py:319
  17.0 1.0 copy-start.6
  18.1 1.0 copy-start.16
  21.8 2.0 %copy-start = (f32[512,2048]{1,0:T(8,128)}, f32[512,2048]{1,0:T(8,128)S(1)}, u32[]{:S(2)}) copy-start(f32[512,2048]{1,0:T(8,128)S(1)} %get-tuple-element.43.factor) | copy-start | bytes 12582916
  23.7 0.8 copy-start.8
  55.8 42.7 %copy-start.1 = (f32[512,2048]{1,0:T(8,128)S(1)}, f32[512,2048]{1,0:T(8,128)}, u32[]{:S(2)}) copy-start(f32[512,2048]{1,0:T(8,128)} %copy-done) | copy-start | bytes 12582916
  55.8 42.7 %copy-start.7 = (bf16[128,2048]{1,0:T(8,128)(2,1)S(1)}, bf16[128,2048]{1,0:T(8,128)(2,1)}, u32[]{:S(2)}) copy-start(bf16[128,2048]{1,0:T(8,128)(2,1)} %copy-done.5) | copy-start | bytes 1572868
  55.9 42.7 %copy-start.9 = (bf16[128,2048]{1,0:T(8,128)(2,1)S(1)}, bf16[128,2048]{1,0:T(8,128)(2,1)}, u32[]{:S(2)}) copy-start(bf16[128,2048]{1,0:T(8,128)(2,1)} %copy-done.8) | copy-start | bytes 1572868
  98.6 24.1 %copy-start.15 = (f32[128]{0:T(128)S(1)}, f32[128]{0:T(128)}, u32[]{:S(2)}) copy-start(f32[128]{0:T(128)} %param.16) | copy-start | bytes 1540
  101.0 16.8 %copy-start.3 = (bf16[128,2048]{1,0:T(8,128)(2,1)}, bf16[128,2048]{1,0:T(8,128)(2,1)S(1)}, u32[]{:S(2)}) copy-start(bf16[128,2048]{1,0:T(8,128)(2,1)S(1)} %get-tuple-element.51.logit_t) | copy-start | bytes 1572868
  117.8 15.5 %all-to-all-start.5 = ((bf16[128,8,128]{2,1,0:T(8,128)(2,1)}), bf16[128,8,128]{2,1,0:T(8,128)(2,1)S(1)}, u32[]{:S(2)}, u32[]{:S(2)}) async-start(bf16[128,8,128]{2,1,0:T(8,128)(2,1)} %shard_map.153), calls=%async_computation.5 | async-start | bytes 524288 | tf_op jit(solution)/shard_map/all_to_all | solution.py:319
  122.7 1.0 copy-start.2
  123.8 1.0 copy-start.4

commit v4 on v3

--- a/solution.py
+++ b/solution.py
@@ -25,7 +25,7 @@
 WIDE = 256
 STEPS = PAIRS // WIDE
 EACH = WIDE // ROWS
-PIECES = 4
+PIECES = 2
 TILES = N // LANES
 
 
@@ -35,16 +35,12 @@
     )
 
 
-def sigmoid(x):
-    return 0.5 * jnp.tanh(0.5 * x) + 0.5
-
-
 def column(row):
     return jnp.broadcast_to(row, (WIDE, row.shape[1])).T
 
 
 def lanes_of(s, offset=0):
-    return pl.ds(pl.multiple_of(s * WIDE + offset, LANES), WIDE)
+    return slice(offset + s * WIDE, offset + (s + 1) * WIDE)
 
 
 def swap_halves(first, second):
@@ -57,51 +53,60 @@
 
 def load_chunk(ref, s):
     parts = [ref[pl.ds(EACH * s + e, ROWS, stride=COLS), :] for e in range(EACH)]
-    return jnp.concatenate(parts, axis=0).T
+    return jnp.concatenate(parts, axis=0).astype(BF16).T.astype(F32)
 
 
 def store_chunk(ref, s, value):
-    value = value.T
+    value = value.astype(BF16).T.astype(F32)
     for e in range(EACH):
         ref[pl.ds(EACH * s + e, ROWS, stride=COLS), :] = value[e * ROWS : (e + 1) * ROWS]
 
 
-def loop(step, unroll=2):
-    def body(group, carry):
-        for u in range(unroll):
-            step(group * unroll + u)
-        return carry
-
-    lax.fori_loop(0, STEPS // unroll, body, 0)
+def loop(step):
+    for s in range(STEPS):
+        step(s)
 
 
 def front_kernel(
-    mask_h, chain_h, pair_h, gain_h, bias_h, w_h,
-    send, zn_t, aux,
-    mask_s, chain_s, pair, gain, bias, w_proj, xs, w_t, sems,
+    mask_h, chain_h, gain_h, bias_h, chain_bias_h, out_gain_h, w_proj_h, w_gate_h, w_out_h,
+    pair_h, cot_h,
+    send, zn_t, grad_update, q_out, slope, factor,
+    mask_s, chain_s, gain, bias, chain_bias, out_gain, w_proj, w_gate, w_out, pair, cot,
+    xs, cs, wp_t, wg_t, sems,
 ):
     small = [
         pltpu.make_async_copy(src, dst, sems.at[n])
         for n, (src, dst) in enumerate(
             (
-                (w_h, w_proj), (gain_h, gain), (bias_h, bias), (mask_h, mask_s),
-                (chain_h, chain_s),
+                (mask_h, mask_s), (chain_h, chain_s), (gain_h, gain), (bias_h, bias),
+                (chain_bias_h, chain_bias), (out_gain_h, out_gain), (w_proj_h, w_proj),
+                (w_gate_h, w_gate), (w_out_h, w_out),
             )
         )
     ]
     pieces = []
     for n in range(PIECES):
         spot = slice(n * COLS // PIECES, (n + 1) * COLS // PIECES)
-        pieces.append(pltpu.make_async_copy(pair_h.at[:, spot], pair.at[:, spot], sems.at[5 + n]))
+        for m, (src, dst) in enumerate(((pair_h, pair), (cot_h, cot))):
+            pieces.append(
+                pltpu.make_async_copy(src.at[:, spot], dst.at[:, spot], sems.at[9 + 2 * n + m])
+            )
     for copy in small + pieces:
         copy.start()
     for copy in small:
         copy.wait()
+    columns = jnp.concatenate(
+        [gain[...], bias[...], 0.5 * chain_bias[...], out_gain[...], jnp.zeros((4, CH), F32)], axis=0
+    ).T
+    gain_c, bias_c, chain_c, out_gain_c = (
+        jnp.broadcast_to(columns[:, n : n + 1], (CH, WIDE)) for n in range(4)
+    )
     row_start = lax.axis_index("row") * ROWS
     col_start = lax.axis_index("col") * COLS
-    w_t[...] = w_proj[...].astype(F32).T.astype(BF16)
-    gain_c = column(gain[...])
-    bias_c = column(bias[...])
+    for n in range(4):
+        weights = w_proj[:, n * CH : (n + 1) * CH].astype(F32).T
+        wp_t[n * CH : (n + 1) * CH] = (weights if n % 2 else 0.5 * weights).astype(BF16)
+    wg_t[...] = (0.5 * w_gate[...].astype(F32).T).astype(BF16)
     lane = lax.broadcasted_iota(jnp.int32, (1, LANES), 1)
     place = lane % ROWS
     mask_row = jnp.zeros((1, LANES), jnp.int32)
@@ -113,66 +118,43 @@
     low = lane < ROWS
 
     def step(s):
+        here = lanes_of(s)
         x = load_chunk(xs.reshape(PAIRS, CH), s)
         mean = jnp.mean(x, axis=0, keepdims=True)
         centred = x - mean
         inverse = lax.rsqrt(jnp.mean(centred * centred, axis=0, keepdims=True) + EPS)
-        normed = centred * inverse
-        zn = (normed * gain_c + bias_c).astype(BF16)
+        zn = (centred * inverse * gain_c + bias_c).astype(BF16)
+        zn_t[:, here] = zn
         mask, same = [], []
         for e in range(0, EACH, 2):
             k = col_start + EACH * s + e
             mask.append((jnp.where(low, mask_s[k], mask_s[k + 1]) * mask_row).astype(F32))
             same.append((jnp.where(low, chain_s[k], chain_s[k + 1]) == chain_row).astype(F32))
-        mask = jnp.concatenate(mask, axis=1)
-        proj = dot(w_t[...], zn, 1, 0)
-        act_a = sigmoid(proj[:CH]) * proj[CH : 2 * CH] * mask
-        act_b = sigmoid(proj[2 * CH : 3 * CH]) * proj[3 * CH :] * mask
-        send[:, lanes_of(s)] = act_a.astype(BF16)
-        send[:, lanes_of(s, PAIRS)] = act_b.astype(BF16)
-        zn_t[:, lanes_of(s)] = zn
-        aux[0:1, lanes_of(s)] = mask
-        aux[1:2, lanes_of(s)] = jnp.concatenate(same, axis=1)
+        half = 0.5 * jnp.concatenate(mask, axis=1)
+        same = jnp.concatenate(same, axis=1)
+        proj = dot(wp_t[...], zn, 1, 0)
+        for side in range(2):
+            base = 2 * CH * side
+            plain = jnp.tanh(proj[base : base + CH]) * half + half
+            act = plain * proj[base + CH : base + 2 * CH]
+            send[:, lanes_of(s, side * PAIRS)] = act.astype(BF16)
+            factor[base : base + CH, here] = (act - act * plain).astype(BF16)
+            factor[base + CH : base + 2 * CH, here] = plain.astype(BF16)
+        gate = 0.5 * jnp.tanh(dot(wg_t[...], zn, 1, 0) + same * chain_c) + 0.5
+        gated = load_chunk(cs.reshape(PAIRS, CH), s) * gate
+        update = gated.astype(BF16)
+        grad_update[:, here] = update
+        slope[:, here] = gated - gated * gate
+        q_out[:, here] = dot(w_out[...], update, 1, 0) * out_gain_c
 
     for n in range(PIECES):
-        pieces[n].wait()
+        pieces[2 * n].wait()
+        pieces[2 * n + 1].wait()
         spot = slice(n * COLS // PIECES, (n + 1) * COLS // PIECES)
         xs[:, spot] = pair[:, spot].astype(F32)
+        cs[:, spot] = cot[:, spot].astype(F32)
         for u in range(STEPS // PIECES):
             step(n * (STEPS // PIECES) + u)
-
-
-def ahead_kernel(
-    cot, zn_t, aux, w_gate, chain_bias, gain, w_out, w_proj,
-    grad_update, q_out, slope, factor, cs, wg_t, wp_t,
-):
-    cs[...] = cot[...].astype(F32).reshape(PAIRS, CH)
-    wg_t[...] = w_gate[...].astype(F32).T.astype(BF16)
-    wp_t[...] = w_proj[...].astype(F32).T.astype(BF16)
-    gain_c = column(gain[...])
-    chain_c = column(chain_bias[...])
-
-    def step(s):
-        here = lanes_of(s)
-        zn = zn_t[:, here]
-        gate = sigmoid(dot(wg_t[...], zn, 1, 0) + aux[1:2, here] * chain_c)
-        gated = load_chunk(cs, s) * gate
-        update = gated.astype(BF16)
-        grad_update[:, here] = update
-        slope[:, here] = gated * (1.0 - gate)
-        q_out[:, here] = dot(w_out[...], update, 1, 0) * gain_c
-        mask = aux[0:1, here]
-        proj = dot(wp_t[...], zn, 1, 0)
-        gate_a = sigmoid(proj[:CH])
-        gate_b = sigmoid(proj[2 * CH : 3 * CH])
-        plain_a = mask * gate_a
-        plain_b = mask * gate_b
-        factor[0:CH, here] = plain_a * proj[CH : 2 * CH] * (1.0 - gate_a)
-        factor[CH : 2 * CH, here] = plain_a
-        factor[2 * CH : 3 * CH, here] = plain_b * proj[3 * CH :] * (1.0 - gate_b)
-        factor[3 * CH : 4 * CH, here] = plain_b
-
-    loop(step)
 
 
 def mix_kernel(recv, send, a_t, b_t, mixed):
@@ -252,15 +234,13 @@
         logit_t[:, here] = (slope[:, here] * update).astype(BF16)
         for part in range(4):
             rows = slice(part * CH, (part + 1) * CH)
-            grad = recv[:, lanes_of(s, (part // 2) * PAIRS)].astype(F32)
-            grad_p[rows, here] = (grad * factor[rows, here]).astype(BF16)
+            grad_p[rows, here] = recv[:, lanes_of(s, (part // 2) * PAIRS)] * factor[rows, here]
 
     loop(step)
-    product = dot(zn_t[...], grad_p[...], 1, 1)
-    for part in range(4):
-        terms[part * CH : (part + 1) * CH] = product[:, part * CH : (part + 1) * CH].astype(BF16)
-    terms[4 * CH : 5 * CH] = dot(y[...], grad_update[...], 1, 1).astype(BF16)
-    terms[5 * CH : 6 * CH] = dot(zn_t[...], logit_t[...], 1, 1).astype(BF16)
+    zn = zn_t[...].T
+    terms[: 4 * CH] = dot(grad_p[...], zn, 1, 0).astype(BF16)
+    terms[4 * CH : 5 * CH] = dot(logit_t[...], zn, 1, 0).astype(BF16)
+    terms[5 * CH : 6 * CH] = dot(y[...], grad_update[...], 1, 1).astype(BF16)
     terms[6 * CH :] = jnp.zeros((2 * CH, CH), BF16)
 
 
@@ -285,16 +265,19 @@
 
 
 def sum_kernel(parts, out):
-    total = jnp.sum(parts[...].astype(F32), axis=0, keepdims=True) * (1.0 / N)
-    out[...] = jnp.broadcast_to(total, out.shape).astype(BF16)
+    total = parts[...].astype(F32)
+    while total.shape[0] > 1:
+        half = total.shape[0] // 2
+        total = total[:half] + total[half:]
+    out[...] = jnp.broadcast_to(total * (1.0 / N), out.shape).astype(BF16)
 
 
 def split_kernel(sums, grad_proj, grad_gate, grad_out):
     whole = sums[...].astype(F32).reshape(8 * DEV, LANES)
     for part in range(4):
-        grad_proj[:, part * CH : (part + 1) * CH] = whole[part * CH : (part + 1) * CH]
-    grad_out[...] = whole[4 * CH : 5 * CH]
-    grad_gate[...] = whole[5 * CH : 6 * CH]
+        grad_proj[:, part * CH : (part + 1) * CH] = whole[part * CH : (part + 1) * CH].T
+    grad_gate[...] = whole[4 * CH : 5 * CH].T
+    grad_out[...] = whole[5 * CH : 6 * CH]
 
 
 def call(kernel, outs, scratch, flops, args, in_hbm=False, vmem=16):
@@ -348,33 +331,29 @@
     def flat(x):
         return x.reshape(1, -1)
 
-    send_ab, zn_t, aux = call(
+    send_ab, zn_t, grad_update, q, slope, factor = call(
         front_kernel,
-        [S((CH, 2 * PAIRS), BF16), S((CH, PAIRS), BF16), S((8, PAIRS), F32)],
         [
-            pltpu.SMEM((N,), jnp.int32), pltpu.SMEM((N,), jnp.int32), V((ROWS, COLS, CH), BF16),
-            V((1, CH), F32), V((1, CH), F32), V((CH, 4 * CH), BF16),
-            V((ROWS, COLS, CH), F32), V((4 * CH, CH), BF16),
-            pltpu.SemaphoreType.DMA((5 + PIECES,)),
+            S((CH, 2 * PAIRS), BF16), S((CH, PAIRS), BF16), S((CH, PAIRS), BF16),
+            S((CH, PAIRS), F32), S((CH, PAIRS), F32), S((4 * CH, PAIRS), BF16),
         ],
-        4 * unit,
-        (res_mask, chain, pair, flat(ln_in_gain), flat(ln_in_bias), w_proj),
+        [
+            pltpu.SMEM((N,), jnp.int32), pltpu.SMEM((N,), jnp.int32),
+            V((1, CH), F32), V((1, CH), F32), V((1, CH), F32), V((1, CH), F32),
+            V((CH, 4 * CH), BF16), V((CH, CH), BF16), V((CH, CH), BF16),
+            V((ROWS, COLS, CH), BF16), V((ROWS, COLS, CH), BF16),
+            V((ROWS, COLS, CH), F32), V((ROWS, COLS, CH), F32),
+            V((4 * CH, CH), BF16), V((CH, CH), BF16),
+            pltpu.SemaphoreType.DMA((9 + 2 * PIECES,)),
+        ],
+        6 * unit,
+        (
+            res_mask, chain, flat(ln_in_gain), flat(ln_in_bias), flat(chain_bias),
+            flat(ln_out_gain), w_proj, w_gate, w_out, pair, cotangent,
+        ),
         in_hbm=True,
     )
     recv_ab = exchange(split_rows(send_ab))
-    grad_update, q, slope, factor = call(
-        ahead_kernel,
-        [
-            S((CH, PAIRS), BF16), S((CH, PAIRS), F32), S((CH, PAIRS), F32),
-            S((4 * CH, PAIRS), F32),
-        ],
-        [V((PAIRS, CH), F32), V((CH, CH), BF16), V((4 * CH, CH), BF16)],
-        6 * unit,
-        (cotangent, zn_t, aux, w_gate, flat(chain_bias), flat(ln_out_gain), w_out, w_proj),
-    )
-    recv_ab, grad_update, q, slope, factor = lax.optimization_barrier(
-        (recv_ab, grad_update, q, slope, factor)
-    )
     send_mixed, a_t, b_t = call(
         mix_kernel,
         [S((DEV, CHUNKS, LANES), BF16), S((N, N), BF16), S((N, N), BF16)],

time: 135 us -> 133 us (0.985)
  blocking collectives: 75.5 us -> 105 us
  starting transfers between devices: 16.4 us -> 4.88 us
  waiting for transfers between devices: 15.5 us -> 6.71 us
  local copies, waits for them, and re-layouts: 8.89 us -> 1.73 us
  Pallas kernels: 16.8 us -> 12.9 us
    all_to_all x4 -> x5, blocking collectives: 75.5 us -> 105 us  [exchange(): return lax.all_to_all(x, AXES, 0, 0, tiled=True)]
    all_to_all x2 -> x1, starting transfers between devices: 16.4 us -> 4.88 us  [exchange(): return lax.all_to_all(x, AXES, 0, 0, tiled=True)]
    all_to_all x2 -> x1, waiting for transfers between devices: 15.5 us -> 6.71 us  [exchange(): return lax.all_to_all(x, AXES, 0, 0, tiled=True)]
    unnamed x40 -> x18, local copies, waits for them, and re-layouts: 8.89 us -> 1.73 us
    pallas_call x9 -> x8, Pallas kernels: 16.8 us -> 12.9 us  [call(): pl.pallas_call(kernel, out_shape=outs, in_specs=[pl.BlockSpec(memory_spac...]
  transfers between devices with their start and end apart: 2 -> 1, of which waited for: 2 -> 1; matrix products, arithmetic and copies ran while one was open for 0% -> 0% of each run, Pallas kernels for 5% -> 2%
where the time goes in v4:
time: 133 us; the launch traced here: 132 us
  blocking collectives  105 us (79%)
  Pallas kernels  12.9 us (10%)
  waiting for transfers between devices  6.71 us (5%)
  starting transfers between devices  4.88 us (4%)
  local copies, waits for them, and re-layouts  1.73 us (1%)
    all_to_all x5, blocking collectives, exchange(): return lax.all_to_all(x, AXES, 0, 0, tiled=True)  105 us
    pallas_call x8, Pallas kernels, call(): pl.pallas_call(kernel, out_shape=outs, in_specs=[pl.BlockSpec(memory_spac...  12.9 us
    all_to_all x1, waiting for transfers between devices, exchange(): return lax.all_to_all(x, AXES, 0, 0, tiled=True)  6.71 us
    all_to_all x1, starting transfers between devices, exchange(): return lax.all_to_all(x, AXES, 0, 0, tiled=True)  4.88 us
  transfers between devices with their start and end apart: 1, of which 1 were waited for; matrix products, arithmetic and copies ran while one was open for 0% of the time, Pallas kernels for 2%

profile of v4, /device:TPU:1, one launch (start us, length us, event | category | flops | bytes accessed | tf_op | source)
XLA Modules:
  0.0 132.1 jit_solution(9660379778043274804)
XLA Ops:
  0.6 4.2 %shard_map.147 = (bf16[128,4096]{1,0:T(8,128)(2,1)S(1)}, bf16[128,2048]{1,0:T(8,128)(2,1)S(1)}, bf16[128,2048]{1,0:T(8,128)(2,1)S(1)}, f32[128,2048]{1,0:T(8,128...) custom-call(s32[512]{0:T(512)} %mask_h.1, s32[512]{0:T(512)} %chain_h.1, f32[1,128]{1,0:T(1,128)} %bitcast.26, ...), custom_call_target="tpu_custom_call" | custom-call | flops 402653184 | bytes 7542784 | tf_op jit(solution)/shard_map/pallas_call | solution.py:290
  4.8 0.2 copy.16
  5.1 29.5 %all_to_all.30.recv = bf16[128,32,128]{2,1,0:T(8,128)(2,1)S(1)} all-to-all(bf16[128,32,128]{2,1,0:T(8,128)(2,1)S(1)} %bitcast.28), channel_id=1, replica_groups=mesh['row'=8,'col'=16] {'col','row'}, dimensions={0} | all-to-all | bytes 2097152 | tf_op jit(solution)/shard_map/all_to_all | solution.py:302
  34.6 0.0 copy-start.4
  34.6 1.0 shard_map.148
  35.7 18.4 %all_to_all.31 = bf16[128,16,128]{2,1,0:T(8,128)(2,1)S(1)} all-to-all(bf16[128,16,128]{2,1,0:T(8,128)(2,1)S(1)} %get-tuple-element.25), channel_id=1, replica_groups=mesh['row'=8,'col'=16] {'col','row'}, dimensions={0} | all-to-all | bytes 1048576 | tf_op jit(solution)/shard_map/all_to_all | solution.py:302
  54.0 0.1 copy.23
  54.2 0.0 copy-done.4
  54.2 0.0 copy-done.5
  54.2 0.8 shard_map.149
  55.0 0.1 copy.18
  55.1 18.0 %all_to_all.32.recv = bf16[128,16,128]{2,1,0:T(8,128)(2,1)S(1)} all-to-all(bf16[128,16,128]{2,1,0:T(8,128)(2,1)S(1)} %bitcast.31), channel_id=1, replica_groups=mesh['row'=8,'col'=16] {'col','row'}, dimensions={0} | all-to-all | bytes 1048576 | tf_op jit(solution)/shard_map/all_to_all | solution.py:302
  73.2 1.0 shard_map.150
  74.2 0.0 copy-start.2
  74.2 23.2 %all_to_all.33 = bf16[128,32,128]{2,1,0:T(8,128)(2,1)S(1)} all-to-all(bf16[128,32,128]{2,1,0:T(8,128)(2,1)S(1)} %shard_map.150), channel_id=1, replica_groups=mesh['row'=8,'col'=16] {'col','row'}, dimensions={0} | all-to-all | bytes 2097152 | tf_op jit(solution)/shard_map/all_to_all | solution.py:302
  97.4 0.5 copy.22
  97.8 0.0 copy-done.2
  97.8 0.0 copy-start
  97.9 0.0 copy-start.1
  97.9 0.0 copy-start.6
  97.9 1.2 shard_map.151
  99.1 15.9 %all_to_all.34.parts = bf16[128,8,128]{2,1,0:T(8,128)(2,1)S(1)} all-to-all(bf16[128,8,128]{2,1,0:T(8,128)(2,1)S(1)} %bitcast.22), channel_id=1, replica_groups=mesh['row'=8,'col'=16] {'col','row'}, dimensions={0} | all-to-all | bytes 524288 | tf_op jit(solution)/shard_map/all_to_all | solution.py:302
  115.0 0.8 shard_map.152
  115.8 4.9 %all-to-all-start.5 = ((bf16[128,8,128]{2,1,0:T(8,128)(2,1)}), bf16[128,8,128]{2,1,0:T(8,128)(2,1)S(1)}, u32[]{:S(2)}, u32[]{:S(2)}) async-start(bf16[128,8,128]{2,1,0:T(8,128)(2,1)} %shard_map.152), calls=%async_computation.5 | async-start | bytes 524288 | tf_op jit(solution)/shard_map/all_to_all | solution.py:302
  120.6 0.0 copy-done
  120.7 0.0 copy-done.1
  120.7 0.0 copy-done.6
  120.7 0.0 copy-start.3
  120.7 0.7 copy-done.3
  121.4 3.1 %shard_map.153 = bf16[64,32,128]{2,1,0:T(8,128)(2,1)} custom-call(bf16[512,2048]{1,0:T(8,128)(2,1)S(1)} %get-tuple-element.38.grad_p, bf16[128,2048]{1,0:T(8,128)(2,1)S(1)} %get-tuple-element.39.logit_t, bf16[64,32,128]{2,1,0:T(8,128)(2,1)S(1)} %copy-done, f32[1,128]{1,0:T(1,128)S(1)} %bitcast.27, bf16[128,512]{1,0:T(8,128)(2,1)S(1)} %copy-done.1, ...), custom_call_target="tpu_custom_call" | custom-call | flops 335544320 | bytes 3834368 | tf_op jit(solution)/shard_map/pallas_call | solution.py:290
  124.6 6.7 %all-to-all-done.5.sums = bf16[128,8,128]{2,1,0:T(8,128)(2,1)S(1)} async-done(((bf16[128,8,128]{2,1,0:T(8,128)(2,1)}), bf16[128,8,128]{2,1,0:T(8,128)(2,1)S(1)}, u32[]{:S(2)}, u32[]{:S(2)}) %all-to-all-start.5) | async-done | bytes 262176 | tf_op jit(solution)/shard_map/all_to_all | solution.py:302
  131.3 0.9 shard_map.154
  (1 shorter events, 0.0 us)
Async XLA Ops:
  34.6 19.6 %copy-start.4 = (f32[128]{0:T(128)S(1)}, f32[128]{0:T(128)}, u32[]{:S(2)}) copy-start(f32[128]{0:T(128)} %param.21) | copy-start | bytes 1540
  34.6 19.6 %copy-start.5 = (f32[128]{0:T(128)S(1)}, f32[128]{0:T(128)}, u32[]{:S(2)}) copy-start(f32[128]{0:T(128)} %param.22) | copy-start | bytes 1540
  74.2 23.7 %copy-start.2 = (bf16[128,128]{1,0:T(8,128)(2,1)S(1)}, bf16[128,128]{1,0:T(8,128)(2,1)}, u32[]{:S(2)}) copy-start(bf16[128,128]{1,0:T(8,128)(2,1)} %w_out.1) | copy-start | bytes 98308
  97.8 22.8 %copy-start = (bf16[64,32,128]{2,1,0:T(8,128)(2,1)S(1)}, bf16[64,32,128]{2,1,0:T(8,128)(2,1)}, u32[]{:S(2)}) copy-start(bf16[64,32,128]{2,1,0:T(8,128)(2,1)} %pair.1) | copy-start | bytes 1572868
  97.9 22.8 %copy-start.1 = (bf16[128,512]{1,0:T(8,128)(2,1)S(1)}, bf16[128,512]{1,0:T(8,128)(2,1)}, u32[]{:S(2)}) copy-start(bf16[128,512]{1,0:T(8,128)(2,1)} %w_proj.1) | copy-start | bytes 393220
  97.9 22.8 %copy-start.6 = (f32[128]{0:T(128)S(1)}, f32[128]{0:T(128)}, u32[]{:S(2)}) copy-start(f32[128]{0:T(128)} %param.16) | copy-start | bytes 1540
  115.8 15.5 %all-to-all-start.5 = ((bf16[128,8,128]{2,1,0:T(8,128)(2,1)}), bf16[128,8,128]{2,1,0:T(8,128)(2,1)S(1)}, u32[]{:S(2)}, u32[]{:S(2)}) async-start(bf16[128,8,128]{2,1,0:T(8,128)(2,1)} %shard_map.152), calls=%async_computation.5 | async-start | bytes 524288 | tf_op jit(solution)/shard_map/all_to_all | solution.py:302
  120.7 0.8 copy-start.3

commit v5 on v4

--- a/solution.py
+++ b/solution.py
@@ -27,6 +27,7 @@
 EACH = WIDE // ROWS
 PIECES = 2
 TILES = N // LANES
+SHARE = 6 * CH // DEV
 
 
 def dot(left, right, dim_left, dim_right):
@@ -240,8 +241,7 @@
     zn = zn_t[...].T
     terms[: 4 * CH] = dot(grad_p[...], zn, 1, 0).astype(BF16)
     terms[4 * CH : 5 * CH] = dot(logit_t[...], zn, 1, 0).astype(BF16)
-    terms[5 * CH : 6 * CH] = dot(y[...], grad_update[...], 1, 1).astype(BF16)
-    terms[6 * CH :] = jnp.zeros((2 * CH, CH), BF16)
+    terms[5 * CH :] = dot(y[...], grad_update[...], 1, 1).astype(BF16)
 
 
 def last_kernel(grad_p, logit_t, pair, gain, w_proj, w_gate, grad_pair, xs):
@@ -265,19 +265,25 @@
 
 
 def sum_kernel(parts, out):
-    total = parts[...].astype(F32)
+    total = parts[...].astype(F32).reshape(DEV // 4, 4 * SHARE, LANES)
     while total.shape[0] > 1:
         half = total.shape[0] // 2
         total = total[:half] + total[half:]
-    out[...] = jnp.broadcast_to(total * (1.0 / N), out.shape).astype(BF16)
+    total = total[0]
+    mine = total[:SHARE]
+    for n in range(1, 4):
+        mine = mine + total[n * SHARE : (n + 1) * SHARE]
+    mine = jnp.concatenate([mine * (1.0 / N)] * 8, axis=0).astype(BF16)
+    for n in range(DEV // 8):
+        out[8 * SHARE * n : 8 * SHARE * (n + 1)] = mine
 
 
 def split_kernel(sums, grad_proj, grad_gate, grad_out):
-    whole = sums[...].astype(F32).reshape(8 * DEV, LANES)
+    whole = sums[...].astype(F32)
     for part in range(4):
         grad_proj[:, part * CH : (part + 1) * CH] = whole[part * CH : (part + 1) * CH].T
     grad_gate[...] = whole[4 * CH : 5 * CH].T
-    grad_out[...] = whole[5 * CH : 6 * CH]
+    grad_out[...] = whole[5 * CH :]
 
 
 def call(kernel, outs, scratch, flops, args, in_hbm=False, vmem=16):
@@ -300,6 +306,10 @@
 
 def exchange(x):
     return lax.all_to_all(x, AXES, 0, 0, tiled=True)
+
+
+def exchange_terms(x):
+    return exchange(x.reshape(DEV, SHARE // 2, 2, LANES)).reshape(x.shape)
 
 
 def split_rows(x):
@@ -377,15 +387,15 @@
     )
     terms, grad_p, logit_t = call(
         back_kernel,
-        [S((8 * DEV, CH), BF16), S((4 * CH, PAIRS), BF16), S((CH, PAIRS), BF16)],
+        [S((6 * CH, CH), BF16), S((4 * CH, PAIRS), BF16), S((CH, PAIRS), BF16)],
         [V((CH, CH), BF16)],
         7 * unit,
         (join_rows(exchange(send_back)), zn_t, factor, y, slope, grad_update, w_out),
     )
-    parts = exchange(split_rows(terms))
-    (summed,) = call(sum_kernel, [S((DEV, 8, LANES), BF16)], [], 0, (parts,))
+    parts = exchange_terms(terms)
+    (summed,) = call(sum_kernel, [S((6 * CH, CH), BF16)], [], 0, (parts,))
     summed, grad_p, logit_t = lax.optimization_barrier((summed, grad_p, logit_t))
-    sums = exchange(summed)
+    sums = exchange_terms(summed)
     (grad_pair,) = call(
         last_kernel,
         [S((ROWS, COLS, CH), BF16)],

time: 133 us -> 131 us (0.985)
  no operation moved by 1% of the time
where the time goes in v5:
time: 131 us
  blocking collectives  105 us (80%)
  Pallas kernels  12.9 us (10%)
  waiting for transfers between devices  7.06 us (5%)
  starting transfers between devices  4.59 us (4%)
    all_to_all x5, blocking collectives, exchange(): return lax.all_to_all(x, AXES, 0, 0, tiled=True)  105 us
    pallas_call x8, Pallas kernels, call(): pl.pallas_call(kernel, out_shape=outs, in_specs=[pl.BlockSpec(memory_spac...  12.9 us
    all_to_all x1, waiting for transfers between devices, exchange(): return lax.all_to_all(x, AXES, 0, 0, tiled=True)  7.06 us
    all_to_all x1, starting transfers between devices, exchange(): return lax.all_to_all(x, AXES, 0, 0, tiled=True)  4.59 us
  transfers between devices with their start and end apart: 1, of which 1 were waited for; matrix products, arithmetic and copies ran while one was open for 0% of the time, Pallas kernels for 2%

profile of v5, /device:TPU:1, one launch (start us, length us, event | category | flops | bytes accessed | tf_op | source)
XLA Modules:
  0.0 131.0 jit_solution(3209326870825562884)
XLA Ops:
  0.6 4.2 %shard_map.147 = (bf16[128,4096]{1,0:T(8,128)(2,1)S(1)}, bf16[128,2048]{1,0:T(8,128)(2,1)S(1)}, bf16[128,2048]{1,0:T(8,128)(2,1)S(1)}, f32[128,2048]{1,0:T(8,128...) custom-call(s32[512]{0:T(512)} %mask_h.1, s32[512]{0:T(512)} %chain_h.1, f32[1,128]{1,0:T(1,128)} %bitcast.31, ...), custom_call_target="tpu_custom_call" | custom-call | flops 402653184 | bytes 7542784 | tf_op jit(solution)/shard_map/pallas_call | solution.py:296
  4.8 0.2 copy.16
  5.1 29.5 %all_to_all.30.recv = bf16[128,32,128]{2,1,0:T(8,128)(2,1)S(1)} all-to-all(bf16[128,32,128]{2,1,0:T(8,128)(2,1)S(1)} %bitcast.33), channel_id=1, replica_groups=mesh['row'=8,'col'=16] {'col','row'}, dimensions={0} | all-to-all | bytes 2097152 | tf_op jit(solution)/shard_map/all_to_all | solution.py:308
  34.6 0.0 copy-start.4
  34.6 1.0 shard_map.148
  35.7 18.4 %all_to_all.31 = bf16[128,16,128]{2,1,0:T(8,128)(2,1)S(1)} all-to-all(bf16[128,16,128]{2,1,0:T(8,128)(2,1)S(1)} %get-tuple-element.25), channel_id=1, replica_groups=mesh['row'=8,'col'=16] {'col','row'}, dimensions={0} | all-to-all | bytes 1048576 | tf_op jit(solution)/shard_map/all_to_all | solution.py:308
  54.0 0.1 copy.23
  54.2 0.0 copy-done.4
  54.2 0.0 copy-done.5
  54.2 0.8 shard_map.149
  55.0 0.1 copy.18
  55.1 18.0 %all_to_all.32.recv = bf16[128,16,128]{2,1,0:T(8,128)(2,1)S(1)} all-to-all(bf16[128,16,128]{2,1,0:T(8,128)(2,1)S(1)} %bitcast.36), channel_id=1, replica_groups=mesh['row'=8,'col'=16] {'col','row'}, dimensions={0} | all-to-all | bytes 1048576 | tf_op jit(solution)/shard_map/all_to_all | solution.py:308
  73.2 1.0 shard_map.150
  74.2 0.0 copy-start.2
  74.2 23.2 %all_to_all.33 = bf16[128,32,128]{2,1,0:T(8,128)(2,1)S(1)} all-to-all(bf16[128,32,128]{2,1,0:T(8,128)(2,1)S(1)} %shard_map.150), channel_id=1, replica_groups=mesh['row'=8,'col'=16] {'col','row'}, dimensions={0} | all-to-all | bytes 2097152 | tf_op jit(solution)/shard_map/all_to_all | solution.py:308
  97.4 0.5 copy.22
  97.8 0.0 copy-done.2
  97.8 0.0 copy-start
  97.9 0.0 copy-start.1
  97.9 0.0 copy-start.3
  97.9 0.0 copy-start.6
  97.9 1.2 shard_map.151
  99.1 15.5 %all_to_all.34 = bf16[128,3,2,128]{3,2,1,0:T(2,128)(2,1)S(1)} all-to-all(bf16[128,3,2,128]{3,2,1,0:T(2,128)(2,1)S(1)} %bitcast.27), channel_id=1, replica_groups=mesh['row'=8,'col'=16] {'col','row'}, dimensions={0} | all-to-all | bytes 393216 | tf_op jit(solution)/shard_map/all_to_all | solution.py:308
  114.6 0.7 shard_map.152
  115.4 4.6 %all-to-all-start.5 = ((bf16[128,3,2,128]{3,2,1,0:T(2,128)(2,1)}), bf16[128,3,2,128]{3,2,1,0:T(2,128)(2,1)S(1)}, u32[]{:S(2)}, u32[]{:S(2)}) async-start(bf16[128,3,2,128]{3,2,1,0:T(2,128)(2,1)} %bitcast.7), calls=%async_computation.5 | async-start | bytes 393216 | tf_op jit(solution)/shard_map/all_to_all | solution.py:308
  120.0 0.0 copy-done
  120.0 0.0 copy-done.1
  120.0 0.0 copy-done.3
  120.0 0.0 copy-done.6
  120.0 3.1 %shard_map.153 = bf16[64,32,128]{2,1,0:T(8,128)(2,1)} custom-call(bf16[512,2048]{1,0:T(8,128)(2,1)S(1)} %get-tuple-element.38.grad_p, bf16[128,2048]{1,0:T(8,128)(2,1)S(1)} %get-tuple-element.39.logit_t, bf16[64,32,128]{2,1,0:T(8,128)(2,1)S(1)} %copy-done, f32[1,128]{1,0:T(1,128)S(1)} %bitcast.32, bf16[128,512]{1,0:T(8,128)(2,1)S(1)} %copy-done.1, ...), custom_call_target="tpu_custom_call" | custom-call | flops 335544320 | bytes 3834368 | tf_op jit(solution)/shard_map/pallas_call | solution.py:296
  123.1 7.1 %all-to-all-done.5 = bf16[128,3,2,128]{3,2,1,0:T(2,128)(2,1)S(1)} async-done(((bf16[128,3,2,128]{3,2,1,0:T(2,128)(2,1)}), bf16[128,3,2,128]{3,2,1,0:T(2,128)(2,1)S(1)}, u32[]{:S(2)}, u32[]{:S(2)}) %all-to-all-start.5) | async-done | bytes 196640 | tf_op jit(solution)/shard_map/all_to_all | solution.py:308
  130.2 0.9 shard_map.154
  (1 shorter events, 0.0 us)
Async XLA Ops:
  34.6 19.6 %copy-start.4 = (f32[128]{0:T(128)S(1)}, f32[128]{0:T(128)}, u32[]{:S(2)}) copy-start(f32[128]{0:T(128)} %param.21) | copy-start | bytes 1540
  34.6 19.6 %copy-start.5 = (f32[128]{0:T(128)S(1)}, f32[128]{0:T(128)}, u32[]{:S(2)}) copy-start(f32[128]{0:T(128)} %param.22) | copy-start | bytes 1540
  74.2 23.7 %copy-start.2 = (bf16[128,128]{1,0:T(8,128)(2,1)S(1)}, bf16[128,128]{1,0:T(8,128)(2,1)}, u32[]{:S(2)}) copy-start(bf16[128,128]{1,0:T(8,128)(2,1)} %w_out.1) | copy-start | bytes 98308
  97.8 22.1 %copy-start = (bf16[64,32,128]{2,1,0:T(8,128)(2,1)S(1)}, bf16[64,32,128]{2,1,0:T(8,128)(2,1)}, u32[]{:S(2)}) copy-start(bf16[64,32,128]{2,1,0:T(8,128)(2,1)} %pair.1) | copy-start | bytes 1572868
  97.9 22.1 %copy-start.1 = (bf16[128,512]{1,0:T(8,128)(2,1)S(1)}, bf16[128,512]{1,0:T(8,128)(2,1)}, u32[]{:S(2)}) copy-start(bf16[128,512]{1,0:T(8,128)(2,1)} %w_proj.1) | copy-start | bytes 393220
  97.9 22.1 %copy-start.3 = (bf16[128,128]{1,0:T(8,128)(2,1)S(1)}, bf16[128,128]{1,0:T(8,128)(2,1)}, u32[]{:S(2)}) copy-start(bf16[128,128]{1,0:T(8,128)(2,1)} %w_gate.1) | copy-start | bytes 98308
  97.9 22.1 %copy-start.6 = (f32[128]{0:T(128)S(1)}, f32[128]{0:T(128)}, u32[]{:S(2)}) copy-start(f32[128]{0:T(128)} %param.16) | copy-start | bytes 1540
  115.4 14.8 %all-to-all-start.5 = ((bf16[128,3,2,128]{3,2,1,0:T(2,128)(2,1)}), bf16[128,3,2,128]{3,2,1,0:T(2,128)(2,1)S(1)}, u32[]{:S(2)}, u32[]{:S(2)}) async-start(bf16[128,3,2,128]{3,2,1,0:T(2,128)(2,1)} %bitcast.7), calls=%async_computation.5 | async-start | bytes 393216 | tf_op jit(solution)/shard_map/all_to_all | solution.py:308

commit v6 on v5

--- a/solution.py
+++ b/solution.py
@@ -10,7 +10,7 @@
 EPS = 1e-05
 F32 = jnp.float32
 BF16 = jnp.bfloat16
-AXES = ("col", "row")
+AXES = ("row", "col")
 
 ROWS = 64
 COLS = 32
@@ -25,7 +25,6 @@
 WIDE = 256
 STEPS = PAIRS // WIDE
 EACH = WIDE // ROWS
-PIECES = 2
 TILES = N // LANES
 SHARE = 6 * CH // DEV
 
@@ -68,57 +67,56 @@
         step(s)
 
 
+def fetch(sems, first, *routes):
+    copies = [
+        pltpu.make_async_copy(src, dst, sems.at[first + n]) for n, (src, dst) in enumerate(routes)
+    ]
+    for copy in copies:
+        copy.start()
+    return copies
+
+
+LANE = (1, LANES)
+
+
+def spread_rows(values, row_start):
+    place = lax.broadcasted_iota(jnp.int32, LANE, 1) % ROWS
+    out = jnp.zeros(LANE, jnp.int32)
+    for i in range(ROWS):
+        out = jnp.where(place == i, values[row_start + i], out)
+    return out
+
+
+def pick(values, col_start, s, combine):
+    low = lax.broadcasted_iota(jnp.int32, LANE, 1) < ROWS
+    parts = []
+    for e in range(0, EACH, 2):
+        k = col_start + EACH * s + e
+        parts.append(combine(jnp.where(low, values[k], values[k + 1])).astype(F32))
+    return jnp.concatenate(parts, axis=1)
+
+
 def front_kernel(
-    mask_h, chain_h, gain_h, bias_h, chain_bias_h, out_gain_h, w_proj_h, w_gate_h, w_out_h,
-    pair_h, cot_h,
-    send, zn_t, grad_update, q_out, slope, factor,
-    mask_s, chain_s, gain, bias, chain_bias, out_gain, w_proj, w_gate, w_out, pair, cot,
-    xs, cs, wp_t, wg_t, sems,
+    mask_h, gain_h, bias_h, w_proj_h, pair_h,
+    send, zn_t, factor,
+    mask_s, gain, bias, w_proj, pair, xs, wp_t, sems,
 ):
-    small = [
-        pltpu.make_async_copy(src, dst, sems.at[n])
-        for n, (src, dst) in enumerate(
-            (
-                (mask_h, mask_s), (chain_h, chain_s), (gain_h, gain), (bias_h, bias),
-                (chain_bias_h, chain_bias), (out_gain_h, out_gain), (w_proj_h, w_proj),
-                (w_gate_h, w_gate), (w_out_h, w_out),
-            )
-        )
-    ]
-    pieces = []
-    for n in range(PIECES):
-        spot = slice(n * COLS // PIECES, (n + 1) * COLS // PIECES)
-        for m, (src, dst) in enumerate(((pair_h, pair), (cot_h, cot))):
-            pieces.append(
-                pltpu.make_async_copy(src.at[:, spot], dst.at[:, spot], sems.at[9 + 2 * n + m])
-            )
-    for copy in small + pieces:
-        copy.start()
-    for copy in small:
+    copies = fetch(
+        sems, 0, (mask_h, mask_s), (gain_h, gain), (bias_h, bias), (w_proj_h, w_proj), (pair_h, pair)
+    )
+    for copy in copies[:4]:
         copy.wait()
-    columns = jnp.concatenate(
-        [gain[...], bias[...], 0.5 * chain_bias[...], out_gain[...], jnp.zeros((4, CH), F32)], axis=0
-    ).T
-    gain_c, bias_c, chain_c, out_gain_c = (
-        jnp.broadcast_to(columns[:, n : n + 1], (CH, WIDE)) for n in range(4)
-    )
     row_start = lax.axis_index("row") * ROWS
     col_start = lax.axis_index("col") * COLS
     for n in range(4):
         weights = w_proj[:, n * CH : (n + 1) * CH].astype(F32).T
         wp_t[n * CH : (n + 1) * CH] = (weights if n % 2 else 0.5 * weights).astype(BF16)
-    wg_t[...] = (0.5 * w_gate[...].astype(F32).T).astype(BF16)
-    lane = lax.broadcasted_iota(jnp.int32, (1, LANES), 1)
-    place = lane % ROWS
-    mask_row = jnp.zeros((1, LANES), jnp.int32)
-    chain_row = jnp.zeros((1, LANES), jnp.int32)
-    for i in range(ROWS):
-        here = place == i
-        mask_row = jnp.where(here, mask_s[row_start + i], mask_row)
-        chain_row = jnp.where(here, chain_s[row_start + i], chain_row)
-    low = lane < ROWS
-
-    def step(s):
+    columns = jnp.concatenate([gain[...], bias[...], jnp.zeros((6, CH), F32)], axis=0).T
+    gain_c, bias_c = (jnp.broadcast_to(columns[:, n : n + 1], (CH, WIDE)) for n in range(2))
+    mask_row = spread_rows(mask_s, row_start)
+    copies[4].wait()
+    xs[...] = pair[...].astype(F32)
+    for s in range(STEPS):
         here = lanes_of(s)
         x = load_chunk(xs.reshape(PAIRS, CH), s)
         mean = jnp.mean(x, axis=0, keepdims=True)
@@ -126,13 +124,7 @@
         inverse = lax.rsqrt(jnp.mean(centred * centred, axis=0, keepdims=True) + EPS)
         zn = (centred * inverse * gain_c + bias_c).astype(BF16)
         zn_t[:, here] = zn
-        mask, same = [], []
-        for e in range(0, EACH, 2):
-            k = col_start + EACH * s + e
-            mask.append((jnp.where(low, mask_s[k], mask_s[k + 1]) * mask_row).astype(F32))
-            same.append((jnp.where(low, chain_s[k], chain_s[k + 1]) == chain_row).astype(F32))
-        half = 0.5 * jnp.concatenate(mask, axis=1)
-        same = jnp.concatenate(same, axis=1)
+        half = 0.5 * pick(mask_s, col_start, s, lambda other: other * mask_row)
         proj = dot(wp_t[...], zn, 1, 0)
         for side in range(2):
             base = 2 * CH * side
@@ -141,30 +133,26 @@
             send[:, lanes_of(s, side * PAIRS)] = act.astype(BF16)
             factor[base : base + CH, here] = (act - act * plain).astype(BF16)
             factor[base + CH : base + 2 * CH, here] = plain.astype(BF16)
-        gate = 0.5 * jnp.tanh(dot(wg_t[...], zn, 1, 0) + same * chain_c) + 0.5
-        gated = load_chunk(cs.reshape(PAIRS, CH), s) * gate
-        update = gated.astype(BF16)
-        grad_update[:, here] = update
-        slope[:, here] = gated - gated * gate
-        q_out[:, here] = dot(w_out[...], update, 1, 0) * out_gain_c
-
-    for n in range(PIECES):
-        pieces[2 * n].wait()
-        pieces[2 * n + 1].wait()
-        spot = slice(n * COLS // PIECES, (n + 1) * COLS // PIECES)
-        xs[:, spot] = pair[:, spot].astype(F32)
-        cs[:, spot] = cot[:, spot].astype(F32)
-        for u in range(STEPS // PIECES):
-            step(n * (STEPS // PIECES) + u)
-
-
-def mix_kernel(recv, send, a_t, b_t, mixed):
+
+
+def mix_kernel(
+    chain_h, chain_bias, out_gain, w_gate, w_out, cot, zn_t, recv,
+    send, a_t, b_t, grad_update, q_out, slope,
+    mixed, chain_s, cs, wg_t, sems,
+):
+    (copy,) = fetch(sems, 0, (chain_h, chain_s))
+    cs[...] = cot[...].astype(F32)
+    wg_t[...] = (0.5 * w_gate[...].astype(F32).T).astype(BF16)
+    columns = jnp.concatenate(
+        [0.5 * chain_bias[...], out_gain[...], jnp.zeros((6, CH), F32)], axis=0
+    ).T
+    chain_c, out_gain_c = (jnp.broadcast_to(columns[:, n : n + 1], (CH, WIDE)) for n in range(2))
     for c in range(NCOL):
         for t in range(TILES):
             for offset, out in ((0, a_t), (CHUNKS, b_t)):
                 rows = slice(offset, offset + CHUNKS)
-                first = recv[8 * c + 2 * t, rows].astype(F32)
-                second = recv[8 * c + 2 * t + 1, rows].astype(F32)
+                first = recv[32 * t + c, rows].astype(F32)
+                second = recv[32 * t + 16 + c, rows].astype(F32)
                 even, odd = swap_halves(first, second)
                 spot = slice(t * LANES, (t + 1) * LANES)
                 out[32 * c : 32 * c + 16, spot] = even.astype(BF16)
@@ -172,13 +160,26 @@
     product = dot(b_t[...], a_t[...], 0, 0)
     for t in range(TILES):
         mixed[t] = product[:, t * LANES : (t + 1) * LANES]
+    copy.wait()
+    row_start = lax.axis_index("row") * ROWS
+    col_start = lax.axis_index("col") * COLS
+    chain_row = spread_rows(chain_s, row_start)
+    for s in range(STEPS):
+        here = lanes_of(s)
+        same = pick(chain_s, col_start, s, lambda other: other == chain_row)
+        gate = 0.5 * jnp.tanh(dot(wg_t[...], zn_t[:, here], 1, 0) + same * chain_c) + 0.5
+        gated = load_chunk(cs.reshape(PAIRS, CH), s) * gate
+        update = gated.astype(BF16)
+        grad_update[:, here] = update
+        slope[:, here] = gated - gated * gate
+        q_out[:, here] = dot(w_out[...], update, 1, 0) * out_gain_c
     for c in range(NCOL):
         for t in range(TILES):
             first = mixed[t, pl.ds(32 * c, CHUNKS, stride=2), :]
             second = mixed[t, pl.ds(32 * c + 1, CHUNKS, stride=2), :]
             even, odd = swap_halves(first, second)
-            send[8 * c + 2 * t] = even.astype(BF16)
-            send[8 * c + 2 * t + 1] = odd.astype(BF16)
+            send[32 * t + c] = even.astype(BF16)
+            send[32 * t + 16 + c] = odd.astype(BF16)
 
 
 def middle_kernel(recv, q_in, gain, bias, send, y_out):
@@ -205,7 +206,7 @@
     for c in range(NCOL):
         for t in range(TILES):
             even, odd = swap_halves(
-                recv[8 * c + 2 * t].astype(F32), recv[8 * c + 2 * t + 1].astype(F32)
+                recv[32 * t + c].astype(F32), recv[32 * t + 16 + c].astype(F32)
             )
             strided[t, pl.ds(32 * c, CHUNKS, stride=2), :] = even
             strided[t, pl.ds(32 * c + 1, CHUNKS, stride=2), :] = odd
@@ -220,8 +221,8 @@
                 even, odd = swap_halves(
                     product[32 * c : 32 * c + 16, spot], product[32 * c + 16 : 32 * c + 32, spot]
                 )
-                send[8 * c + 2 * t, rows] = even.astype(BF16)
-                send[8 * c + 2 * t + 1, rows] = odd.astype(BF16)
+                send[32 * t + c, rows] = even.astype(BF16)
+                send[32 * t + 16 + c, rows] = odd.astype(BF16)
 
 
 def back_kernel(
@@ -286,17 +287,19 @@
     grad_out[...] = whole[5 * CH :]
 
 
-def call(kernel, outs, scratch, flops, args, in_hbm=False, vmem=16):
-    space = pltpu.HBM if in_hbm else pltpu.VMEM
+def call(kernel, outs, scratch, flops, args, hbm=0, vmem=16):
     moved = sum(x.size * x.dtype.itemsize for x in args) + sum(
         x.size * x.dtype.itemsize for x in outs
     )
-    if in_hbm:
-        args = [pltpu.with_memory_space_constraint(x, pltpu.HBM) for x in args]
+    spaces = [pltpu.HBM] * hbm + [pltpu.VMEM] * (len(args) - hbm)
+    args = [
+        pltpu.with_memory_space_constraint(x, pltpu.HBM) if n < hbm else x
+        for n, x in enumerate(args)
+    ]
     return pl.pallas_call(
         kernel,
         out_shape=outs,
-        in_specs=[pl.BlockSpec(memory_space=space)] * len(args),
+        in_specs=[pl.BlockSpec(memory_space=space) for space in spaces],
         out_specs=[pl.BlockSpec(memory_space=pltpu.VMEM)] * len(outs),
         scratch_shapes=scratch,
         compiler_params=pltpu.CompilerParams(vmem_limit_bytes=vmem << 20),
@@ -309,7 +312,8 @@
 
 
 def exchange_terms(x):
-    return exchange(x.reshape(DEV, SHARE // 2, 2, LANES)).reshape(x.shape)
+    split = x.reshape(DEV, SHARE // 2, 2, LANES)
+    return lax.all_to_all(split, AXES[::-1], 0, 0, tiled=True).reshape(x.shape)
 
 
 def split_rows(x):
@@ -341,35 +345,34 @@
     def flat(x):
         return x.reshape(1, -1)
 
-    send_ab, zn_t, grad_update, q, slope, factor = call(
+    send_ab, zn_t, factor = call(
         front_kernel,
+        [S((CH, 2 * PAIRS), BF16), S((CH, PAIRS), BF16), S((4 * CH, PAIRS), BF16)],
         [
-            S((CH, 2 * PAIRS), BF16), S((CH, PAIRS), BF16), S((CH, PAIRS), BF16),
-            S((CH, PAIRS), F32), S((CH, PAIRS), F32), S((4 * CH, PAIRS), BF16),
+            pltpu.SMEM((N,), jnp.int32), V((1, CH), F32), V((1, CH), F32), V((CH, 4 * CH), BF16),
+            V((ROWS, COLS, CH), BF16), V((ROWS, COLS, CH), F32), V((4 * CH, CH), BF16),
+            pltpu.SemaphoreType.DMA((5,)),
+        ],
+        4 * unit,
+        (res_mask, flat(ln_in_gain), flat(ln_in_bias), w_proj, pair),
+        hbm=5,
+    )
+    recv_ab = exchange(split_rows(send_ab))
+    send_mixed, a_t, b_t, grad_update, q, slope = call(
+        mix_kernel,
+        [
+            S((DEV, CHUNKS, LANES), BF16), S((N, N), BF16), S((N, N), BF16),
+            S((CH, PAIRS), BF16), S((CH, PAIRS), F32), S((CH, PAIRS), F32),
         ],
         [
-            pltpu.SMEM((N,), jnp.int32), pltpu.SMEM((N,), jnp.int32),
-            V((1, CH), F32), V((1, CH), F32), V((1, CH), F32), V((1, CH), F32),
-            V((CH, 4 * CH), BF16), V((CH, CH), BF16), V((CH, CH), BF16),
-            V((ROWS, COLS, CH), BF16), V((ROWS, COLS, CH), BF16),
-            V((ROWS, COLS, CH), F32), V((ROWS, COLS, CH), F32),
-            V((4 * CH, CH), BF16), V((CH, CH), BF16),
-            pltpu.SemaphoreType.DMA((9 + 2 * PIECES,)),
+            V((TILES, N, LANES), F32), pltpu.SMEM((N,), jnp.int32), V((ROWS, COLS, CH), F32),
+            V((CH, CH), BF16), pltpu.SemaphoreType.DMA((1,)),
         ],
-        6 * unit,
+        2 * N * N * N + 2 * unit,
         (
-            res_mask, chain, flat(ln_in_gain), flat(ln_in_bias), flat(chain_bias),
-            flat(ln_out_gain), w_proj, w_gate, w_out, pair, cotangent,
+            chain, flat(chain_bias), flat(ln_out_gain), w_gate, w_out, cotangent, zn_t, recv_ab,
         ),
-        in_hbm=True,
-    )
-    recv_ab = exchange(split_rows(send_ab))
-    send_mixed, a_t, b_t = call(
-        mix_kernel,
-        [S((DEV, CHUNKS, LANES), BF16), S((N, N), BF16), S((N, N), BF16)],
-        [V((TILES, N, LANES), F32)],
-        2 * N * N * N,
-        (recv_ab,),
+        hbm=1,
     )
     send_grad, y = call(
         middle_kernel,

time: 131 us -> 130 us (level)
  blocking collectives: 105 us -> 103 us
    all_to_all x5 -> x4, blocking collectives: 105 us -> 88.6 us  [exchange(): return lax.all_to_all(x, AXES, 0, 0, tiled=True)]
    all_to_all x0 -> x1, blocking collectives: none -> 14.6 us  [exchange_terms(): return lax.all_to_all(split, AXES[::-1], 0, 0, tiled=True).reshape(x.shape)]
where the time goes in v6:
time: 130 us; the launch traced here: 129 us
  blocking collectives  103 us (79%)
  Pallas kernels  12.7 us (10%)
  waiting for transfers between devices  7.07 us (5%)
  starting transfers between devices  4.59 us (4%)
    all_to_all x4, blocking collectives, exchange(): return lax.all_to_all(x, AXES, 0, 0, tiled=True)  88.6 us
    all_to_all x1, blocking collectives, exchange_terms(): return lax.all_to_all(split, AXES[::-1], 0, 0, tiled=True).reshape(x.shape)  14.6 us
    pallas_call x8, Pallas kernels, call(): pl.pallas_call(kernel, out_shape=outs, in_specs=[pl.BlockSpec(memory_spac...  12.7 us
    all_to_all x1, waiting for transfers between devices, exchange_terms(): return lax.all_to_all(split, AXES[::-1], 0, 0, tiled=True).reshape(x.shape)  7.07 us
    all_to_all x1, starting transfers between devices, exchange_terms(): return lax.all_to_all(split, AXES[::-1], 0, 0, tiled=True).reshape(x.shape)  4.59 us
  transfers between devices with their start and end apart: 1, of which 1 were waited for; matrix products, arithmetic and copies ran while one was open for 0% of the time, Pallas kernels for 2%

profile of v6, /device:TPU:1, one launch (start us, length us, event | category | flops | bytes accessed | tf_op | source)
XLA Modules:
  0.0 129.4 jit_solution(13534203947120753648)
XLA Ops:
  0.6 2.8 %shard_map.147 = (bf16[128,4096]{1,0:T(8,128)(2,1)S(1)}, bf16[128,2048]{1,0:T(8,128)(2,1)S(1)}, bf16[512,2048]{1,0:T(8,128)(2,1)S(1)}) custom-call(s32[512]{0:T(512)} %mask_h.1, f32[1,128]{1,0:T(1,128)} %bitcast.32, f32[1,128]{1,0:T(1,128)} %bitcast.38, bf16[128,512]{1,0:T(8,128)(2,1)} %w_proj.1, bf16[64,32,128]{2,1,0:T(8,128)(2,1)} %pair.1), custom_call_target="tpu_custom_call" | custom-call | flops 268435456 | bytes 4328448 | tf_op jit(solution)/shard_map/pallas_call | solution.py:299
  3.4 0.0 copy-start
  3.4 0.0 copy-start.2
  3.4 0.0 copy-start.3
  3.5 0.0 copy-start.5
  3.5 0.0 copy-start.6
  3.5 0.2 copy.16
  3.7 30.0 %all_to_all.30.recv = bf16[128,32,128]{2,1,0:T(8,128)(2,1)S(1)} all-to-all(bf16[128,32,128]{2,1,0:T(8,128)(2,1)S(1)} %bitcast.34), channel_id=1, replica_groups=mesh['row'=8,'col'=16] {'row','col'}, dimensions={0} | all-to-all | bytes 2097152 | tf_op jit(solution)/shard_map/all_to_all | solution.py:311
  33.7 0.0 copy-done
  33.8 0.0 copy-done.2
  33.8 0.0 copy-done.5
  33.8 0.0 copy-done.6
  33.8 0.0 copy-start.7
  33.8 2.2 %shard_map.148 = (bf16[128,16,128]{2,1,0:T(8,128)(2,1)S(1)}, bf16[512,512]{1,0:T(8,128)(2,1)S(1)}, bf16[512,512]{1,0:T(8,128)(2,1)S(1)}, bf16[128,2048]{1,0:T(8,...) custom-call(s32[512]{0:T(512)} %chain_h.1, f32[1,128]{1,0:T(1,128)S(1)} %bitcast.30, ...), custom_call_target="tpu_custom_call" | custom-call | flops 402653184 | bytes 6360064 | tf_op jit(solution)/shard_map/pallas_call | solution.py:299
  36.0 18.2 %all_to_all.31 = bf16[128,16,128]{2,1,0:T(8,128)(2,1)S(1)} all-to-all(bf16[128,16,128]{2,1,0:T(8,128)(2,1)S(1)} %get-tuple-element.26), channel_id=1, replica_groups=mesh['row'=8,'col'=16] {'row','col'}, dimensions={0} | all-to-all | bytes 1048576 | tf_op jit(solution)/shard_map/all_to_all | solution.py:311
  54.1 0.1 copy.23
  54.3 0.8 shard_map.149
  55.1 0.1 copy.18
  55.3 17.8 %all_to_all.32.recv = bf16[128,16,128]{2,1,0:T(8,128)(2,1)S(1)} all-to-all(bf16[128,16,128]{2,1,0:T(8,128)(2,1)S(1)} %bitcast.37), channel_id=1, replica_groups=mesh['row'=8,'col'=16] {'row','col'}, dimensions={0} | all-to-all | bytes 1048576 | tf_op jit(solution)/shard_map/all_to_all | solution.py:311
  73.0 1.0 shard_map.150
  74.0 22.7 %all_to_all.33 = bf16[128,32,128]{2,1,0:T(8,128)(2,1)S(1)} all-to-all(bf16[128,32,128]{2,1,0:T(8,128)(2,1)S(1)} %shard_map.150), channel_id=1, replica_groups=mesh['row'=8,'col'=16] {'row','col'}, dimensions={0} | all-to-all | bytes 2097152 | tf_op jit(solution)/shard_map/all_to_all | solution.py:311
  96.7 0.5 copy.22
  97.2 0.0 copy-start.1
  97.2 0.0 copy-start.4
  97.2 0.0 copy-start.8
  97.2 1.2 shard_map.151
  98.4 14.6 %all_to_all.34 = bf16[128,3,2,128]{3,2,1,0:T(2,128)(2,1)S(1)} all-to-all(bf16[128,3,2,128]{3,2,1,0:T(2,128)(2,1)S(1)} %bitcast.27), channel_id=1, replica_groups=mesh['row'=8,'col'=16] {'col','row'}, dimensions={0} | all-to-all | bytes 393216 | tf_op jit(solution)/shard_map/all_to_all | solution.py:316
  113.0 0.7 shard_map.152
  113.8 4.6 %all-to-all-start.5 = ((bf16[128,3,2,128]{3,2,1,0:T(2,128)(2,1)}), bf16[128,3,2,128]{3,2,1,0:T(2,128)(2,1)S(1)}, u32[]{:S(2)}, u32[]{:S(2)}) async-start(bf16[128,3,2,128]{3,2,1,0:T(2,128)(2,1)} %bitcast.7), calls=%async_computation.5 | async-start | bytes 393216 | tf_op jit(solution)/shard_map/all_to_all | solution.py:316
  118.4 3.1 %shard_map.153 = bf16[64,32,128]{2,1,0:T(8,128)(2,1)} custom-call(bf16[512,2048]{1,0:T(8,128)(2,1)S(1)} %get-tuple-element.38.grad_p, bf16[128,2048]{1,0:T(8,128)(2,1)S(1)} %get-tuple-element.39.logit_t, bf16[64,32,128]{2,1,0:T(8,128)(2,1)S(1)} %copy-done.1, f32[1,128]{1,0:T(1,128)S(1)} %bitcast.33, bf16[128,512]{1,0:T(8,128)(2,1)S(1)} %copy-done.4, ...), custom_call_target="tpu_custom_call" | custom-call | flops 335544320 | bytes 3834368 | tf_op jit(solution)/shard_map/pallas_call | solution.py:299
  121.5 7.1 %all-to-all-done.5 = bf16[128,3,2,128]{3,2,1,0:T(2,128)(2,1)S(1)} async-done(((bf16[128,3,2,128]{3,2,1,0:T(2,128)(2,1)}), bf16[128,3,2,128]{3,2,1,0:T(2,128)(2,1)S(1)}, u32[]{:S(2)}, u32[]{:S(2)}) %all-to-all-start.5) | async-done | bytes 196640 | tf_op jit(solution)/shard_map/all_to_all | solution.py:316
  128.6 0.9 shard_map.154
  (5 shorter events, 0.0 us)
Async XLA Ops:
  3.4 30.3 %copy-start = (bf16[64,32,128]{2,1,0:T(8,128)(2,1)S(1)}, bf16[64,32,128]{2,1,0:T(8,128)(2,1)}, u32[]{:S(2)}) copy-start(bf16[64,32,128]{2,1,0:T(8,128)(2,1)} %cot.1) | copy-start | bytes 1572868
  3.4 30.3 %copy-start.2 = (bf16[128,128]{1,0:T(8,128)(2,1)S(1)}, bf16[128,128]{1,0:T(8,128)(2,1)}, u32[]{:S(2)}) copy-start(bf16[128,128]{1,0:T(8,128)(2,1)} %w_out.3) | copy-start | bytes 98308
  3.4 30.3 %copy-start.3 = (bf16[128,128]{1,0:T(8,128)(2,1)S(1)}, bf16[128,128]{1,0:T(8,128)(2,1)}, u32[]{:S(2)}) copy-start(bf16[128,128]{1,0:T(8,128)(2,1)} %w_gate.3) | copy-start | bytes 98308
  3.5 30.3 %copy-start.5 = (f32[128]{0:T(128)S(1)}, f32[128]{0:T(128)}, u32[]{:S(2)}) copy-start(f32[128]{0:T(128)} %param.21) | copy-start | bytes 1540
  3.5 30.3 %copy-start.6 = (f32[128]{0:T(128)S(1)}, f32[128]{0:T(128)}, u32[]{:S(2)}) copy-start(f32[128]{0:T(128)} %param.20) | copy-start | bytes 1540
  33.8 20.5 %copy-start.7 = (f32[128]{0:T(128)S(1)}, f32[128]{0:T(128)}, u32[]{:S(2)}) copy-start(f32[128]{0:T(128)} %param.22) | copy-start | bytes 1540
  97.2 21.2 %copy-start.1 = (bf16[64,32,128]{2,1,0:T(8,128)(2,1)S(1)}, bf16[64,32,128]{2,1,0:T(8,128)(2,1)}, u32[]{:S(2)}) copy-start(bf16[64,32,128]{2,1,0:T(8,128)(2,1)} %pair.1) | copy-start | bytes 1572868
  97.2 21.2 %copy-start.4 = (bf16[128,512]{1,0:T(8,128)(2,1)S(1)}, bf16[128,512]{1,0:T(8,128)(2,1)}, u32[]{:S(2)}) copy-start(bf16[128,512]{1,0:T(8,128)(2,1)} %w_proj.1) | copy-start | bytes 393220
  97.2 21.2 %copy-start.8 = (f32[128]{0:T(128)S(1)}, f32[128]{0:T(128)}, u32[]{:S(2)}) copy-start(f32[128]{0:T(128)} %param.16) | copy-start | bytes 1540
  113.8 14.8 %all-to-all-start.5 = ((bf16[128,3,2,128]{3,2,1,0:T(2,128)(2,1)}), bf16[128,3,2,128]{3,2,1,0:T(2,128)(2,1)S(1)}, u32[]{:S(2)}, u32[]{:S(2)}) async-start(bf16[128,3,2,128]{3,2,1,0:T(2,128)(2,1)} %bitcast.7), calls=%async_computation.5 | async-start | bytes 393216 | tf_op jit(solution)/shard_map/all_to_all | solution.py:316

commit v7 on v6

--- a/solution.py
+++ b/solution.py
@@ -279,15 +279,21 @@
         out[8 * SHARE * n : 8 * SHARE * (n + 1)] = mine
 
 
-def split_kernel(sums, grad_proj, grad_gate, grad_out):
-    whole = sums[...].astype(F32)
+def split_kernel(sums, grad_proj, grad_gate, grad_out, wide, gate, out, sems):
+    copies = []
     for part in range(4):
-        grad_proj[:, part * CH : (part + 1) * CH] = whole[part * CH : (part + 1) * CH].T
-    grad_gate[...] = whole[4 * CH : 5 * CH].T
-    grad_out[...] = whole[5 * CH :]
-
-
-def call(kernel, outs, scratch, flops, args, hbm=0, vmem=16):
+        spot = slice(part * CH, (part + 1) * CH)
+        wide[:, spot] = sums[spot].astype(F32).T
+        copies += fetch(sems, part, (wide.at[:, spot], grad_proj.at[:, spot]))
+    gate[...] = sums[4 * CH : 5 * CH].astype(F32).T
+    copies += fetch(sems, 4, (gate, grad_gate))
+    out[...] = sums[5 * CH :].astype(F32)
+    copies += fetch(sems, 5, (out, grad_out))
+    for copy in copies:
+        copy.wait()
+
+
+def call(kernel, outs, scratch, flops, args, hbm=0, out_space=pltpu.VMEM, vmem=16):
     moved = sum(x.size * x.dtype.itemsize for x in args) + sum(
         x.size * x.dtype.itemsize for x in outs
     )
@@ -300,7 +306,7 @@
         kernel,
         out_shape=outs,
         in_specs=[pl.BlockSpec(memory_space=space) for space in spaces],
-        out_specs=[pl.BlockSpec(memory_space=pltpu.VMEM)] * len(outs),
+        out_specs=[pl.BlockSpec(memory_space=out_space)] * len(outs),
         scratch_shapes=scratch,
         compiler_params=pltpu.CompilerParams(vmem_limit_bytes=vmem << 20),
         cost_estimate=pl.CostEstimate(flops=flops, bytes_accessed=moved, transcendentals=0),
@@ -407,7 +413,12 @@
         (grad_p, logit_t, pair, flat(ln_in_gain), w_proj, w_gate),
     )
     grad_proj, grad_gate, grad_out = call(
-        split_kernel, [S((CH, 4 * CH), F32), S((CH, CH), F32), S((CH, CH), F32)], [], 0, (sums,)
+        split_kernel,
+        [S((CH, 4 * CH), F32), S((CH, CH), F32), S((CH, CH), F32)],
+        [V((CH, 4 * CH), F32), V((CH, CH), F32), V((CH, CH), F32), pltpu.SemaphoreType.DMA((6,))],
+        0,
+        (sums,),
+        out_space=pltpu.HBM,
     )
     return (grad_pair, grad_proj, grad_gate, grad_out)
 

time: 130 us -> 130 us (level)
  no operation moved by 1% of the time
where the time goes in v7:
time: 130 us; the launch traced here: 129 us
  blocking collectives  103 us (79%)
  Pallas kernels  12.7 us (10%)
  waiting for transfers between devices  7.07 us (5%)
  starting transfers between devices  4.59 us (4%)
    all_to_all x4, blocking collectives, exchange(): return lax.all_to_all(x, AXES, 0, 0, tiled=True)  88.6 us
    all_to_all x1, blocking collectives, exchange_terms(): return lax.all_to_all(split, AXES[::-1], 0, 0, tiled=True).reshape(x.shape)  14.6 us
    pallas_call x8, Pallas kernels, call(): pl.pallas_call(kernel, out_shape=outs, in_specs=[pl.BlockSpec(memory_spac...  12.7 us
    all_to_all x1, waiting for transfers between devices, exchange_terms(): return lax.all_to_all(split, AXES[::-1], 0, 0, tiled=True).reshape(x.shape)  7.07 us
    all_to_all x1, starting transfers between devices, exchange_terms(): return lax.all_to_all(split, AXES[::-1], 0, 0, tiled=True).reshape(x.shape)  4.59 us
  transfers between devices with their start and end apart: 1, of which 1 were waited for; matrix products, arithmetic and copies ran while one was open for 0% of the time, Pallas kernels for 2%

profile of v7, /device:TPU:1, one launch (start us, length us, event | category | flops | bytes accessed | tf_op | source)
XLA Modules:
  0.0 129.5 jit_solution(16858531216792065033)
XLA Ops:
  0.6 2.8 %shard_map.147 = (bf16[128,4096]{1,0:T(8,128)(2,1)S(1)}, bf16[128,2048]{1,0:T(8,128)(2,1)S(1)}, bf16[512,2048]{1,0:T(8,128)(2,1)S(1)}) custom-call(s32[512]{0:T(512)} %mask_h.1, f32[1,128]{1,0:T(1,128)} %bitcast.32, f32[1,128]{1,0:T(1,128)} %bitcast.38, bf16[128,512]{1,0:T(8,128)(2,1)} %w_proj.1, bf16[64,32,128]{2,1,0:T(8,128)(2,1)} %pair.1), custom_call_target="tpu_custom_call" | custom-call | flops 268435456 | bytes 4328448 | tf_op jit(solution)/shard_map/pallas_call | solution.py:305
  3.4 0.0 copy-start
  3.4 0.0 copy-start.2
  3.4 0.0 copy-start.3
  3.5 0.0 copy-start.5
  3.5 0.0 copy-start.6
  3.5 0.2 copy.16
  3.7 30.0 %all_to_all.30.recv = bf16[128,32,128]{2,1,0:T(8,128)(2,1)S(1)} all-to-all(bf16[128,32,128]{2,1,0:T(8,128)(2,1)S(1)} %bitcast.34), channel_id=1, replica_groups=mesh['row'=8,'col'=16] {'row','col'}, dimensions={0} | all-to-all | bytes 2097152 | tf_op jit(solution)/shard_map/all_to_all | solution.py:317
  33.7 0.0 copy-done
  33.8 0.0 copy-done.2
  33.8 0.0 copy-done.3
  33.8 0.0 copy-start.7
  33.8 2.2 %shard_map.148 = (bf16[128,16,128]{2,1,0:T(8,128)(2,1)S(1)}, bf16[512,512]{1,0:T(8,128)(2,1)S(1)}, bf16[512,512]{1,0:T(8,128)(2,1)S(1)}, bf16[128,2048]{1,0:T(8,...) custom-call(s32[512]{0:T(512)} %chain_h.1, f32[1,128]{1,0:T(1,128)S(1)} %bitcast.30, ...), custom_call_target="tpu_custom_call" | custom-call | flops 402653184 | bytes 6360064 | tf_op jit(solution)/shard_map/pallas_call | solution.py:305
  36.0 18.2 %all_to_all.31 = bf16[128,16,128]{2,1,0:T(8,128)(2,1)S(1)} all-to-all(bf16[128,16,128]{2,1,0:T(8,128)(2,1)S(1)} %get-tuple-element.26), channel_id=1, replica_groups=mesh['row'=8,'col'=16] {'row','col'}, dimensions={0} | all-to-all | bytes 1048576 | tf_op jit(solution)/shard_map/all_to_all | solution.py:317
  54.1 0.1 copy.23
  54.3 0.0 copy-done.7
  54.3 0.8 shard_map.149
  55.1 0.1 copy.18
  55.3 17.8 %all_to_all.32.recv = bf16[128,16,128]{2,1,0:T(8,128)(2,1)S(1)} all-to-all(bf16[128,16,128]{2,1,0:T(8,128)(2,1)S(1)} %bitcast.37), channel_id=1, replica_groups=mesh['row'=8,'col'=16] {'row','col'}, dimensions={0} | all-to-all | bytes 1048576 | tf_op jit(solution)/shard_map/all_to_all | solution.py:317
  73.0 1.0 shard_map.150
  74.0 22.7 %all_to_all.33 = bf16[128,32,128]{2,1,0:T(8,128)(2,1)S(1)} all-to-all(bf16[128,32,128]{2,1,0:T(8,128)(2,1)S(1)} %shard_map.150), channel_id=1, replica_groups=mesh['row'=8,'col'=16] {'row','col'}, dimensions={0} | all-to-all | bytes 2097152 | tf_op jit(solution)/shard_map/all_to_all | solution.py:317
  96.7 0.5 copy.22
  97.2 0.0 copy-start.1
  97.2 0.0 copy-start.4
  97.2 0.0 copy-start.8
  97.2 1.2 shard_map.151
  98.4 14.6 %all_to_all.34 = bf16[128,3,2,128]{3,2,1,0:T(2,128)(2,1)S(1)} all-to-all(bf16[128,3,2,128]{3,2,1,0:T(2,128)(2,1)S(1)} %bitcast.27), channel_id=1, replica_groups=mesh['row'=8,'col'=16] {'col','row'}, dimensions={0} | all-to-all | bytes 393216 | tf_op jit(solution)/shard_map/all_to_all | solution.py:322
  113.0 0.7 shard_map.152
  113.8 4.6 %all-to-all-start.5 = ((bf16[128,3,2,128]{3,2,1,0:T(2,128)(2,1)}), bf16[128,3,2,128]{3,2,1,0:T(2,128)(2,1)S(1)}, u32[]{:S(2)}, u32[]{:S(2)}) async-start(bf16[128,3,2,128]{3,2,1,0:T(2,128)(2,1)} %bitcast.7), calls=%async_computation.5 | async-start | bytes 393216 | tf_op jit(solution)/shard_map/all_to_all | solution.py:322
  118.4 3.1 %shard_map.153 = bf16[64,32,128]{2,1,0:T(8,128)(2,1)} custom-call(bf16[512,2048]{1,0:T(8,128)(2,1)S(1)} %get-tuple-element.38.grad_p, bf16[128,2048]{1,0:T(8,128)(2,1)S(1)} %get-tuple-element.39.logit_t, bf16[64,32,128]{2,1,0:T(8,128)(2,1)S(1)} %copy-done.1, f32[1,128]{1,0:T(1,128)S(1)} %bitcast.33, bf16[128,512]{1,0:T(8,128)(2,1)S(1)} %copy-done.4, ...), custom_call_target="tpu_custom_call" | custom-call | flops 335544320 | bytes 3834368 | tf_op jit(solution)/shard_map/pallas_call | solution.py:305
  121.5 7.1 %all-to-all-done.5 = bf16[128,3,2,128]{3,2,1,0:T(2,128)(2,1)S(1)} async-done(((bf16[128,3,2,128]{3,2,1,0:T(2,128)(2,1)}), bf16[128,3,2,128]{3,2,1,0:T(2,128)(2,1)S(1)}, u32[]{:S(2)}, u32[]{:S(2)}) %all-to-all-start.5) | async-done | bytes 196640 | tf_op jit(solution)/shard_map/all_to_all | solution.py:322
  128.6 0.9 shard_map.154
  (5 shorter events, 0.0 us)
Async XLA Ops:
  3.4 30.3 %copy-start = (bf16[64,32,128]{2,1,0:T(8,128)(2,1)S(1)}, bf16[64,32,128]{2,1,0:T(8,128)(2,1)}, u32[]{:S(2)}) copy-start(bf16[64,32,128]{2,1,0:T(8,128)(2,1)} %cot.1) | copy-start | bytes 1572868
  3.4 30.3 %copy-start.2 = (bf16[128,128]{1,0:T(8,128)(2,1)S(1)}, bf16[128,128]{1,0:T(8,128)(2,1)}, u32[]{:S(2)}) copy-start(bf16[128,128]{1,0:T(8,128)(2,1)} %w_out.3) | copy-start | bytes 98308
  3.4 30.3 %copy-start.3 = (bf16[128,128]{1,0:T(8,128)(2,1)S(1)}, bf16[128,128]{1,0:T(8,128)(2,1)}, u32[]{:S(2)}) copy-start(bf16[128,128]{1,0:T(8,128)(2,1)} %w_gate.3) | copy-start | bytes 98308
  3.5 30.3 %copy-start.5 = (f32[128]{0:T(128)S(1)}, f32[128]{0:T(128)}, u32[]{:S(2)}) copy-start(f32[128]{0:T(128)} %param.21) | copy-start | bytes 1540
  3.5 30.3 %copy-start.6 = (f32[128]{0:T(128)S(1)}, f32[128]{0:T(128)}, u32[]{:S(2)}) copy-start(f32[128]{0:T(128)} %param.20) | copy-start | bytes 1540
  33.8 20.5 %copy-start.7 = (f32[128]{0:T(128)S(1)}, f32[128]{0:T(128)}, u32[]{:S(2)}) copy-start(f32[128]{0:T(128)} %param.22) | copy-start | bytes 1540
  97.2 21.2 %copy-start.1 = (bf16[64,32,128]{2,1,0:T(8,128)(2,1)S(1)}, bf16[64,32,128]{2,1,0:T(8,128)(2,1)}, u32[]{:S(2)}) copy-start(bf16[64,32,128]{2,1,0:T(8,128)(2,1)} %pair.1) | copy-start | bytes 1572868
  97.2 21.2 %copy-start.4 = (bf16[128,512]{1,0:T(8,128)(2,1)S(1)}, bf16[128,512]{1,0:T(8,128)(2,1)}, u32[]{:S(2)}) copy-start(bf16[128,512]{1,0:T(8,128)(2,1)} %w_proj.1) | copy-start | bytes 393220
  97.2 21.2 %copy-start.8 = (f32[128]{0:T(128)S(1)}, f32[128]{0:T(128)}, u32[]{:S(2)}) copy-start(f32[128]{0:T(128)} %param.16) | copy-start | bytes 1540
  113.8 14.8 %all-to-all-start.5 = ((bf16[128,3,2,128]{3,2,1,0:T(2,128)(2,1)}), bf16[128,3,2,128]{3,2,1,0:T(2,128)(2,1)S(1)}, u32[]{:S(2)}, u32[]{:S(2)}) async-start(bf16[128,3,2,128]{3,2,1,0:T(2,128)(2,1)} %bitcast.7), calls=%async_computation.5 | async-start | bytes 393216 | tf_op jit(solution)/shard_map/all_to_all | solution.py:322

commit v8 on v7

--- a/solution.py
+++ b/solution.py
@@ -202,7 +202,10 @@
     loop(step)
 
 
-def unmix_kernel(recv, a_t, b_t, send, strided, grad):
+def unmix_kernel(
+    recv, a_t, b_t, zn_t, y, slope, grad_update, w_out, send, logit_t, terms, strided, grad, wo_t
+):
+    wo_t[...] = w_out[...].astype(F32).T.astype(BF16)
     for c in range(NCOL):
         for t in range(TILES):
             even, odd = swap_halves(
@@ -212,6 +215,12 @@
             strided[t, pl.ds(32 * c + 1, CHUNKS, stride=2), :] = odd
     for t in range(TILES):
         grad[:, t * LANES : (t + 1) * LANES] = strided[t].astype(BF16)
+    for s in range(STEPS):
+        here = lanes_of(s)
+        update = dot(wo_t[...], y[:, here], 1, 0)
+        logit_t[:, here] = (slope[:, here] * update).astype(BF16)
+    terms[:CH] = dot(logit_t[...], zn_t[...].T, 1, 0).astype(BF16)
+    terms[CH:] = dot(y[...], grad_update[...], 1, 1).astype(BF16)
     for offset, left, dim in ((0, b_t, 0), (CHUNKS, a_t, 1)):
         product = dot(left[...], grad[...], 1, dim)
         rows = slice(offset, offset + CHUNKS)
@@ -225,24 +234,14 @@
                 send[32 * t + 16 + c, rows] = odd.astype(BF16)
 
 
-def back_kernel(
-    recv, zn_t, factor, y, slope, grad_update, w_out, terms, grad_p, logit_t, wo_t
-):
-    wo_t[...] = w_out[...].astype(F32).T.astype(BF16)
-
-    def step(s):
-        here = lanes_of(s)
-        update = dot(wo_t[...], y[:, here], 1, 0)
-        logit_t[:, here] = (slope[:, here] * update).astype(BF16)
+def back_kernel(recv, zn_t, factor, terms_in, terms, grad_p):
+    for s in range(STEPS):
+        here = lanes_of(s)
         for part in range(4):
             rows = slice(part * CH, (part + 1) * CH)
             grad_p[rows, here] = recv[:, lanes_of(s, (part // 2) * PAIRS)] * factor[rows, here]
-
-    loop(step)
-    zn = zn_t[...].T
-    terms[: 4 * CH] = dot(grad_p[...], zn, 1, 0).astype(BF16)
-    terms[4 * CH : 5 * CH] = dot(logit_t[...], zn, 1, 0).astype(BF16)
-    terms[5 * CH :] = dot(y[...], grad_update[...], 1, 1).astype(BF16)
+    terms[: 4 * CH] = dot(grad_p[...], zn_t[...].T, 1, 0).astype(BF16)
+    terms[4 * CH :] = terms_in[...]
 
 
 def last_kernel(grad_p, logit_t, pair, gain, w_proj, w_gate, grad_pair, xs):
@@ -387,19 +386,19 @@
         0,
         (join_rows(exchange(send_mixed)), q, flat(ln_out_gain), flat(ln_out_bias)),
     )
-    (send_back,) = call(
+    send_back, logit_t, terms_in = call(
         unmix_kernel,
-        [S((DEV, 2 * CHUNKS, LANES), BF16)],
-        [V((TILES, N, LANES), F32), V((N, N), BF16)],
-        4 * N * N * N,
-        (exchange(split_rows(send_grad)), a_t, b_t),
-    )
-    terms, grad_p, logit_t = call(
+        [S((DEV, 2 * CHUNKS, LANES), BF16), S((CH, PAIRS), BF16), S((2 * CH, CH), BF16)],
+        [V((TILES, N, LANES), F32), V((N, N), BF16), V((CH, CH), BF16)],
+        4 * N * N * N + 3 * unit,
+        (exchange(split_rows(send_grad)), a_t, b_t, zn_t, y, slope, grad_update, w_out),
+    )
+    terms, grad_p = call(
         back_kernel,
-        [S((6 * CH, CH), BF16), S((4 * CH, PAIRS), BF16), S((CH, PAIRS), BF16)],
-        [V((CH, CH), BF16)],
-        7 * unit,
-        (join_rows(exchange(send_back)), zn_t, factor, y, slope, grad_update, w_out),
+        [S((6 * CH, CH), BF16), S((4 * CH, PAIRS), BF16)],
+        [],
+        4 * unit,
+        (join_rows(exchange(send_back)), zn_t, factor, terms_in),
     )
     parts = exchange_terms(terms)
     (summed,) = call(sum_kernel, [S((6 * CH, CH), BF16)], [], 0, (parts,))

time: 130 us -> 130 us (level)
  no operation moved by 1% of the time
where the time goes in v8:
time: 130 us; the launch traced here: 129 us
  blocking collectives  103 us (79%)
  Pallas kernels  12.7 us (10%)
  waiting for transfers between devices  7.06 us (5%)
  starting transfers between devices  4.59 us (4%)
    all_to_all x4, blocking collectives, exchange(): return lax.all_to_all(x, AXES, 0, 0, tiled=True)  88.6 us
    all_to_all x1, blocking collectives, exchange_terms(): return lax.all_to_all(split, AXES[::-1], 0, 0, tiled=True).reshape(x.shape)  14.6 us
    pallas_call x8, Pallas kernels, call(): pl.pallas_call(kernel, out_shape=outs, in_specs=[pl.BlockSpec(memory_spac...  12.7 us
    all_to_all x1, waiting for transfers between devices, exchange_terms(): return lax.all_to_all(split, AXES[::-1], 0, 0, tiled=True).reshape(x.shape)  7.06 us
    all_to_all x1, starting transfers between devices, exchange_terms(): return lax.all_to_all(split, AXES[::-1], 0, 0, tiled=True).reshape(x.shape)  4.59 us
  transfers between devices with their start and end apart: 1, of which 1 were waited for; matrix products, arithmetic and copies ran while one was open for 0% of the time, Pallas kernels for 2%

profile of v8, /device:TPU:1, one launch (start us, length us, event | category | flops | bytes accessed | tf_op | source)
XLA Modules:
  0.0 129.4 jit_solution(1858338081272921820)
XLA Ops:
  0.6 2.8 %shard_map.147 = (bf16[128,4096]{1,0:T(8,128)(2,1)S(1)}, bf16[128,2048]{1,0:T(8,128)(2,1)S(1)}, bf16[512,2048]{1,0:T(8,128)(2,1)S(1)}) custom-call(s32[512]{0:T(512)} %mask_h.1, f32[1,128]{1,0:T(1,128)} %bitcast.32, f32[1,128]{1,0:T(1,128)} %bitcast.38, bf16[128,512]{1,0:T(8,128)(2,1)} %w_proj.1, bf16[64,32,128]{2,1,0:T(8,128)(2,1)} %pair.1), custom_call_target="tpu_custom_call" | custom-call | flops 268435456 | bytes 4328448 | tf_op jit(solution)/shard_map/pallas_call | solution.py:304
  3.4 0.0 copy-start
  3.4 0.0 copy-start.2
  3.4 0.0 copy-start.3
  3.5 0.0 copy-start.5
  3.5 0.0 copy-start.6
  3.5 0.2 copy.16
  3.7 30.0 %all_to_all.30.recv = bf16[128,32,128]{2,1,0:T(8,128)(2,1)S(1)} all-to-all(bf16[128,32,128]{2,1,0:T(8,128)(2,1)S(1)} %bitcast.34), channel_id=1, replica_groups=mesh['row'=8,'col'=16] {'row','col'}, dimensions={0} | all-to-all | bytes 2097152 | tf_op jit(solution)/shard_map/all_to_all | solution.py:316
  33.8 0.0 copy-start.7
  33.8 2.2 %shard_map.148 = (bf16[128,16,128]{2,1,0:T(8,128)(2,1)S(1)}, bf16[512,512]{1,0:T(8,128)(2,1)S(1)}, bf16[512,512]{1,0:T(8,128)(2,1)S(1)}, bf16[128,2048]{1,0:T(8,...) custom-call(s32[512]{0:T(512)} %chain_h.1, f32[1,128]{1,0:T(1,128)S(1)} %bitcast.30, ...), custom_call_target="tpu_custom_call" | custom-call | flops 402653184 | bytes 6360064 | tf_op jit(solution)/shard_map/pallas_call | solution.py:304
  36.0 18.2 %all_to_all.31 = bf16[128,16,128]{2,1,0:T(8,128)(2,1)S(1)} all-to-all(bf16[128,16,128]{2,1,0:T(8,128)(2,1)S(1)} %get-tuple-element.28), channel_id=1, replica_groups=mesh['row'=8,'col'=16] {'row','col'}, dimensions={0} | all-to-all | bytes 1048576 | tf_op jit(solution)/shard_map/all_to_all | solution.py:316
  54.1 0.1 copy.23
  54.3 0.0 copy-done.7
  54.3 0.8 shard_map.149
  55.1 0.1 copy.18
  55.2 17.8 %all_to_all.32.recv = bf16[128,16,128]{2,1,0:T(8,128)(2,1)S(1)} all-to-all(bf16[128,16,128]{2,1,0:T(8,128)(2,1)S(1)} %bitcast.37), channel_id=1, replica_groups=mesh['row'=8,'col'=16] {'row','col'}, dimensions={0} | all-to-all | bytes 1048576 | tf_op jit(solution)/shard_map/all_to_all | solution.py:316
  73.0 1.4 %shard_map.150 = (bf16[128,32,128]{2,1,0:T(8,128)(2,1)S(1)}, bf16[128,2048]{1,0:T(8,128)(2,1)S(1)}, bf16[256,128]{1,0:T(8,128)(2,1)S(1)}) custom-call(bf16[128,16,128]{2,1,0:T(8,128)(2,1)S(1)} %all_to_all.32.recv, bf16[512,512]{1,0:T(8,128)(2,1)S(1)} %get-tuple-element.31.a_t, bf16[512,512]{1,0:T(8,128)(2,1)S(1)} %get-tuple-element.32.b_t, ...), custom_call_target="tpu_custom_call" | custom-call | flops 738197504 | bytes 5865472 | tf_op jit(solution)/shard_map/pallas_call | solution.py:304
  74.4 22.7 %all_to_all.33 = bf16[128,32,128]{2,1,0:T(8,128)(2,1)S(1)} all-to-all(bf16[128,32,128]{2,1,0:T(8,128)(2,1)S(1)} %get-tuple-element.36), channel_id=1, replica_groups=mesh['row'=8,'col'=16] {'row','col'}, dimensions={0} | all-to-all | bytes 2097152 | tf_op jit(solution)/shard_map/all_to_all | solution.py:316
  97.1 0.5 copy.22
  97.6 0.0 copy-start.1
  97.6 0.0 copy-start.4
  97.6 0.0 copy-start.8
  97.6 0.8 shard_map.151
  98.4 14.6 %all_to_all.34 = bf16[128,3,2,128]{3,2,1,0:T(2,128)(2,1)S(1)} all-to-all(bf16[128,3,2,128]{3,2,1,0:T(2,128)(2,1)S(1)} %bitcast.27), channel_id=1, replica_groups=mesh['row'=8,'col'=16] {'col','row'}, dimensions={0} | all-to-all | bytes 393216 | tf_op jit(solution)/shard_map/all_to_all | solution.py:321
  113.0 0.7 shard_map.152
  113.7 4.6 %all-to-all-start.5 = ((bf16[128,3,2,128]{3,2,1,0:T(2,128)(2,1)}), bf16[128,3,2,128]{3,2,1,0:T(2,128)(2,1)S(1)}, u32[]{:S(2)}, u32[]{:S(2)}) async-start(bf16[128,3,2,128]{3,2,1,0:T(2,128)(2,1)} %bitcast.7), calls=%async_computation.5 | async-start | bytes 393216 | tf_op jit(solution)/shard_map/all_to_all | solution.py:321
  118.3 0.0 copy-done.1
  118.3 0.0 copy-done.4
  118.3 0.0 copy-done.8
  118.4 3.1 %shard_map.153 = bf16[64,32,128]{2,1,0:T(8,128)(2,1)} custom-call(bf16[512,2048]{1,0:T(8,128)(2,1)S(1)} %get-tuple-element.42.grad_p, bf16[128,2048]{1,0:T(8,128)(2,1)S(1)} %get-tuple-element.43.logit_t, bf16[64,32,128]{2,1,0:T(8,128)(2,1)S(1)} %copy-done.1, f32[1,128]{1,0:T(1,128)S(1)} %bitcast.33, bf16[128,512]{1,0:T(8,128)(2,1)S(1)} %copy-done.4, ...), custom_call_target="tpu_custom_call" | custom-call | flops 335544320 | bytes 3834368 | tf_op jit(solution)/shard_map/pallas_call | solution.py:304
  121.5 7.1 %all-to-all-done.5 = bf16[128,3,2,128]{3,2,1,0:T(2,128)(2,1)S(1)} async-done(((bf16[128,3,2,128]{3,2,1,0:T(2,128)(2,1)}), bf16[128,3,2,128]{3,2,1,0:T(2,128)(2,1)S(1)}, u32[]{:S(2)}, u32[]{:S(2)}) %all-to-all-start.5) | async-done | bytes 196640 | tf_op jit(solution)/shard_map/all_to_all | solution.py:321
  128.5 0.9 shard_map.154
  (5 shorter events, 0.0 us)
Async XLA Ops:
  3.4 30.3 %copy-start = (bf16[64,32,128]{2,1,0:T(8,128)(2,1)S(1)}, bf16[64,32,128]{2,1,0:T(8,128)(2,1)}, u32[]{:S(2)}) copy-start(bf16[64,32,128]{2,1,0:T(8,128)(2,1)} %cot.1) | copy-start | bytes 1572868
  3.4 30.3 %copy-start.2 = (bf16[128,128]{1,0:T(8,128)(2,1)S(1)}, bf16[128,128]{1,0:T(8,128)(2,1)}, u32[]{:S(2)}) copy-start(bf16[128,128]{1,0:T(8,128)(2,1)} %w_out.3) | copy-start | bytes 98308
  3.4 30.3 %copy-start.3 = (bf16[128,128]{1,0:T(8,128)(2,1)S(1)}, bf16[128,128]{1,0:T(8,128)(2,1)}, u32[]{:S(2)}) copy-start(bf16[128,128]{1,0:T(8,128)(2,1)} %w_gate.3) | copy-start | bytes 98308
  3.5 30.3 %copy-start.5 = (f32[128]{0:T(128)S(1)}, f32[128]{0:T(128)}, u32[]{:S(2)}) copy-start(f32[128]{0:T(128)} %param.21) | copy-start | bytes 1540
  3.5 30.3 %copy-start.6 = (f32[128]{0:T(128)S(1)}, f32[128]{0:T(128)}, u32[]{:S(2)}) copy-start(f32[128]{0:T(128)} %param.20) | copy-start | bytes 1540
  33.8 20.5 %copy-start.7 = (f32[128]{0:T(128)S(1)}, f32[128]{0:T(128)}, u32[]{:S(2)}) copy-start(f32[128]{0:T(128)} %param.22) | copy-start | bytes 1540
  97.6 20.8 %copy-start.1 = (bf16[64,32,128]{2,1,0:T(8,128)(2,1)S(1)}, bf16[64,32,128]{2,1,0:T(8,128)(2,1)}, u32[]{:S(2)}) copy-start(bf16[64,32,128]{2,1,0:T(8,128)(2,1)} %pair.1) | copy-start | bytes 1572868
  97.6 20.8 %copy-start.4 = (bf16[128,512]{1,0:T(8,128)(2,1)S(1)}, bf16[128,512]{1,0:T(8,128)(2,1)}, u32[]{:S(2)}) copy-start(bf16[128,512]{1,0:T(8,128)(2,1)} %w_proj.1) | copy-start | bytes 393220
  97.6 20.8 %copy-start.8 = (f32[128]{0:T(128)S(1)}, f32[128]{0:T(128)}, u32[]{:S(2)}) copy-start(f32[128]{0:T(128)} %param.16) | copy-start | bytes 1540
  113.7 14.8 %all-to-all-start.5 = ((bf16[128,3,2,128]{3,2,1,0:T(2,128)(2,1)}), bf16[128,3,2,128]{3,2,1,0:T(2,128)(2,1)S(1)}, u32[]{:S(2)}, u32[]{:S(2)}) async-start(bf16[128,3,2,128]{3,2,1,0:T(2,128)(2,1)} %bitcast.7), calls=%async_computation.5 | async-start | bytes 393216 | tf_op jit(solution)/shard_map/all_to_all | solution.py:321
